TPU v7x, 512 devices: a whole 4x4x16 slice. The times are simulated.
512 devices in a mesh: src: 16 (over y_hi, x, core), rcv: 32 (over y_lo, z).
Axes of the slice: x: 4, y: 4 (y_hi: 2, y_lo: 2; y = y_hi * 2 + y_lo), z: 16, core: 2. Of those that a mesh axis runs over, the one named last changes fastest.
Arguments:
- spectra: bfloat16 [2, 8, 192, 8192], P(None, None, 'src', 'rcv'), as said below
- alive: int32 [192, 8192], P('src', 'rcv'), may hold values 0 or 1
Outputs:
- stacked: bfloat16 [2, 8, 8192, 8192], P(None, None, 'src', 'rcv')
Inputs may be any that keep to these rules, and one draw needn't show every extreme that they name: spectra: every entry is a random factor times an amplitude of its window and channel that spreads over a factor of 15.
All inputs are finite; a program needn't handle non-finite values. No bound on the sum of `alive` on one device may be relied on, other than what follows from the above.
Results may differ from a plain program's by a relative error of at most 0.0057.
Values may be sent and summed in bfloat16 or wider, within the bound.
No kernel may reach another device: no remote copies, remote signals or barrier semaphores. Data moves between devices by JAX's collectives and lax.ppermute only.
A program may use at most 64 MiB of HBM per device.

v0:
```python
import jax
import jax.numpy as jnp
from jax import lax
from jax.sharding import PartitionSpec as P


def spread(block, axis, holder):
    block = jnp.where(lax.axis_index(axis) == holder, block, jnp.zeros_like(block))
    return lax.psum(block, axis)


def whiten(spectra, alive, bins):
    values = spectra.astype(jnp.float32)
    power = jnp.sum(values * values, axis=(0, 1)) / bins
    factor = alive.astype(jnp.float32) / jnp.sqrt(jnp.maximum(power, 0.5))
    return (values * factor).astype(jnp.bfloat16)


def cross_terms(source_part, receiver_part):
    swapped = jnp.stack((receiver_part[1], -receiver_part[0]))
    real_sum = jnp.einsum(
        "kfwc,kfwd->fcd", source_part, receiver_part, preferred_element_type=jnp.float32
    )
    imag_sum = jnp.einsum(
        "kfwc,kfwd->fcd", source_part, swapped, preferred_element_type=jnp.float32
    )
    return jnp.stack((real_sum, imag_sum))


def body(spectra, alive):
    bins = spectra.shape[1]
    whitened = whiten(spectra, alive, bins)
    ratio = lax.axis_size("rcv") // lax.axis_size("src")
    row_index = lax.axis_index("src")
    receivers = lax.all_gather(whitened, "src", axis=2, tiled=True)
    blocks = []
    for offset in range(ratio):
        blocks.append(spread(receivers, "rcv", row_index * ratio + offset))
    sources = jnp.concatenate(blocks, axis=3)
    stacked = cross_terms(sources, receivers)
    total_windows = receivers.shape[2]
    factor = jnp.float32(1.0) / jnp.sqrt(jnp.float32(total_windows))
    return (stacked * factor).astype(jnp.bfloat16)


def solution(mesh):
    return jax.shard_map(
        body,
        mesh=mesh,
        in_specs=(P(None, None, "src", "rcv"), P("src", "rcv")),
        out_specs=P(None, None, "src", "rcv"),
        check_vma=False,
    )
```

profile of v0, /device:TPU:2, one launch (start us, length us, event | category | flops | bytes accessed | tf_op | source)
XLA Modules:
  0.0 363.6 jit_solution(11212525343441608051)
XLA Ops:
  6.5 0.0 all-gather.2.cloned.1.call-start
  6.5 0.9 fusion.4
  7.5 0.7 rsqrt_multiply_fusion
  8.2 1.6 fusion.5
  9.8 0.0 all-gather.2.cloned.1.call-update
  9.8 0.0 all-reduce.3.cloned.1.call-start
  9.8 67.1 %all-gather.2.cloned.1.call-done = bf16[2,8,192,256]{3,1,0,2:T(8,128)(2,1)} async-done(((bf16[2,8,12,256]{3,1,0,2:T(8,128)(2,1)}), bf16[2,8,192,256]{3,1,0,2:T(8,128)(2,1)}) %all-gather.2.cloned.1.call-update) | async-done | bytes 1572880 | tf_op jit(solution)/shard_map/all_gather | solution.py:35
  77.0 4.1 %fusion.9 = (bf16[2,8,192,256]{3,2,0,1:T(8,128)(2,1)S(1)}, bf16[2,8,192,256]{3,2,0,1:T(8,128)(2,1)}, bf16[2,8,192,256]{3,2,0,1:T(8,128)(2,1)}) fusion(bf16[2,8,192,256]{3,1,0,2:T(8,128)(2,1)} %all-gather.2.cloned.1.call-done, pred[]{:T(512)S(6)} %eq.6, pred[]{:T(512)S(6)} %eq.7), kind=kLoop, calls=%fused_computation.20 | loop fusion | flops 1572864 | bytes 6291458 | tf_op jit(solution)/shard_map/all_gather | solution.py:35
  81.1 0.0 all-reduce.3.cloned.1.call-update
  81.1 0.1 fusion.8
  81.2 267.8 %all-reduce.3.cloned.1.call-done = (bf16[2,8,192,256]{3,2,0,1:T(8,128)(2,1)}, bf16[2,8,192,256]{3,2,0,1:T(8,128)(2,1)}) async-done(((bf16[2,8,192,256]{3,2,0,1:T(8,128)(2,1)}, bf16[2,8,192,256]{3,2,0,1:T(8,128)(2,1)}), (bf16[2,8,192,256]{3,2,0,1:T(8,128)(2,1)}, bf16[2,8,192,256]{3,2,0,1:T(8,128)(2,1)})) %all-reduce.3.cloned.1.call-update) | async-done | bytes 3145744 | tf_op jit(solution)/shard_map/psum | solution.py:9
  349.0 0.0 copy-start.1
  349.0 1.7 constant_dynamic-update-slice_fusion.1
  350.7 0.2 copy-done.1
  350.9 0.1 constant_dynamic-update-slice_fusion
  351.1 0.0 copy-start
  351.1 1.4 convolution_bitcast_fusion
  352.5 0.0 copy-done
  352.5 1.6 convolution_bitcast_fusion.1
  354.2 2.6 fusion
Async XLA Ops:
  6.5 70.4 %all-gather.2.cloned.1.call-start = ((), (), s32[]{:S(2)}) async-start(), calls=%async_computation | async-start | bytes 1671168 | tf_op jit(solution)/shard_map/all_gather | solution.py:35
  9.8 339.3 %all-reduce.3.cloned.1.call-start = ((), (), s32[]{:S(2)}) async-start(), calls=%async_computation.1 | async-start | bytes 6291456 | tf_op jit(solution)/shard_map/psum | solution.py:9
  349.0 1.9 copy-start.1
  351.1 1.5 copy-start
Sparse Core Ops, SparseCore 0:
  10.7 66.2 all-gather.1
  81.2 267.7 all-reduce.2
where the time goes:
time: 364 us
  waiting for transfers between devices  335 us (92%)
  between operations  13.5 us (4%)
  other arithmetic  9.98 us (3%)
    psum x1, waiting for transfers between devices, spread(): return lax.psum(block, axis)  268 us
    all_gather x1, waiting for transfers between devices, body(): receivers = lax.all_gather(whitened, 'src', axis=2, tiled=True)  67.1 us
  transfers between devices with their start and end apart: 2, of which 2 were waited for; matrix products, arithmetic and copies ran while one was open for 0% of the time, Pallas kernels for 0%

commit v1 on v0

v1 whole, which is shorter than its diff:
```python
import jax
import jax.numpy as jnp
import numpy as np
from jax import lax
from jax.experimental import pallas as pl
from jax.experimental.pallas import tpu as pltpu
from jax.sharding import PartitionSpec as P

OWN_SLOTS = ((0, -5, 5), (-1, -6, 4), (1, -4, 6), (-2, -7, 3), (2, -3, 7), (8,))
NEIGHBOUR_SLOTS = ((0, -5, 5), (-1, -6, 4), (1, -4, 6), (-2, -7, 3), (2, -3, 7, 8))


def whiten_kernel(bins, spectra_ref, alive_ref, out_ref, rows_ref):
    windows = spectra_ref.shape[1]
    for window in range(windows):
        real = spectra_ref[0, window].astype(jnp.float32)
        imag = spectra_ref[1, window].astype(jnp.float32)
        power = jnp.sum(real * real + imag * imag, axis=0, keepdims=True) / bins
        live = alive_ref[window : window + 1, :].astype(jnp.float32)
        factor = live / jnp.sqrt(jnp.maximum(power, 0.5))
        rows_ref[0, window] = real * factor
        rows_ref[1, window] = imag * factor
    values = rows_ref[...].reshape(2 * windows, bins, rows_ref.shape[-1])
    out_ref[...] = jnp.swapaxes(values, 0, 1).astype(jnp.bfloat16)


def whiten(spectra, alive):
    _, bins, windows, channels = spectra.shape
    by_window = jnp.swapaxes(spectra, 1, 2)
    return pl.pallas_call(
        lambda *refs: whiten_kernel(bins, *refs),
        out_shape=jax.ShapeDtypeStruct((bins, 2 * windows, channels), jnp.bfloat16),
        scratch_shapes=[pltpu.VMEM((2, windows, bins, channels), jnp.float32)],
        name="whiten",
    )(by_window, alive)


def receiver_kernel(in_ref, out_ref):
    slices, _, rows, channels = in_ref.shape
    for piece in range(slices):
        block = in_ref[piece, 0]
        wide = block.astype(jnp.float32)
        turned = jnp.concatenate((wide[rows // 2 :], -wide[: rows // 2]), axis=0)
        out_ref[0, piece, :, :channels] = block
        out_ref[0, piece, :, channels:] = turned.astype(jnp.bfloat16)


def receiver_pairs(receivers):
    slices, bins, rows, channels = receivers.shape
    return pl.pallas_call(
        receiver_kernel,
        grid=(bins,),
        in_specs=[pl.BlockSpec((slices, 1, rows, channels), lambda f: (0, f, 0, 0))],
        out_specs=pl.BlockSpec((1, slices, rows, 2 * channels), lambda f: (f, 0, 0, 0)),
        out_shape=jax.ShapeDtypeStruct((bins, slices, rows, 2 * channels), jnp.bfloat16),
        name="receiver_pairs",
    )(receivers)


def stack_kernel(parities, scale, place_ref, *refs):
    groups = refs[: len(parities)]
    pairs_ref, out_ref, even_ref, odd_ref = refs[len(parities) :]
    rows = groups[0].shape[2]
    channels = groups[0].shape[3]
    slot = 0
    for group, parity in zip(groups, parities):
        for i in range(group.shape[0]):
            held = odd_ref if parity[i] else even_ref
            held[place_ref[slot]] = group[i, 0]
            slot += 1
    pairs = pairs_ref[0].reshape(-1, 2 * channels)
    for held, side in ((even_ref, place_ref[slot]), (odd_ref, 1 - place_ref[slot])):
        total = lax.dot_general(
            held[...].reshape(-1, channels),
            pairs,
            (((0,), (0,)), ((), ())),
            preferred_element_type=jnp.float32,
        )
        total = (total * scale).astype(jnp.bfloat16)
        at = pl.ds(pl.multiple_of(side * channels, channels), channels)
        out_ref[0, 0, at, :] = total[:, :channels]
        out_ref[1, 0, at, :] = total[:, channels:]


def stack(groups, parities, place, pairs, scale):
    bins, slices, rows, twice = pairs.shape
    channels = twice // 2
    return pl.pallas_call(
        lambda *refs: stack_kernel(parities, scale, *refs),
        grid=(bins,),
        in_specs=[pl.BlockSpec(memory_space=pltpu.SMEM)]
        + [pl.BlockSpec((g.shape[0], 1, rows, channels), lambda f: (0, f, 0, 0)) for g in groups]
        + [pl.BlockSpec((1, slices, rows, twice), lambda f: (f, 0, 0, 0))],
        out_specs=pl.BlockSpec((2, 1, 2 * channels, channels), lambda f: (0, f, 0, 0)),
        out_shape=jax.ShapeDtypeStruct((2, bins, 2 * channels, channels), jnp.bfloat16),
        scratch_shapes=[pltpu.VMEM((slices, rows, channels), jnp.bfloat16)] * 2,
        name="stack",
    )(place, *groups, pairs)


def body(spectra, alive):
    rows_n, cols_n = lax.axis_size("src"), lax.axis_size("rcv")
    length = cols_n // 2
    windows = spectra.shape[2] * rows_n

    def along(z_of, step):
        return z_of // length * length + (z_of % length + step) % length

    def shift(block, step):
        return lax.ppermute(block, "rcv", [(r, along(r, step)) for r in range(cols_n)])

    def trade(block):
        return lax.ppermute(block, "rcv", [(r, (r + length) % cols_n) for r in range(cols_n)])

    def deal(block, step):
        pairs = [
            (s * cols_n + 2 * d + o, d * cols_n + along(2 * s + o, step))
            for s in range(rows_n)
            for d in range(rows_n)
            for o in range(2)
        ]
        return lax.ppermute(block, ("src", "rcv"), pairs)

    local = whiten(spectra, alive)
    dealt = [deal(local, step)[None] for step in (0, 5, -5)]
    receivers = lax.all_to_all(
        jnp.broadcast_to(local[None], (rows_n,) + local.shape), "src", 0, 0
    )
    *dealt, receivers = lax.optimization_barrier((*dealt, receivers))
    first = jnp.concatenate(dealt, axis=0)
    up, down, other = shift(first, 1), shift(first, -1), trade(first)
    up2, down2, far = shift(up, 1), shift(down, -1), shift(down[2:], -2)
    other_up, other_down = shift(other, 1), shift(other, -1)
    other_up2 = shift(other_up, 1)
    last = trade(jnp.concatenate((down2, far), axis=0))
    pairs = receiver_pairs(receivers)

    groups = (first, up, down, up2, down2, far, other, other_up, other_down, other_up2, last)
    own = lax.axis_index("rcv") // length
    z = lax.axis_index("rcv") % length
    offsets = OWN_SLOTS + NEIGHBOUR_SLOTS
    swaps = [i >= len(OWN_SLOTS) for i, group in enumerate(offsets) for _ in group]
    steps = [step % length for group in offsets for step in group]
    row = jnp.where(np.array(swaps), 1 - own, own)
    place = row * (rows_n // 2) + lax.rem(z + np.array(steps, np.int32), length) // 2
    place = jnp.append(place, z % 2).astype(jnp.int32)
    parities = tuple(tuple(step % 2 for step in group) for group in offsets)
    scale = 1.0 / float(windows) ** 0.5
    return stack(groups, parities, place, pairs, scale)


def solution(mesh):
    return jax.shard_map(
        body,
        mesh=mesh,
        in_specs=(P(None, None, "src", "rcv"), P("src", "rcv")),
        out_specs=P(None, None, "src", "rcv"),
        check_vma=False,
    )
```

time: 364 us -> 116 us (0.32)
  the two profiles are of different devices: /device:TPU:2 before, /device:TPU:28 now
where the time goes in v1:
time: 116 us
  starting transfers between devices  70.2 us (61%)
  waiting for transfers between devices  24.8 us (21%)
  Pallas kernels  16.5 us (14%)
  local copies, waits for them, and re-layouts  3.05 us (3%)
    ppermute x8, starting transfers between devices, shift(): lax.ppermute(block, 'rcv', [(r, along(r, step)) for r in range(cols_n)])  30.8 us
    ppermute x3, starting transfers between devices, deal(): return lax.ppermute(block, ('src', 'rcv'), pairs)  23.9 us
    ppermute x8, waiting for transfers between devices, shift(): lax.ppermute(block, 'rcv', [(r, along(r, step)) for r in range(cols_n)])  13.6 us
    ppermute x3, waiting for transfers between devices, deal(): return lax.ppermute(block, ('src', 'rcv'), pairs)  11.2 us
    pallas_call x1, Pallas kernels, stack(): pl.pallas_call(lambda *refs: stack_kernel(parities, scale, *refs), grid=(...  8.93 us
    ppermute x2, starting transfers between devices, trade(): lax.ppermute(block, 'rcv', [(r, (r + length) % cols_n) for r in range(col...  8.24 us
    all_to_all x1, starting transfers between devices, body(): lax.all_to_all(jnp.broadcast_to(local[None], (rows_n,) + local.shape), 's...  7.23 us
    pallas_call x1, Pallas kernels, receiver_pairs(): pl.pallas_call(receiver_kernel, grid=(bins,), in_specs=[pl.BlockSpec((sli...  5.93 us
  transfers between devices with their start and end apart: 14, of which 5 were waited for; matrix products, arithmetic and copies ran while one was open for 1% of the time, Pallas kernels for 5%

profile of v1, /device:TPU:28, one launch (start us, length us, event | category | flops | bytes accessed | tf_op | source)
XLA Modules:
  0.0 115.6 jit_solution(8220047816540909945)
XLA Ops:
  0.0 1.7 %whiten.1 = bf16[8,24,256]{2,1,0:T(8,128)(2,1)} custom-call(bf16[2,12,8,256]{3,2,1,0:T(8,128)(2,1)} %bitcast.8, s32[12,256]{1,0:T(8,128)} %refs_1_.1), custom_call_target="tpu_custom_call" | custom-call | tf_op jit(solution)/shard_map/whiten/pallas_call | solution.py:30
  1.7 0.0 copy-start.5
  1.7 0.0 copy-start.7
  1.7 0.0 copy-start.8
  1.7 2.3 %broadcast_in_dim.28 = bf16[16,8,24,256]{3,2,1,0:T(8,128)(2,1)} broadcast(bf16[8,24,256]{2,1,0:T(8,128)(2,1)} %whiten.1), dimensions={1,2,3} | broadcast | bytes 1671168 | tf_op jit(solution)/shard_map/broadcast_in_dim | solution.py:127
  3.9 7.2 %all-to-all-start = ((bf16[16,8,24,256]{3,2,1,0:T(8,128)(2,1)}), bf16[16,8,24,256]{3,2,1,0:T(8,128)(2,1)S(1)}, u32[]{:S(2)}, u32[]{:S(2)}) async-start(bf16[16,8,24,256]{3,2,1,0:T(8,128)(2,1)} %broadcast_in_dim.28), calls=%async_computation | async-start | bytes 3145728 | tf_op jit(solution)/shard_map/all_to_all | solution.py:126
  11.1 0.0 copy-done.5
  11.2 6.5 %collective-permute-start.2 = (bf16[8,24,256]{2,1,0:T(8,128)(2,1)S(1)}, bf16[8,24,256]{2,1,0:T(8,128)(2,1)S(1)}, u32[]{:S(2)}, u32[]{:S(2)}) collective-permute-start(bf16[8,24,256]{2,1,0:T(8,128)(2,1)S(1)} %copy-done.5), channel_id=1, source_target_pairs={{0,11},{1,12},{2,43},{3,44},{4,75},{5,76},{6,107},{7,108},{8,139},... | collective-permute-start | bytes 294920 | tf_op jit(solution)/shard_map/ppermute | solution.py:122
  17.7 10.8 %collective-permute-start.1 = (bf16[8,24,256]{2,1,0:T(8,128)(2,1)S(1)}, bf16[8,24,256]{2,1,0:T(8,128)(2,1)S(1)}, u32[]{:S(2)}, u32[]{:S(2)}) collective-permute-start(bf16[8,24,256]{2,1,0:T(8,128)(2,1)S(1)} %copy-done.5), channel_id=1, source_target_pairs={{0,5},{1,6},{2,37},{3,38},{4,69},{5,70},{6,101},{7,102},{8,133},{9... | collective-permute-start | bytes 294920 | tf_op jit(solution)/shard_map/ppermute | solution.py:122
  28.5 6.6 %collective-permute-start = (bf16[8,24,256]{2,1,0:T(8,128)(2,1)S(1)}, bf16[8,24,256]{2,1,0:T(8,128)(2,1)S(1)}, u32[]{:S(2)}, u32[]{:S(2)}) collective-permute-start(bf16[8,24,256]{2,1,0:T(8,128)(2,1)S(1)} %copy-done.5), channel_id=1, source_target_pairs={{0,0},{1,1},{2,32},{3,33},{4,64},{5,65},{6,96},{7,97},{8,128},{9,1... | collective-permute-start | bytes 294920 | tf_op jit(solution)/shard_map/ppermute | solution.py:122
  35.1 0.0 collective-permute-done.2
  35.1 0.0 collective-permute-done.1
  35.1 11.2 %collective-permute-done = bf16[8,24,256]{2,1,0:T(8,128)(2,1)S(1)} collective-permute-done((bf16[8,24,256]{2,1,0:T(8,128)(2,1)S(1)}, bf16[8,24,256]{2,1,0:T(8,128)(2,1)S(1)}, u32[]{:S(2)}, u32[]{:S(2)}) %collective-permute-start) | collective-permute-done | bytes 98336 | tf_op jit(solution)/shard_map/ppermute | solution.py:122
  46.3 0.0 all-to-all-done.in_ref
  46.3 0.0 copy-start
  46.3 0.0 copy-start.3
  46.3 6.9 %collective-permute-start.4 = (bf16[3,8,24,256]{3,2,1,0:T(8,128)(2,1)S(1)}, bf16[3,8,24,256]{3,2,1,0:T(8,128)(2,1)S(1)}, u32[]{:S(2)}, u32[]{:S(2)}) collective-permute-start(bf16[3,8,24,256]{3,2,1,0:T(8,128)(2,1)S(1)} %constant_dynamic-update-slice_fusion.refs_1_), channel_id=1, source_target_pairs={{0,15},{1,0},{2,1},{3,2},{4,3},{5,4},{6,5},{7,6},{8,7},{9,8},{10,9... | collective-permute-start | bytes 884744 | tf_op jit(solution)/shard_map/ppermute | solution.py:110
  53.3 4.0 %collective-permute-start.8 = (bf16[3,8,24,256]{3,2,1,0:T(8,128)(2,1)S(1)}, bf16[3,8,24,256]{3,2,1,0:T(8,128)(2,1)}, u32[]{:S(2)}, u32[]{:S(2)}) collective-permute-start(bf16[3,8,24,256]{3,2,1,0:T(8,128)(2,1)S(1)} %constant_dynamic-update-slice_fusion.refs_1_), channel_id=1, source_target_pairs={{0,16},{1,17},{2,18},{3,19},{4,20},{5,21},{6,22},{7,23},{8,24},{9,... | collective-permute-start | bytes 884744 | tf_op jit(solution)/shard_map/ppermute | solution.py:113
  57.2 3.0 %collective-permute-done.4.refs_3_ = bf16[3,8,24,256]{3,2,1,0:T(8,128)(2,1)S(1)} collective-permute-done((bf16[3,8,24,256]{3,2,1,0:T(8,128)(2,1)S(1)}, bf16[3,8,24,256]{3,2,1,0:T(8,128)(2,1)S(1)}, u32[]{:S(2)}, u32[]{:S(2)}) %collective-permute-start.4) | collective-permute-done | bytes 294944 | tf_op jit(solution)/shard_map/ppermute | solution.py:110
  60.3 0.0 copy-start.2
  60.3 5.6 %collective-permute-start.6 = (bf16[3,8,24,256]{3,2,1,0:T(8,128)(2,1)S(1)}, bf16[3,8,24,256]{3,2,1,0:T(8,128)(2,1)S(1)}, u32[]{:S(2)}, u32[]{:S(2)}) collective-permute-start(bf16[3,8,24,256]{3,2,1,0:T(8,128)(2,1)S(1)} %collective-permute-done.4.refs_3_), channel_id=1, source_target_pairs={{0,15},{1,0},{2,1},{3,2},{4,3},{5,4},{6,5},{7,6},{8,7},{9,8},{10,9... | collective-permute-start | bytes 884744 | tf_op jit(solution)/shard_map/ppermute | solution.py:110
  65.9 1.9 %collective-permute-start.3 = (bf16[3,8,24,256]{3,2,1,0:T(8,128)(2,1)S(1)}, bf16[3,8,24,256]{3,2,1,0:T(8,128)(2,1)}, u32[]{:S(2)}, u32[]{:S(2)}) collective-permute-start(bf16[3,8,24,256]{3,2,1,0:T(8,128)(2,1)S(1)} %constant_dynamic-update-slice_fusion.refs_1_), channel_id=1, source_target_pairs={{0,1},{1,2},{2,3},{3,4},{4,5},{5,6},{6,7},{7,8},{8,9},{9,10},{10,1... | collective-permute-start | bytes 884744 | tf_op jit(solution)/shard_map/ppermute | solution.py:110
  67.8 0.0 collective-permute-done.8.refs_7_
  67.8 1.9 %collective-permute-start.9 = (bf16[3,8,24,256]{3,2,1,0:T(8,128)(2,1)}, bf16[3,8,24,256]{3,2,1,0:T(8,128)(2,1)}, u32[]{:S(2)}, u32[]{:S(2)}) collective-permute-start(bf16[3,8,24,256]{3,2,1,0:T(8,128)(2,1)} %collective-permute-done.8.refs_7_), channel_id=1, source_target_pairs={{0,1},{1,2},{2,3},{3,4},{4,5},{5,6},{6,7},{7,8},{8,9},{9,10},{10,1... | collective-permute-start | bytes 884744 | tf_op jit(solution)/shard_map/ppermute | solution.py:110
  69.8 6.6 %collective-permute-start.7 = (bf16[1,8,24,256]{3,2,1,0:T(8,128)(2,1)S(1)}, bf16[1,8,24,256]{3,2,1,0:T(8,128)(2,1)S(1)}, u32[]{:S(2)}, u32[]{:S(2)}) collective-permute-start(bf16[1,8,24,256]{3,2,1,0:T(8,128)(2,1)S(1)} %slice.4), channel_id=1, source_target_pairs={{0,14},{1,15},{2,0},{3,1},{4,2},{5,3},{6,4},{7,5},{8,6},{9,7},{10,... | collective-permute-start | bytes 294920 | tf_op jit(solution)/shard_map/ppermute | solution.py:110
  76.3 3.5 %collective-permute-done.7.refs_6_ = bf16[1,8,24,256]{3,2,1,0:T(8,128)(2,1)S(1)} collective-permute-done((bf16[1,8,24,256]{3,2,1,0:T(8,128)(2,1)S(1)}, bf16[1,8,24,256]{3,2,1,0:T(8,128)(2,1)S(1)}, u32[]{:S(2)}, u32[]{:S(2)}) %collective-permute-start.7) | collective-permute-done | bytes 98336 | tf_op jit(solution)/shard_map/ppermute | solution.py:110
  79.8 0.0 copy-start.4
  79.8 0.0 collective-permute-done.6.refs_5_
  79.8 0.0 copy-start.1
  79.9 4.3 %collective-permute-start.12 = (bf16[4,8,24,256]{3,2,1,0:T(8,128)(2,1)S(1)}, bf16[4,8,24,256]{3,2,1,0:T(8,128)(2,1)S(1)}, u32[]{:S(2)}, u32[]{:S(2)}) collective-permute-start(bf16[4,8,24,256]{3,2,1,0:T(8,128)(2,1)S(1)} %pad_maximum_fusion), channel_id=1, source_target_pairs={{0,16},{1,17},{2,18},{3,19},{4,20},{5,21},{6,22},{7,23},{8,24},{9,... | collective-permute-start | bytes 1179656 | tf_op jit(solution)/shard_map/ppermute | solution.py:113
  84.2 4.1 %collective-permute-start.10 = (bf16[3,8,24,256]{3,2,1,0:T(8,128)(2,1)}, bf16[3,8,24,256]{3,2,1,0:T(8,128)(2,1)}, u32[]{:S(2)}, u32[]{:S(2)}) collective-permute-start(bf16[3,8,24,256]{3,2,1,0:T(8,128)(2,1)} %collective-permute-done.8.refs_7_), channel_id=1, source_target_pairs={{0,15},{1,0},{2,1},{3,2},{4,3},{5,4},{6,5},{7,6},{8,7},{9,8},{10,9... | collective-permute-start | bytes 884744 | tf_op jit(solution)/shard_map/ppermute | solution.py:110
  88.3 0.0 collective-permute-done.3.refs_2_
  88.3 1.9 %collective-permute-start.5 = (bf16[3,8,24,256]{3,2,1,0:T(8,128)(2,1)}, bf16[3,8,24,256]{3,2,1,0:T(8,128)(2,1)}, u32[]{:S(2)}, u32[]{:S(2)}) collective-permute-start(bf16[3,8,24,256]{3,2,1,0:T(8,128)(2,1)} %collective-permute-done.3.refs_2_), channel_id=1, source_target_pairs={{0,1},{1,2},{2,3},{3,4},{4,5},{5,6},{6,7},{7,8},{8,9},{9,10},{10,1... | collective-permute-start | bytes 884744 | tf_op jit(solution)/shard_map/ppermute | solution.py:110
  90.2 0.0 collective-permute-done.9.refs_8_
  90.2 1.9 %collective-permute-start.11 = (bf16[3,8,24,256]{3,2,1,0:T(8,128)(2,1)}, bf16[3,8,24,256]{3,2,1,0:T(8,128)(2,1)}, u32[]{:S(2)}, u32[]{:S(2)}) collective-permute-start(bf16[3,8,24,256]{3,2,1,0:T(8,128)(2,1)} %collective-permute-done.9.refs_8_), channel_id=1, source_target_pairs={{0,1},{1,2},{2,3},{3,4},{4,5},{5,6},{6,7},{7,8},{8,9},{9,10},{10,1... | collective-permute-start | bytes 884744 | tf_op jit(solution)/shard_map/ppermute | solution.py:110
  92.1 0.0 copy-done.7
  92.2 0.0 copy-done.8
  92.2 0.7 pad_add_fusion.refs_0_
  92.9 0.0 copy-done
  92.9 5.9 %receiver_pairs.1.refs_12_ = bf16[8,16,24,512]{3,2,1,0:T(8,128)(2,1)} custom-call(bf16[16,8,24,256]{3,2,1,0:T(8,128)(2,1)} %copy-done), custom_call_target="tpu_custom_call" | custom-call | tf_op jit(solution)/shard_map/receiver_pairs/pallas_call | solution.py:50
  98.8 0.0 collective-permute-done.10.refs_9_
  98.8 2.9 %collective-permute-done.5.refs_4_ = bf16[3,8,24,256]{3,2,1,0:T(8,128)(2,1)} collective-permute-done((bf16[3,8,24,256]{3,2,1,0:T(8,128)(2,1)}, bf16[3,8,24,256]{3,2,1,0:T(8,128)(2,1)}, u32[]{:S(2)}, u32[]{:S(2)}) %collective-permute-start.5) | collective-permute-done | bytes 294944 | tf_op jit(solution)/shard_map/ppermute | solution.py:110
  101.6 4.2 %collective-permute-done.11.refs_10_ = bf16[3,8,24,256]{3,2,1,0:T(8,128)(2,1)} collective-permute-done((bf16[3,8,24,256]{3,2,1,0:T(8,128)(2,1)}, bf16[3,8,24,256]{3,2,1,0:T(8,128)(2,1)}, u32[]{:S(2)}, u32[]{:S(2)}) %collective-permute-start.11) | collective-permute-done | bytes 294944 | tf_op jit(solution)/shard_map/ppermute | solution.py:110
  105.9 0.0 collective-permute-done.12.refs_11_
  105.9 0.0 copy-done.3
  105.9 0.0 copy-done.2
  105.9 0.0 copy-done.4
  105.9 0.0 copy-done.1
  105.9 0.0 copy-start.6
  105.9 0.7 copy-done.6
  106.7 8.9 %stack.1 = bf16[2,8,512,256]{3,2,1,0:T(8,128)(2,1)} custom-call(s32[33]{0:T(128)} %pad_add_fusion.refs_0_, bf16[3,8,24,256]{3,2,1,0:T(8,128)(2,1)} %copy-done.3, bf16[3,8,24,256]{3,2,1,0:T(8,128)(2,1)} %collective-permute-done.3.refs_2_, bf16[3,8,24,256]{3,2,1,0:T(8,128)(2,1)} %copy-done.2, bf16[3,8,24,256]{3,2,1,0:T(8,128)(2,1)} %collective-permute-done.5.refs_4_, ...), custom_call_target="tpu_custom_call" | custom-call | tf_op jit(solution)/shard_map/stack/pallas_call | solution.py:88
  (6 shorter events, 0.1 us)
Async XLA Ops:
  1.7 9.5 %copy-start.5 = (bf16[8,24,256]{2,1,0:T(8,128)(2,1)S(1)}, bf16[8,24,256]{2,1,0:T(8,128)(2,1)}, u32[]{:S(2)}) copy-start(bf16[8,24,256]{2,1,0:T(8,128)(2,1)} %whiten.1) | copy-start | bytes 294916
  1.7 90.5 %copy-start.7 = (s32[32]{0:T(128)S(1)}, s32[32]{0:T(128)}, u32[]{:S(2)}) copy-start(s32[32]{0:T(128)} %constant.60.clone) | copy-start | bytes 388
  1.7 90.5 %copy-start.8 = (pred[32]{0:T(512)(128)(4,1)S(1)}, pred[32]{0:T(512)(128)(4,1)}, u32[]{:S(2)}) copy-start(pred[32]{0:T(512)(128)(4,1)} %constant.59.clone) | copy-start | bytes 100
  3.9 42.4 %all-to-all-start = ((bf16[16,8,24,256]{3,2,1,0:T(8,128)(2,1)}), bf16[16,8,24,256]{3,2,1,0:T(8,128)(2,1)S(1)}, u32[]{:S(2)}, u32[]{:S(2)}) async-start(bf16[16,8,24,256]{3,2,1,0:T(8,128)(2,1)} %broadcast_in_dim.28), calls=%async_computation | async-start | bytes 3145728 | tf_op jit(solution)/shard_map/all_to_all | solution.py:126
  11.2 23.9 %collective-permute-start.2 = (bf16[8,24,256]{2,1,0:T(8,128)(2,1)S(1)}, bf16[8,24,256]{2,1,0:T(8,128)(2,1)S(1)}, u32[]{:S(2)}, u32[]{:S(2)}) collective-permute-start(bf16[8,24,256]{2,1,0:T(8,128)(2,1)S(1)} %copy-done.5), channel_id=1, source_target_pairs={{0,11},{1,12},{2,43},{3,44},{4,75},{5,76},{6,107},{7,108},{8,139},... | collective-permute-start | bytes 294920 | tf_op jit(solution)/shard_map/ppermute | solution.py:122
  17.7 17.4 %collective-permute-start.1 = (bf16[8,24,256]{2,1,0:T(8,128)(2,1)S(1)}, bf16[8,24,256]{2,1,0:T(8,128)(2,1)S(1)}, u32[]{:S(2)}, u32[]{:S(2)}) collective-permute-start(bf16[8,24,256]{2,1,0:T(8,128)(2,1)S(1)} %copy-done.5), channel_id=1, source_target_pairs={{0,5},{1,6},{2,37},{3,38},{4,69},{5,70},{6,101},{7,102},{8,133},{9... | collective-permute-start | bytes 294920 | tf_op jit(solution)/shard_map/ppermute | solution.py:122
  28.5 17.8 %collective-permute-start = (bf16[8,24,256]{2,1,0:T(8,128)(2,1)S(1)}, bf16[8,24,256]{2,1,0:T(8,128)(2,1)S(1)}, u32[]{:S(2)}, u32[]{:S(2)}) collective-permute-start(bf16[8,24,256]{2,1,0:T(8,128)(2,1)S(1)} %copy-done.5), channel_id=1, source_target_pairs={{0,0},{1,1},{2,32},{3,33},{4,64},{5,65},{6,96},{7,97},{8,128},{9,1... | collective-permute-start | bytes 294920 | tf_op jit(solution)/shard_map/ppermute | solution.py:122
  46.3 46.6 %copy-start = (bf16[16,8,24,256]{3,2,1,0:T(8,128)(2,1)}, bf16[16,8,24,256]{3,2,1,0:T(8,128)(2,1)S(1)}, u32[]{:S(2)}) copy-start(bf16[16,8,24,256]{3,2,1,0:T(8,128)(2,1)S(1)} %all-to-all-done.in_ref) | copy-start | bytes 4718596
  46.3 59.6 %copy-start.3 = (bf16[3,8,24,256]{3,2,1,0:T(8,128)(2,1)}, bf16[3,8,24,256]{3,2,1,0:T(8,128)(2,1)S(1)}, u32[]{:S(2)}) copy-start(bf16[3,8,24,256]{3,2,1,0:T(8,128)(2,1)S(1)} %constant_dynamic-update-slice_fusion.refs_1_) | copy-start | bytes 884740
  46.3 13.9 %collective-permute-start.4 = (bf16[3,8,24,256]{3,2,1,0:T(8,128)(2,1)S(1)}, bf16[3,8,24,256]{3,2,1,0:T(8,128)(2,1)S(1)}, u32[]{:S(2)}, u32[]{:S(2)}) collective-permute-start(bf16[3,8,24,256]{3,2,1,0:T(8,128)(2,1)S(1)} %constant_dynamic-update-slice_fusion.refs_1_), channel_id=1, source_target_pairs={{0,15},{1,0},{2,1},{3,2},{4,3},{5,4},{6,5},{7,6},{8,7},{9,8},{10,9... | collective-permute-start | bytes 884744 | tf_op jit(solution)/shard_map/ppermute | solution.py:110
  53.3 14.5 %collective-permute-start.8 = (bf16[3,8,24,256]{3,2,1,0:T(8,128)(2,1)S(1)}, bf16[3,8,24,256]{3,2,1,0:T(8,128)(2,1)}, u32[]{:S(2)}, u32[]{:S(2)}) collective-permute-start(bf16[3,8,24,256]{3,2,1,0:T(8,128)(2,1)S(1)} %constant_dynamic-update-slice_fusion.refs_1_), channel_id=1, source_target_pairs={{0,16},{1,17},{2,18},{3,19},{4,20},{5,21},{6,22},{7,23},{8,24},{9,... | collective-permute-start | bytes 884744 | tf_op jit(solution)/shard_map/ppermute | solution.py:113
  60.3 45.6 %copy-start.2 = (bf16[3,8,24,256]{3,2,1,0:T(8,128)(2,1)}, bf16[3,8,24,256]{3,2,1,0:T(8,128)(2,1)S(1)}, u32[]{:S(2)}) copy-start(bf16[3,8,24,256]{3,2,1,0:T(8,128)(2,1)S(1)} %collective-permute-done.4.refs_3_) | copy-start | bytes 884740
  60.3 19.5 %collective-permute-start.6 = (bf16[3,8,24,256]{3,2,1,0:T(8,128)(2,1)S(1)}, bf16[3,8,24,256]{3,2,1,0:T(8,128)(2,1)S(1)}, u32[]{:S(2)}, u32[]{:S(2)}) collective-permute-start(bf16[3,8,24,256]{3,2,1,0:T(8,128)(2,1)S(1)} %collective-permute-done.4.refs_3_), channel_id=1, source_target_pairs={{0,15},{1,0},{2,1},{3,2},{4,3},{5,4},{6,5},{7,6},{8,7},{9,8},{10,9... | collective-permute-start | bytes 884744 | tf_op jit(solution)/shard_map/ppermute | solution.py:110
  65.9 22.4 %collective-permute-start.3 = (bf16[3,8,24,256]{3,2,1,0:T(8,128)(2,1)S(1)}, bf16[3,8,24,256]{3,2,1,0:T(8,128)(2,1)}, u32[]{:S(2)}, u32[]{:S(2)}) collective-permute-start(bf16[3,8,24,256]{3,2,1,0:T(8,128)(2,1)S(1)} %constant_dynamic-update-slice_fusion.refs_1_), channel_id=1, source_target_pairs={{0,1},{1,2},{2,3},{3,4},{4,5},{5,6},{6,7},{7,8},{8,9},{9,10},{10,1... | collective-permute-start | bytes 884744 | tf_op jit(solution)/shard_map/ppermute | solution.py:110
  67.8 22.4 %collective-permute-start.9 = (bf16[3,8,24,256]{3,2,1,0:T(8,128)(2,1)}, bf16[3,8,24,256]{3,2,1,0:T(8,128)(2,1)}, u32[]{:S(2)}, u32[]{:S(2)}) collective-permute-start(bf16[3,8,24,256]{3,2,1,0:T(8,128)(2,1)} %collective-permute-done.8.refs_7_), channel_id=1, source_target_pairs={{0,1},{1,2},{2,3},{3,4},{4,5},{5,6},{6,7},{7,8},{8,9},{9,10},{10,1... | collective-permute-start | bytes 884744 | tf_op jit(solution)/shard_map/ppermute | solution.py:110
  69.8 10.1 %collective-permute-start.7 = (bf16[1,8,24,256]{3,2,1,0:T(8,128)(2,1)S(1)}, bf16[1,8,24,256]{3,2,1,0:T(8,128)(2,1)S(1)}, u32[]{:S(2)}, u32[]{:S(2)}) collective-permute-start(bf16[1,8,24,256]{3,2,1,0:T(8,128)(2,1)S(1)} %slice.4), channel_id=1, source_target_pairs={{0,14},{1,15},{2,0},{3,1},{4,2},{5,3},{6,4},{7,5},{8,6},{9,7},{10,... | collective-permute-start | bytes 294920 | tf_op jit(solution)/shard_map/ppermute | solution.py:110
  79.8 26.1 %copy-start.4 = (bf16[1,8,24,256]{3,2,1,0:T(8,128)(2,1)}, bf16[1,8,24,256]{3,2,1,0:T(8,128)(2,1)S(1)}, u32[]{:S(2)}) copy-start(bf16[1,8,24,256]{3,2,1,0:T(8,128)(2,1)S(1)} %collective-permute-done.7.refs_6_) | copy-start | bytes 294916
  79.8 26.1 %copy-start.1 = (bf16[3,8,24,256]{3,2,1,0:T(8,128)(2,1)}, bf16[3,8,24,256]{3,2,1,0:T(8,128)(2,1)S(1)}, u32[]{:S(2)}) copy-start(bf16[3,8,24,256]{3,2,1,0:T(8,128)(2,1)S(1)} %collective-permute-done.6.refs_5_) | copy-start | bytes 884740
  79.9 26.0 %collective-permute-start.12 = (bf16[4,8,24,256]{3,2,1,0:T(8,128)(2,1)S(1)}, bf16[4,8,24,256]{3,2,1,0:T(8,128)(2,1)S(1)}, u32[]{:S(2)}, u32[]{:S(2)}) collective-permute-start(bf16[4,8,24,256]{3,2,1,0:T(8,128)(2,1)S(1)} %pad_maximum_fusion), channel_id=1, source_target_pairs={{0,16},{1,17},{2,18},{3,19},{4,20},{5,21},{6,22},{7,23},{8,24},{9,... | collective-permute-start | bytes 1179656 | tf_op jit(solution)/shard_map/ppermute | solution.py:113
  84.2 14.6 %collective-permute-start.10 = (bf16[3,8,24,256]{3,2,1,0:T(8,128)(2,1)}, bf16[3,8,24,256]{3,2,1,0:T(8,128)(2,1)}, u32[]{:S(2)}, u32[]{:S(2)}) collective-permute-start(bf16[3,8,24,256]{3,2,1,0:T(8,128)(2,1)} %collective-permute-done.8.refs_7_), channel_id=1, source_target_pairs={{0,15},{1,0},{2,1},{3,2},{4,3},{5,4},{6,5},{7,6},{8,7},{9,8},{10,9... | collective-permute-start | bytes 884744 | tf_op jit(solution)/shard_map/ppermute | solution.py:110
  88.3 13.4 %collective-permute-start.5 = (bf16[3,8,24,256]{3,2,1,0:T(8,128)(2,1)}, bf16[3,8,24,256]{3,2,1,0:T(8,128)(2,1)}, u32[]{:S(2)}, u32[]{:S(2)}) collective-permute-start(bf16[3,8,24,256]{3,2,1,0:T(8,128)(2,1)} %collective-permute-done.3.refs_2_), channel_id=1, source_target_pairs={{0,1},{1,2},{2,3},{3,4},{4,5},{5,6},{6,7},{7,8},{8,9},{9,10},{10,1... | collective-permute-start | bytes 884744 | tf_op jit(solution)/shard_map/ppermute | solution.py:110
  90.2 15.7 %collective-permute-start.11 = (bf16[3,8,24,256]{3,2,1,0:T(8,128)(2,1)}, bf16[3,8,24,256]{3,2,1,0:T(8,128)(2,1)}, u32[]{:S(2)}, u32[]{:S(2)}) collective-permute-start(bf16[3,8,24,256]{3,2,1,0:T(8,128)(2,1)} %collective-permute-done.9.refs_8_), channel_id=1, source_target_pairs={{0,1},{1,2},{2,3},{3,4},{4,5},{5,6},{6,7},{7,8},{8,9},{9,10},{10,1... | collective-permute-start | bytes 884744 | tf_op jit(solution)/shard_map/ppermute | solution.py:110
  105.9 0.7 copy-start.6

commit v2 on v1

v2 whole, which is shorter than its diff:
```python
import jax
import jax.numpy as jnp
import numpy as np
from jax import lax
from jax.experimental import pallas as pl
from jax.experimental.pallas import tpu as pltpu
from jax.sharding import PartitionSpec as P

TILE = 8
STEP = 2

OWN_SLOTS = ((0, -5, 5), (-1, -6, 4), (1, -4, 6), (-2, -7, 3), (2, -3, 7), (8,))
NEIGHBOUR_SLOTS = ((0, -5, 5), (-1, -6, 4), (1, -4, 6), (-2, -7, 3), (2, -3, 7, 8))


def row_of(part, window, windows):
    head = windows // TILE * TILE
    if window < head:
        return part * (2 * windows - head) + window
    return head + part * (windows - head) + window - head


def whiten_kernel(bins, spectra_ref, alive_ref, out_ref, copies_ref, rows_ref):
    windows = spectra_ref.shape[1]
    for window in range(windows):
        real = spectra_ref[0, window].astype(jnp.float32)
        imag = spectra_ref[1, window].astype(jnp.float32)
        power = jnp.sum(real * real + imag * imag, axis=0, keepdims=True) / bins
        live = alive_ref[window : window + 1, :].astype(jnp.float32)
        factor = live / jnp.sqrt(jnp.maximum(power, 0.5))
        rows_ref[row_of(0, window, windows)] = real * factor
        rows_ref[row_of(1, window, windows)] = imag * factor
    out_ref[...] = jnp.swapaxes(rows_ref[...], 0, 1).astype(jnp.bfloat16)
    for i in range(copies_ref.shape[0]):
        copies_ref[i] = out_ref[...]


def whiten(spectra, alive, copies):
    _, bins, windows, channels = spectra.shape
    by_window = jnp.swapaxes(spectra, 1, 2)
    return pl.pallas_call(
        lambda *refs: whiten_kernel(bins, *refs),
        out_shape=(
            jax.ShapeDtypeStruct((bins, 2 * windows, channels), jnp.bfloat16),
            jax.ShapeDtypeStruct((copies, bins, 2 * windows, channels), jnp.bfloat16),
        ),
        scratch_shapes=[pltpu.VMEM((2 * windows, bins, channels), jnp.float32)],
        name="whiten",
    )(by_window, alive)


def receiver_kernel(*refs):
    *in_refs, out_ref = refs
    slices, bins, rows, channels = in_refs[0].shape
    head = rows // 2 // TILE * TILE
    tail = rows - head
    half = (tail - head) // 2
    for f in range(bins):
        for piece in range(slices * len(in_refs)):
            block = in_refs[piece // slices][piece % slices, f]
            out_ref[f, piece, :, :channels] = block
            out_ref[f, piece, :head, channels:] = block[tail:]
            out_ref[f, piece, tail:, channels:] = -block[:head]
            mixed = block[head:tail].astype(jnp.float32)
            turned = jnp.concatenate((mixed[half:], -mixed[:half]), axis=0)
            out_ref[f, piece, head:tail, channels:] = turned.astype(jnp.bfloat16)


def receiver_pairs(receivers):
    slices, bins, rows, channels = receivers[0].shape
    total = slices * len(receivers)
    return pl.pallas_call(
        receiver_kernel,
        grid=(bins // STEP,),
        in_specs=[pl.BlockSpec((slices, STEP, rows, channels), lambda f: (0, f, 0, 0))] * len(receivers),
        out_specs=pl.BlockSpec((STEP, total, rows, 2 * channels), lambda f: (f, 0, 0, 0)),
        out_shape=jax.ShapeDtypeStruct((bins, total, rows, 2 * channels), jnp.bfloat16),
        name="receiver_pairs",
    )(*receivers)


def stack_kernel(parities, scale, place_ref, *refs):
    groups = refs[: len(parities)]
    pairs_ref, out_ref, even_ref, odd_ref = refs[len(parities) :]
    channels = groups[0].shape[3]
    parity_at = sum(group.shape[0] for group in groups)
    for f in range(out_ref.shape[1]):
        slot = 0
        for group, parity in zip(groups, parities):
            for i in range(group.shape[0]):
                held = odd_ref if parity[i] else even_ref
                held[f, place_ref[slot]] = group[i, f]
                slot += 1
        pairs = pairs_ref[f].reshape(-1, 2 * channels)
        for held, side in ((even_ref, place_ref[parity_at]), (odd_ref, 1 - place_ref[parity_at])):
            total = lax.dot_general(
                held[f].reshape(-1, channels),
                pairs,
                (((0,), (0,)), ((), ())),
                preferred_element_type=jnp.float32,
            )
            total = (total * scale).astype(jnp.bfloat16)
            at = pl.ds(pl.multiple_of(side * channels, channels), channels)
            out_ref[0, f, at, :] = total[:, :channels]
            out_ref[1, f, at, :] = total[:, channels:]


def stack(groups, parities, place, pairs, scale):
    bins, slices, rows, twice = pairs.shape
    channels = twice // 2
    return pl.pallas_call(
        lambda *refs: stack_kernel(parities, scale, *refs),
        grid=(bins // STEP,),
        in_specs=[pl.BlockSpec(memory_space=pltpu.SMEM)]
        + [pl.BlockSpec((g.shape[0], STEP, rows, channels), lambda f: (0, f, 0, 0)) for g in groups]
        + [pl.BlockSpec((STEP, slices, rows, twice), lambda f: (f, 0, 0, 0))],
        out_specs=pl.BlockSpec((2, STEP, 2 * channels, channels), lambda f: (0, f, 0, 0)),
        out_shape=jax.ShapeDtypeStruct((2, bins, 2 * channels, channels), jnp.bfloat16),
        scratch_shapes=[pltpu.VMEM((STEP, slices, rows, channels), jnp.bfloat16)] * 2,
        name="stack",
    )(place, *groups, pairs)


def body(spectra, alive):
    rows_n, cols_n = lax.axis_size("src"), lax.axis_size("rcv")
    length = cols_n // 2
    windows = spectra.shape[2] * rows_n

    def along(z_of, step):
        return z_of // length * length + (z_of % length + step) % length

    def shift(block, step):
        return lax.ppermute(block, "rcv", [(r, along(r, step)) for r in range(cols_n)])

    def trade(block):
        return lax.ppermute(block, "rcv", [(r, (r + length) % cols_n) for r in range(cols_n)])

    def deal(block, step):
        pairs = [
            (s * cols_n + 2 * d + o, d * cols_n + along(2 * s + o, step))
            for s in range(rows_n)
            for d in range(rows_n)
            for o in range(2)
        ]
        return lax.ppermute(block, ("src", "rcv"), pairs)

    def cross(block, bit):
        return lax.ppermute(block, "src", [(s, s ^ bit) for s in range(rows_n)])

    local, copies = whiten(spectra, alive, rows_n)
    dealt = [deal(local, step)[None] for step in (0, 5, -5)]
    receivers = (lax.all_to_all(copies, "src", 0, 0),)
    first = jnp.concatenate(dealt, axis=0)
    up, down, other = shift(first, 1), shift(first, -1), trade(first)
    up2, down2, far = shift(up, 1), shift(down, -1), shift(down[2:], -2)
    far, pairs = lax.optimization_barrier((far, receiver_pairs(receivers)))
    other_up, other_down = shift(other, 1), shift(other, -1)
    other_up2 = trade(up2)
    last = trade(jnp.concatenate((down2, far), axis=0))

    groups = (first, up, down, up2, down2, far, other, other_up, other_down, other_up2, last)
    own = lax.axis_index("rcv") // length
    z = lax.axis_index("rcv") % length
    offsets = OWN_SLOTS + NEIGHBOUR_SLOTS
    swaps = [i >= len(OWN_SLOTS) for i, group in enumerate(offsets) for _ in group]
    steps = [step % length for group in offsets for step in group]
    row = jnp.where(np.array(swaps), 1 - own, own)
    place = row * (rows_n // 2) + lax.rem(z + np.array(steps, np.int32), length) // 2
    place = jnp.append(place, z % 2).astype(jnp.int32)
    parities = tuple(tuple(step % 2 for step in group) for group in offsets)
    scale = 1.0 / float(windows) ** 0.5
    return stack(groups, parities, place, pairs, scale)


def solution(mesh):
    return jax.shard_map(
        body,
        mesh=mesh,
        in_specs=(P(None, None, "src", "rcv"), P("src", "rcv")),
        out_specs=P(None, None, "src", "rcv"),
        check_vma=False,
    )
```

time: 116 us -> 110 us (0.948)
  the two profiles are of different devices: /device:TPU:28 before, /device:TPU:20 now
where the time goes in v2:
time: 110 us; the launch traced here: 109 us
  starting transfers between devices  67.4 us (61%)
  waiting for transfers between devices  25 us (23%)
  Pallas kernels  13.1 us (12%)
  local copies, waits for them, and re-layouts  2.65 us (2%)
    ppermute x7, starting transfers between devices, shift(): lax.ppermute(block, 'rcv', [(r, along(r, step)) for r in range(cols_n)])  27.4 us
    ppermute x3, starting transfers between devices, deal(): return lax.ppermute(block, ('src', 'rcv'), pairs)  22.8 us
    ppermute x7, waiting for transfers between devices, shift(): lax.ppermute(block, 'rcv', [(r, along(r, step)) for r in range(cols_n)])  12.3 us
    ppermute x3, waiting for transfers between devices, deal(): return lax.ppermute(block, ('src', 'rcv'), pairs)  12 us
    all_to_all x1, starting transfers between devices, body(): receivers = (lax.all_to_all(copies, 'src', 0, 0),)  9.36 us
    ppermute x3, starting transfers between devices, trade(): lax.ppermute(block, 'rcv', [(r, (r + length) % cols_n) for r in range(col...  7.76 us
    pallas_call x1, Pallas kernels, stack(): pl.pallas_call(lambda *refs: stack_kernel(parities, scale, *refs), grid=(...  6.91 us
    pallas_call x1, Pallas kernels, receiver_pairs(): pl.pallas_call(receiver_kernel, grid=(bins // STEP,), in_specs=[pl.BlockS...  3.95 us
  transfers between devices with their start and end apart: 14, of which 5 were waited for; matrix products, arithmetic and copies ran while one was open for 1% of the time, Pallas kernels for 4%

profile of v2, /device:TPU:20, one launch (start us, length us, event | category | flops | bytes accessed | tf_op | source)
XLA Modules:
  0.0 109.2 jit_solution(7606871156333562565)
XLA Ops:
  0.0 2.3 %whiten.1 = (bf16[8,24,256]{2,1,0:T(8,128)(2,1)}, bf16[16,8,24,256]{3,2,1,0:T(8,128)(2,1)}) custom-call(bf16[2,12,8,256]{3,2,1,0:T(8,128)(2,1)} %bitcast.8, s32[12,256]{1,0:T(8,128)} %refs_1_.1), custom_call_target="tpu_custom_call" | custom-call | tf_op jit(solution)/shard_map/whiten/pallas_call | solution.py:41
  2.3 0.0 copy-start.14
  2.3 9.4 %all-to-all-start = ((bf16[16,8,24,256]{3,2,1,0:T(8,128)(2,1)}), bf16[16,8,24,256]{3,2,1,0:T(8,128)(2,1)S(1)}, u32[]{:S(2)}, u32[]{:S(2)}) async-start(bf16[16,8,24,256]{3,2,1,0:T(8,128)(2,1)} %get-tuple-element.10), calls=%async_computation | async-start | bytes 3145728 | tf_op jit(solution)/shard_map/all_to_all | solution.py:152
  11.6 0.0 copy-done.14
  11.6 3.3 %collective-permute-start.2 = (bf16[8,24,256]{2,1,0:T(8,128)(2,1)S(1)}, bf16[8,24,256]{2,1,0:T(8,128)(2,1)S(1)}, u32[]{:S(2)}, u32[]{:S(2)}) collective-permute-start(bf16[8,24,256]{2,1,0:T(8,128)(2,1)S(1)} %copy-done.14), channel_id=1, source_target_pairs={{0,11},{1,12},{2,43},{3,44},{4,75},{5,76},{6,107},{7,108},{8,139},... | collective-permute-start | bytes 294920 | tf_op jit(solution)/shard_map/ppermute | solution.py:145
  14.9 12.9 %collective-permute-start.1 = (bf16[8,24,256]{2,1,0:T(8,128)(2,1)S(1)}, bf16[8,24,256]{2,1,0:T(8,128)(2,1)S(1)}, u32[]{:S(2)}, u32[]{:S(2)}) collective-permute-start(bf16[8,24,256]{2,1,0:T(8,128)(2,1)S(1)} %copy-done.14), channel_id=1, source_target_pairs={{0,5},{1,6},{2,37},{3,38},{4,69},{5,70},{6,101},{7,102},{8,133},{9... | collective-permute-start | bytes 294920 | tf_op jit(solution)/shard_map/ppermute | solution.py:145
  27.9 6.6 %collective-permute-start = (bf16[8,24,256]{2,1,0:T(8,128)(2,1)S(1)}, bf16[8,24,256]{2,1,0:T(8,128)(2,1)S(1)}, u32[]{:S(2)}, u32[]{:S(2)}) collective-permute-start(bf16[8,24,256]{2,1,0:T(8,128)(2,1)S(1)} %copy-done.14), channel_id=1, source_target_pairs={{0,0},{1,1},{2,32},{3,33},{4,64},{5,65},{6,96},{7,97},{8,128},{9,1... | collective-permute-start | bytes 294920 | tf_op jit(solution)/shard_map/ppermute | solution.py:145
  34.4 0.0 collective-permute-done.2
  34.5 0.0 collective-permute-done.1
  34.5 12.0 %collective-permute-done = bf16[8,24,256]{2,1,0:T(8,128)(2,1)S(1)} collective-permute-done((bf16[8,24,256]{2,1,0:T(8,128)(2,1)S(1)}, bf16[8,24,256]{2,1,0:T(8,128)(2,1)S(1)}, u32[]{:S(2)}, u32[]{:S(2)}) %collective-permute-start) | collective-permute-done | bytes 98336 | tf_op jit(solution)/shard_map/ppermute | solution.py:145
  46.5 0.0 copy-start.12
  46.5 0.0 copy-start.13
  46.5 0.0 copy-start.2
  46.5 6.5 %collective-permute-start.4 = (bf16[3,8,24,256]{3,2,1,0:T(8,128)(2,1)S(1)}, bf16[3,8,24,256]{3,2,1,0:T(8,128)(2,1)S(1)}, u32[]{:S(2)}, u32[]{:S(2)}) collective-permute-start(bf16[3,8,24,256]{3,2,1,0:T(8,128)(2,1)S(1)} %pad_maximum_fusion.1.refs_1_), channel_id=1, source_target_pairs={{0,15},{1,0},{2,1},{3,2},{4,3},{5,4},{6,5},{7,6},{8,7},{9,8},{10,9... | collective-permute-start | bytes 884744 | tf_op jit(solution)/shard_map/ppermute | solution.py:133
  53.0 1.9 %collective-permute-start.3 = (bf16[3,8,24,256]{3,2,1,0:T(8,128)(2,1)S(1)}, bf16[3,8,24,256]{3,2,1,0:T(8,128)(2,1)S(1)}, u32[]{:S(2)}, u32[]{:S(2)}) collective-permute-start(bf16[3,8,24,256]{3,2,1,0:T(8,128)(2,1)S(1)} %pad_maximum_fusion.1.refs_1_), channel_id=1, source_target_pairs={{0,1},{1,2},{2,3},{3,4},{4,5},{5,6},{6,7},{7,8},{8,9},{9,10},{10,1... | collective-permute-start | bytes 884744 | tf_op jit(solution)/shard_map/ppermute | solution.py:133
  55.0 5.3 %collective-permute-done.4.refs_3_ = bf16[3,8,24,256]{3,2,1,0:T(8,128)(2,1)S(1)} collective-permute-done((bf16[3,8,24,256]{3,2,1,0:T(8,128)(2,1)S(1)}, bf16[3,8,24,256]{3,2,1,0:T(8,128)(2,1)S(1)}, u32[]{:S(2)}, u32[]{:S(2)}) %collective-permute-start.4) | collective-permute-done | bytes 294944 | tf_op jit(solution)/shard_map/ppermute | solution.py:133
  60.3 0.0 copy-start.3
  60.3 5.6 %collective-permute-start.6 = (bf16[3,8,24,256]{3,2,1,0:T(8,128)(2,1)S(1)}, bf16[3,8,24,256]{3,2,1,0:T(8,128)(2,1)S(1)}, u32[]{:S(2)}, u32[]{:S(2)}) collective-permute-start(bf16[3,8,24,256]{3,2,1,0:T(8,128)(2,1)S(1)} %collective-permute-done.4.refs_3_), channel_id=1, source_target_pairs={{0,15},{1,0},{2,1},{3,2},{4,3},{5,4},{6,5},{7,6},{8,7},{9,8},{10,9... | collective-permute-start | bytes 884744 | tf_op jit(solution)/shard_map/ppermute | solution.py:133
  65.9 1.9 %collective-permute-start.8 = (bf16[3,8,24,256]{3,2,1,0:T(8,128)(2,1)S(1)}, bf16[3,8,24,256]{3,2,1,0:T(8,128)(2,1)S(1)}, u32[]{:S(2)}, u32[]{:S(2)}) collective-permute-start(bf16[3,8,24,256]{3,2,1,0:T(8,128)(2,1)S(1)} %pad_maximum_fusion.1.refs_1_), channel_id=1, source_target_pairs={{0,16},{1,17},{2,18},{3,19},{4,20},{5,21},{6,22},{7,23},{8,24},{9,... | collective-permute-start | bytes 884744 | tf_op jit(solution)/shard_map/ppermute | solution.py:136
  67.8 0.0 collective-permute-done.3.refs_2_
  67.8 0.0 copy-start.6
  67.8 1.9 %collective-permute-start.5 = (bf16[3,8,24,256]{3,2,1,0:T(8,128)(2,1)S(1)}, bf16[3,8,24,256]{3,2,1,0:T(8,128)(2,1)S(1)}, u32[]{:S(2)}, u32[]{:S(2)}) collective-permute-start(bf16[3,8,24,256]{3,2,1,0:T(8,128)(2,1)S(1)} %collective-permute-done.3.refs_2_), channel_id=1, source_target_pairs={{0,1},{1,2},{2,3},{3,4},{4,5},{5,6},{6,7},{7,8},{8,9},{9,10},{10,1... | collective-permute-start | bytes 884744 | tf_op jit(solution)/shard_map/ppermute | solution.py:133
  69.8 3.4 %collective-permute-start.7 = (bf16[1,8,24,256]{3,2,1,0:T(8,128)(2,1)S(1)}, bf16[1,8,24,256]{3,2,1,0:T(8,128)(2,1)S(1)}, u32[]{:S(2)}, u32[]{:S(2)}) collective-permute-start(bf16[1,8,24,256]{3,2,1,0:T(8,128)(2,1)S(1)} %slice.4), channel_id=1, source_target_pairs={{0,14},{1,15},{2,0},{3,1},{4,2},{5,3},{6,4},{7,5},{8,6},{9,7},{10,... | collective-permute-start | bytes 294920 | tf_op jit(solution)/shard_map/ppermute | solution.py:133
  73.2 0.0 all-to-all-done.refs_0_
  73.2 0.0 copy-start
  73.2 1.1 %copy-done = bf16[16,8,24,256]{3,2,1,0:T(8,128)(2,1)} copy-done((bf16[16,8,24,256]{3,2,1,0:T(8,128)(2,1)}, bf16[16,8,24,256]{3,2,1,0:T(8,128)(2,1)S(1)}, u32[]{:S(2)}) %copy-start) | copy-done | bytes 1572888
  74.3 4.0 %receiver_pairs.1.refs_12_ = bf16[8,16,24,512]{3,2,1,0:T(8,128)(2,1)} custom-call(bf16[16,8,24,256]{3,2,1,0:T(8,128)(2,1)} %copy-done), custom_call_target="tpu_custom_call" | custom-call | tf_op jit(solution)/shard_map/receiver_pairs/pallas_call | solution.py:72
  78.3 0.0 collective-permute-done.7.refs_6_
  78.3 0.0 copy-start.4
  78.3 0.0 collective-permute-done.6.refs_5_
  78.3 0.0 copy-start.1
  78.3 3.9 %collective-permute-start.12 = (bf16[4,8,24,256]{3,2,1,0:T(8,128)(2,1)S(1)}, bf16[4,8,24,256]{3,2,1,0:T(8,128)(2,1)S(1)}, u32[]{:S(2)}, u32[]{:S(2)}) collective-permute-start(bf16[4,8,24,256]{3,2,1,0:T(8,128)(2,1)S(1)} %pad_maximum_fusion), channel_id=1, source_target_pairs={{0,16},{1,17},{2,18},{3,19},{4,20},{5,21},{6,22},{7,23},{8,24},{9,... | collective-permute-start | bytes 1179656 | tf_op jit(solution)/shard_map/ppermute | solution.py:136
  82.3 0.0 collective-permute-done.8.refs_7_
  82.3 0.0 copy-start.7
  82.3 6.2 %collective-permute-start.10 = (bf16[3,8,24,256]{3,2,1,0:T(8,128)(2,1)S(1)}, bf16[3,8,24,256]{3,2,1,0:T(8,128)(2,1)S(1)}, u32[]{:S(2)}, u32[]{:S(2)}) collective-permute-start(bf16[3,8,24,256]{3,2,1,0:T(8,128)(2,1)S(1)} %collective-permute-done.8.refs_7_), channel_id=1, source_target_pairs={{0,15},{1,0},{2,1},{3,2},{4,3},{5,4},{6,5},{7,6},{8,7},{9,8},{10,9... | collective-permute-start | bytes 884744 | tf_op jit(solution)/shard_map/ppermute | solution.py:133
  88.5 1.9 %collective-permute-start.9 = (bf16[3,8,24,256]{3,2,1,0:T(8,128)(2,1)S(1)}, bf16[3,8,24,256]{3,2,1,0:T(8,128)(2,1)S(1)}, u32[]{:S(2)}, u32[]{:S(2)}) collective-permute-start(bf16[3,8,24,256]{3,2,1,0:T(8,128)(2,1)S(1)} %collective-permute-done.8.refs_7_), channel_id=1, source_target_pairs={{0,1},{1,2},{2,3},{3,4},{4,5},{5,6},{6,7},{7,8},{8,9},{9,10},{10,1... | collective-permute-start | bytes 884744 | tf_op jit(solution)/shard_map/ppermute | solution.py:133
  90.5 0.0 collective-permute-done.5.refs_4_
  90.5 0.0 copy-start.8
  90.5 1.9 %collective-permute-start.11 = (bf16[3,8,24,256]{3,2,1,0:T(8,128)(2,1)S(1)}, bf16[3,8,24,256]{3,2,1,0:T(8,128)(2,1)S(1)}, u32[]{:S(2)}, u32[]{:S(2)}) collective-permute-start(bf16[3,8,24,256]{3,2,1,0:T(8,128)(2,1)S(1)} %collective-permute-done.5.refs_4_), channel_id=1, source_target_pairs={{0,16},{1,17},{2,18},{3,19},{4,20},{5,21},{6,22},{7,23},{8,24},{9,... | collective-permute-start | bytes 884744 | tf_op jit(solution)/shard_map/ppermute | solution.py:136
  92.4 0.0 copy-done.12
  92.4 0.0 copy-done.13
  92.5 0.6 pad_add_fusion.refs_0_
  93.1 1.6 %collective-permute-done.10.refs_9_ = bf16[3,8,24,256]{3,2,1,0:T(8,128)(2,1)S(1)} collective-permute-done((bf16[3,8,24,256]{3,2,1,0:T(8,128)(2,1)S(1)}, bf16[3,8,24,256]{3,2,1,0:T(8,128)(2,1)S(1)}, u32[]{:S(2)}, u32[]{:S(2)}) %collective-permute-start.10) | collective-permute-done | bytes 294944 | tf_op jit(solution)/shard_map/ppermute | solution.py:133
  94.7 0.0 copy-start.9
  94.7 5.3 %collective-permute-done.9.refs_8_ = bf16[3,8,24,256]{3,2,1,0:T(8,128)(2,1)S(1)} collective-permute-done((bf16[3,8,24,256]{3,2,1,0:T(8,128)(2,1)S(1)}, bf16[3,8,24,256]{3,2,1,0:T(8,128)(2,1)S(1)}, u32[]{:S(2)}, u32[]{:S(2)}) %collective-permute-start.9) | collective-permute-done | bytes 294944 | tf_op jit(solution)/shard_map/ppermute | solution.py:133
  100.0 0.0 copy-start.10
  100.0 0.7 collective-permute-done.11.refs_10_
  100.7 0.0 copy-start.11
  100.7 0.7 copy-done.11
  101.5 0.0 collective-permute-done.12.refs_11_
  101.5 0.0 copy-done.2
  101.5 0.0 copy-done.3
  101.5 0.0 copy-done.6
  101.5 0.0 copy-done.4
  101.5 0.0 copy-done.1
  101.5 0.0 copy-done.7
  101.5 0.0 copy-done.8
  101.5 0.0 copy-done.9
  101.5 0.0 copy-done.10
  101.5 0.0 copy-start.5
  101.5 0.7 copy-done.5
  102.3 6.9 %stack.1 = bf16[2,8,512,256]{3,2,1,0:T(8,128)(2,1)} custom-call(s32[33]{0:T(128)} %pad_add_fusion.refs_0_, bf16[3,8,24,256]{3,2,1,0:T(8,128)(2,1)} %copy-done.2, bf16[3,8,24,256]{3,2,1,0:T(8,128)(2,1)} %copy-done.6, bf16[3,8,24,256]{3,2,1,0:T(8,128)(2,1)} %copy-done.3, bf16[3,8,24,256]{3,2,1,0:T(8,128)(2,1)} %copy-done.8, bf16[3,8,24,256]{3,2,1,0:T(8,128)(2,1)} %copy-done.1, ...), custom_call_target="tpu_custom_call" | custom-call | tf_op jit(solution)/shard_map/stack/pallas_call | solution.py:111
  (4 shorter events, 0.1 us)
Async XLA Ops:
  2.3 9.4 %copy-start.14 = (bf16[8,24,256]{2,1,0:T(8,128)(2,1)S(1)}, bf16[8,24,256]{2,1,0:T(8,128)(2,1)}, u32[]{:S(2)}) copy-start(bf16[8,24,256]{2,1,0:T(8,128)(2,1)} %get-tuple-element.9) | copy-start | bytes 294916
  2.3 70.9 %all-to-all-start = ((bf16[16,8,24,256]{3,2,1,0:T(8,128)(2,1)}), bf16[16,8,24,256]{3,2,1,0:T(8,128)(2,1)S(1)}, u32[]{:S(2)}, u32[]{:S(2)}) async-start(bf16[16,8,24,256]{3,2,1,0:T(8,128)(2,1)} %get-tuple-element.10), calls=%async_computation | async-start | bytes 3145728 | tf_op jit(solution)/shard_map/all_to_all | solution.py:152
  11.6 22.8 %collective-permute-start.2 = (bf16[8,24,256]{2,1,0:T(8,128)(2,1)S(1)}, bf16[8,24,256]{2,1,0:T(8,128)(2,1)S(1)}, u32[]{:S(2)}, u32[]{:S(2)}) collective-permute-start(bf16[8,24,256]{2,1,0:T(8,128)(2,1)S(1)} %copy-done.14), channel_id=1, source_target_pairs={{0,11},{1,12},{2,43},{3,44},{4,75},{5,76},{6,107},{7,108},{8,139},... | collective-permute-start | bytes 294920 | tf_op jit(solution)/shard_map/ppermute | solution.py:145
  14.9 19.5 %collective-permute-start.1 = (bf16[8,24,256]{2,1,0:T(8,128)(2,1)S(1)}, bf16[8,24,256]{2,1,0:T(8,128)(2,1)S(1)}, u32[]{:S(2)}, u32[]{:S(2)}) collective-permute-start(bf16[8,24,256]{2,1,0:T(8,128)(2,1)S(1)} %copy-done.14), channel_id=1, source_target_pairs={{0,5},{1,6},{2,37},{3,38},{4,69},{5,70},{6,101},{7,102},{8,133},{9... | collective-permute-start | bytes 294920 | tf_op jit(solution)/shard_map/ppermute | solution.py:145
  27.9 18.6 %collective-permute-start = (bf16[8,24,256]{2,1,0:T(8,128)(2,1)S(1)}, bf16[8,24,256]{2,1,0:T(8,128)(2,1)S(1)}, u32[]{:S(2)}, u32[]{:S(2)}) collective-permute-start(bf16[8,24,256]{2,1,0:T(8,128)(2,1)S(1)} %copy-done.14), channel_id=1, source_target_pairs={{0,0},{1,1},{2,32},{3,33},{4,64},{5,65},{6,96},{7,97},{8,128},{9,1... | collective-permute-start | bytes 294920 | tf_op jit(solution)/shard_map/ppermute | solution.py:145
  46.5 46.0 %copy-start.12 = (s32[32]{0:T(128)S(1)}, s32[32]{0:T(128)}, u32[]{:S(2)}) copy-start(s32[32]{0:T(128)} %constant.60.clone) | copy-start | bytes 388
  46.5 46.0 %copy-start.13 = (pred[32]{0:T(512)(128)(4,1)S(1)}, pred[32]{0:T(512)(128)(4,1)}, u32[]{:S(2)}) copy-start(pred[32]{0:T(512)(128)(4,1)} %constant.59.clone) | copy-start | bytes 100
  46.5 55.0 %copy-start.2 = (bf16[3,8,24,256]{3,2,1,0:T(8,128)(2,1)}, bf16[3,8,24,256]{3,2,1,0:T(8,128)(2,1)S(1)}, u32[]{:S(2)}) copy-start(bf16[3,8,24,256]{3,2,1,0:T(8,128)(2,1)S(1)} %pad_maximum_fusion.1.refs_1_) | copy-start | bytes 884740
  46.5 13.8 %collective-permute-start.4 = (bf16[3,8,24,256]{3,2,1,0:T(8,128)(2,1)S(1)}, bf16[3,8,24,256]{3,2,1,0:T(8,128)(2,1)S(1)}, u32[]{:S(2)}, u32[]{:S(2)}) collective-permute-start(bf16[3,8,24,256]{3,2,1,0:T(8,128)(2,1)S(1)} %pad_maximum_fusion.1.refs_1_), channel_id=1, source_target_pairs={{0,15},{1,0},{2,1},{3,2},{4,3},{5,4},{6,5},{7,6},{8,7},{9,8},{10,9... | collective-permute-start | bytes 884744 | tf_op jit(solution)/shard_map/ppermute | solution.py:133
  53.0 14.8 %collective-permute-start.3 = (bf16[3,8,24,256]{3,2,1,0:T(8,128)(2,1)S(1)}, bf16[3,8,24,256]{3,2,1,0:T(8,128)(2,1)S(1)}, u32[]{:S(2)}, u32[]{:S(2)}) collective-permute-start(bf16[3,8,24,256]{3,2,1,0:T(8,128)(2,1)S(1)} %pad_maximum_fusion.1.refs_1_), channel_id=1, source_target_pairs={{0,1},{1,2},{2,3},{3,4},{4,5},{5,6},{6,7},{7,8},{8,9},{9,10},{10,1... | collective-permute-start | bytes 884744 | tf_op jit(solution)/shard_map/ppermute | solution.py:133
  60.3 41.2 %copy-start.3 = (bf16[3,8,24,256]{3,2,1,0:T(8,128)(2,1)}, bf16[3,8,24,256]{3,2,1,0:T(8,128)(2,1)S(1)}, u32[]{:S(2)}) copy-start(bf16[3,8,24,256]{3,2,1,0:T(8,128)(2,1)S(1)} %collective-permute-done.4.refs_3_) | copy-start | bytes 884740
  60.3 18.0 %collective-permute-start.6 = (bf16[3,8,24,256]{3,2,1,0:T(8,128)(2,1)S(1)}, bf16[3,8,24,256]{3,2,1,0:T(8,128)(2,1)S(1)}, u32[]{:S(2)}, u32[]{:S(2)}) collective-permute-start(bf16[3,8,24,256]{3,2,1,0:T(8,128)(2,1)S(1)} %collective-permute-done.4.refs_3_), channel_id=1, source_target_pairs={{0,15},{1,0},{2,1},{3,2},{4,3},{5,4},{6,5},{7,6},{8,7},{9,8},{10,9... | collective-permute-start | bytes 884744 | tf_op jit(solution)/shard_map/ppermute | solution.py:133
  65.9 16.4 %collective-permute-start.8 = (bf16[3,8,24,256]{3,2,1,0:T(8,128)(2,1)S(1)}, bf16[3,8,24,256]{3,2,1,0:T(8,128)(2,1)S(1)}, u32[]{:S(2)}, u32[]{:S(2)}) collective-permute-start(bf16[3,8,24,256]{3,2,1,0:T(8,128)(2,1)S(1)} %pad_maximum_fusion.1.refs_1_), channel_id=1, source_target_pairs={{0,16},{1,17},{2,18},{3,19},{4,20},{5,21},{6,22},{7,23},{8,24},{9,... | collective-permute-start | bytes 884744 | tf_op jit(solution)/shard_map/ppermute | solution.py:136
  67.8 33.6 %copy-start.6 = (bf16[3,8,24,256]{3,2,1,0:T(8,128)(2,1)}, bf16[3,8,24,256]{3,2,1,0:T(8,128)(2,1)S(1)}, u32[]{:S(2)}) copy-start(bf16[3,8,24,256]{3,2,1,0:T(8,128)(2,1)S(1)} %collective-permute-done.3.refs_2_) | copy-start | bytes 884740
  67.8 22.6 %collective-permute-start.5 = (bf16[3,8,24,256]{3,2,1,0:T(8,128)(2,1)S(1)}, bf16[3,8,24,256]{3,2,1,0:T(8,128)(2,1)S(1)}, u32[]{:S(2)}, u32[]{:S(2)}) collective-permute-start(bf16[3,8,24,256]{3,2,1,0:T(8,128)(2,1)S(1)} %collective-permute-done.3.refs_2_), channel_id=1, source_target_pairs={{0,1},{1,2},{2,3},{3,4},{4,5},{5,6},{6,7},{7,8},{8,9},{9,10},{10,1... | collective-permute-start | bytes 884744 | tf_op jit(solution)/shard_map/ppermute | solution.py:133
  69.8 8.5 %collective-permute-start.7 = (bf16[1,8,24,256]{3,2,1,0:T(8,128)(2,1)S(1)}, bf16[1,8,24,256]{3,2,1,0:T(8,128)(2,1)S(1)}, u32[]{:S(2)}, u32[]{:S(2)}) collective-permute-start(bf16[1,8,24,256]{3,2,1,0:T(8,128)(2,1)S(1)} %slice.4), channel_id=1, source_target_pairs={{0,14},{1,15},{2,0},{3,1},{4,2},{5,3},{6,4},{7,5},{8,6},{9,7},{10,... | collective-permute-start | bytes 294920 | tf_op jit(solution)/shard_map/ppermute | solution.py:133
  73.2 1.1 %copy-start = (bf16[16,8,24,256]{3,2,1,0:T(8,128)(2,1)}, bf16[16,8,24,256]{3,2,1,0:T(8,128)(2,1)S(1)}, u32[]{:S(2)}) copy-start(bf16[16,8,24,256]{3,2,1,0:T(8,128)(2,1)S(1)} %all-to-all-done.refs_0_) | copy-start | bytes 4718596
  78.3 23.2 %copy-start.4 = (bf16[1,8,24,256]{3,2,1,0:T(8,128)(2,1)}, bf16[1,8,24,256]{3,2,1,0:T(8,128)(2,1)S(1)}, u32[]{:S(2)}) copy-start(bf16[1,8,24,256]{3,2,1,0:T(8,128)(2,1)S(1)} %collective-permute-done.7.refs_6_) | copy-start | bytes 294916
  78.3 23.2 %copy-start.1 = (bf16[3,8,24,256]{3,2,1,0:T(8,128)(2,1)}, bf16[3,8,24,256]{3,2,1,0:T(8,128)(2,1)S(1)}, u32[]{:S(2)}) copy-start(bf16[3,8,24,256]{3,2,1,0:T(8,128)(2,1)S(1)} %collective-permute-done.6.refs_5_) | copy-start | bytes 884740
  78.3 23.1 %collective-permute-start.12 = (bf16[4,8,24,256]{3,2,1,0:T(8,128)(2,1)S(1)}, bf16[4,8,24,256]{3,2,1,0:T(8,128)(2,1)S(1)}, u32[]{:S(2)}, u32[]{:S(2)}) collective-permute-start(bf16[4,8,24,256]{3,2,1,0:T(8,128)(2,1)S(1)} %pad_maximum_fusion), channel_id=1, source_target_pairs={{0,16},{1,17},{2,18},{3,19},{4,20},{5,21},{6,22},{7,23},{8,24},{9,... | collective-permute-start | bytes 1179656 | tf_op jit(solution)/shard_map/ppermute | solution.py:136
  82.3 19.2 %copy-start.7 = (bf16[3,8,24,256]{3,2,1,0:T(8,128)(2,1)}, bf16[3,8,24,256]{3,2,1,0:T(8,128)(2,1)S(1)}, u32[]{:S(2)}) copy-start(bf16[3,8,24,256]{3,2,1,0:T(8,128)(2,1)S(1)} %collective-permute-done.8.refs_7_) | copy-start | bytes 884740
  82.3 12.4 %collective-permute-start.10 = (bf16[3,8,24,256]{3,2,1,0:T(8,128)(2,1)S(1)}, bf16[3,8,24,256]{3,2,1,0:T(8,128)(2,1)S(1)}, u32[]{:S(2)}, u32[]{:S(2)}) collective-permute-start(bf16[3,8,24,256]{3,2,1,0:T(8,128)(2,1)S(1)} %collective-permute-done.8.refs_7_), channel_id=1, source_target_pairs={{0,15},{1,0},{2,1},{3,2},{4,3},{5,4},{6,5},{7,6},{8,7},{9,8},{10,9... | collective-permute-start | bytes 884744 | tf_op jit(solution)/shard_map/ppermute | solution.py:133
  88.5 11.5 %collective-permute-start.9 = (bf16[3,8,24,256]{3,2,1,0:T(8,128)(2,1)S(1)}, bf16[3,8,24,256]{3,2,1,0:T(8,128)(2,1)S(1)}, u32[]{:S(2)}, u32[]{:S(2)}) collective-permute-start(bf16[3,8,24,256]{3,2,1,0:T(8,128)(2,1)S(1)} %collective-permute-done.8.refs_7_), channel_id=1, source_target_pairs={{0,1},{1,2},{2,3},{3,4},{4,5},{5,6},{6,7},{7,8},{8,9},{9,10},{10,1... | collective-permute-start | bytes 884744 | tf_op jit(solution)/shard_map/ppermute | solution.py:133
  90.5 11.0 %copy-start.8 = (bf16[3,8,24,256]{3,2,1,0:T(8,128)(2,1)}, bf16[3,8,24,256]{3,2,1,0:T(8,128)(2,1)S(1)}, u32[]{:S(2)}) copy-start(bf16[3,8,24,256]{3,2,1,0:T(8,128)(2,1)S(1)} %collective-permute-done.5.refs_4_) | copy-start | bytes 884740
  90.5 10.3 %collective-permute-start.11 = (bf16[3,8,24,256]{3,2,1,0:T(8,128)(2,1)S(1)}, bf16[3,8,24,256]{3,2,1,0:T(8,128)(2,1)S(1)}, u32[]{:S(2)}, u32[]{:S(2)}) collective-permute-start(bf16[3,8,24,256]{3,2,1,0:T(8,128)(2,1)S(1)} %collective-permute-done.5.refs_4_), channel_id=1, source_target_pairs={{0,16},{1,17},{2,18},{3,19},{4,20},{5,21},{6,22},{7,23},{8,24},{9,... | collective-permute-start | bytes 884744 | tf_op jit(solution)/shard_map/ppermute | solution.py:136
  94.7 6.8 %copy-start.9 = (bf16[3,8,24,256]{3,2,1,0:T(8,128)(2,1)}, bf16[3,8,24,256]{3,2,1,0:T(8,128)(2,1)S(1)}, u32[]{:S(2)}) copy-start(bf16[3,8,24,256]{3,2,1,0:T(8,128)(2,1)S(1)} %collective-permute-done.10.refs_9_) | copy-start | bytes 884740
  100.0 1.5 %copy-start.10 = (bf16[3,8,24,256]{3,2,1,0:T(8,128)(2,1)}, bf16[3,8,24,256]{3,2,1,0:T(8,128)(2,1)S(1)}, u32[]{:S(2)}) copy-start(bf16[3,8,24,256]{3,2,1,0:T(8,128)(2,1)S(1)} %collective-permute-done.9.refs_8_) | copy-start | bytes 884740
  100.7 0.7 copy-start.11
  101.5 0.8 copy-start.5

commit v3 on v2

--- a/solution.py
+++ b/solution.py
@@ -7,6 +7,7 @@
 from jax.sharding import PartitionSpec as P
 
 TILE = 8
+STACK_STEP = 4
 STEP = 2
 
 OWN_SLOTS = ((0, -5, 5), (-1, -6, 4), (1, -4, 6), (-2, -7, 3), (2, -3, 7), (8,))
@@ -110,13 +111,13 @@
     channels = twice // 2
     return pl.pallas_call(
         lambda *refs: stack_kernel(parities, scale, *refs),
-        grid=(bins // STEP,),
+        grid=(bins // STACK_STEP,),
         in_specs=[pl.BlockSpec(memory_space=pltpu.SMEM)]
-        + [pl.BlockSpec((g.shape[0], STEP, rows, channels), lambda f: (0, f, 0, 0)) for g in groups]
-        + [pl.BlockSpec((STEP, slices, rows, twice), lambda f: (f, 0, 0, 0))],
-        out_specs=pl.BlockSpec((2, STEP, 2 * channels, channels), lambda f: (0, f, 0, 0)),
+        + [pl.BlockSpec((g.shape[0], STACK_STEP, rows, channels), lambda f: (0, f, 0, 0)) for g in groups]
+        + [pl.BlockSpec((STACK_STEP, slices, rows, twice), lambda f: (f, 0, 0, 0))],
+        out_specs=pl.BlockSpec((2, STACK_STEP, 2 * channels, channels), lambda f: (0, f, 0, 0)),
         out_shape=jax.ShapeDtypeStruct((2, bins, 2 * channels, channels), jnp.bfloat16),
-        scratch_shapes=[pltpu.VMEM((STEP, slices, rows, channels), jnp.bfloat16)] * 2,
+        scratch_shapes=[pltpu.VMEM((STACK_STEP, slices, rows, channels), jnp.bfloat16)] * 2,
         name="stack",
     )(place, *groups, pairs)
 

time: 110 us -> 109 us (level)
  no operation moved by 1% of the time
where the time goes in v3:
time: 109 us; the launch traced here: 108 us
  starting transfers between devices  67.4 us (62%)
  waiting for transfers between devices  25 us (23%)
  Pallas kernels  12.3 us (11%)
  local copies, waits for them, and re-layouts  2.65 us (2%)
    ppermute x7, starting transfers between devices, shift(): lax.ppermute(block, 'rcv', [(r, along(r, step)) for r in range(cols_n)])  27.4 us
    ppermute x3, starting transfers between devices, deal(): return lax.ppermute(block, ('src', 'rcv'), pairs)  22.8 us
    ppermute x7, waiting for transfers between devices, shift(): lax.ppermute(block, 'rcv', [(r, along(r, step)) for r in range(cols_n)])  12.3 us
    ppermute x3, waiting for transfers between devices, deal(): return lax.ppermute(block, ('src', 'rcv'), pairs)  12 us
    all_to_all x1, starting transfers between devices, body(): receivers = (lax.all_to_all(copies, 'src', 0, 0),)  9.36 us
    ppermute x3, starting transfers between devices, trade(): lax.ppermute(block, 'rcv', [(r, (r + length) % cols_n) for r in range(col...  7.76 us
    pallas_call x1, Pallas kernels, stack(): pl.pallas_call(lambda *refs: stack_kernel(parities, scale, *refs), grid=(...  6.04 us
    pallas_call x1, Pallas kernels, receiver_pairs(): pl.pallas_call(receiver_kernel, grid=(bins // STEP,), in_specs=[pl.BlockS...  3.95 us
  transfers between devices with their start and end apart: 14, of which 5 were waited for; matrix products, arithmetic and copies ran while one was open for 1% of the time, Pallas kernels for 4%

profile of v3, /device:TPU:20, one launch (start us, length us, event | category | flops | bytes accessed | tf_op | source)
XLA Modules:
  0.0 108.3 jit_solution(6244857784728516029)
XLA Ops:
  0.0 2.3 %whiten.1 = (bf16[8,24,256]{2,1,0:T(8,128)(2,1)}, bf16[16,8,24,256]{3,2,1,0:T(8,128)(2,1)}) custom-call(bf16[2,12,8,256]{3,2,1,0:T(8,128)(2,1)} %bitcast.8, s32[12,256]{1,0:T(8,128)} %refs_1_.1), custom_call_target="tpu_custom_call" | custom-call | tf_op jit(solution)/shard_map/whiten/pallas_call | solution.py:42
  2.3 0.0 copy-start.14
  2.3 9.4 %all-to-all-start = ((bf16[16,8,24,256]{3,2,1,0:T(8,128)(2,1)}), bf16[16,8,24,256]{3,2,1,0:T(8,128)(2,1)S(1)}, u32[]{:S(2)}, u32[]{:S(2)}) async-start(bf16[16,8,24,256]{3,2,1,0:T(8,128)(2,1)} %get-tuple-element.10), calls=%async_computation | async-start | bytes 3145728 | tf_op jit(solution)/shard_map/all_to_all | solution.py:153
  11.6 0.0 copy-done.14
  11.6 3.3 %collective-permute-start.2 = (bf16[8,24,256]{2,1,0:T(8,128)(2,1)S(1)}, bf16[8,24,256]{2,1,0:T(8,128)(2,1)S(1)}, u32[]{:S(2)}, u32[]{:S(2)}) collective-permute-start(bf16[8,24,256]{2,1,0:T(8,128)(2,1)S(1)} %copy-done.14), channel_id=1, source_target_pairs={{0,11},{1,12},{2,43},{3,44},{4,75},{5,76},{6,107},{7,108},{8,139},... | collective-permute-start | bytes 294920 | tf_op jit(solution)/shard_map/ppermute | solution.py:146
  14.9 12.9 %collective-permute-start.1 = (bf16[8,24,256]{2,1,0:T(8,128)(2,1)S(1)}, bf16[8,24,256]{2,1,0:T(8,128)(2,1)S(1)}, u32[]{:S(2)}, u32[]{:S(2)}) collective-permute-start(bf16[8,24,256]{2,1,0:T(8,128)(2,1)S(1)} %copy-done.14), channel_id=1, source_target_pairs={{0,5},{1,6},{2,37},{3,38},{4,69},{5,70},{6,101},{7,102},{8,133},{9... | collective-permute-start | bytes 294920 | tf_op jit(solution)/shard_map/ppermute | solution.py:146
  27.9 6.6 %collective-permute-start = (bf16[8,24,256]{2,1,0:T(8,128)(2,1)S(1)}, bf16[8,24,256]{2,1,0:T(8,128)(2,1)S(1)}, u32[]{:S(2)}, u32[]{:S(2)}) collective-permute-start(bf16[8,24,256]{2,1,0:T(8,128)(2,1)S(1)} %copy-done.14), channel_id=1, source_target_pairs={{0,0},{1,1},{2,32},{3,33},{4,64},{5,65},{6,96},{7,97},{8,128},{9,1... | collective-permute-start | bytes 294920 | tf_op jit(solution)/shard_map/ppermute | solution.py:146
  34.4 0.0 collective-permute-done.2
  34.5 0.0 collective-permute-done.1
  34.5 12.0 %collective-permute-done = bf16[8,24,256]{2,1,0:T(8,128)(2,1)S(1)} collective-permute-done((bf16[8,24,256]{2,1,0:T(8,128)(2,1)S(1)}, bf16[8,24,256]{2,1,0:T(8,128)(2,1)S(1)}, u32[]{:S(2)}, u32[]{:S(2)}) %collective-permute-start) | collective-permute-done | bytes 98336 | tf_op jit(solution)/shard_map/ppermute | solution.py:146
  46.5 0.0 copy-start.12
  46.5 0.0 copy-start.13
  46.5 0.0 copy-start.2
  46.5 6.5 %collective-permute-start.4 = (bf16[3,8,24,256]{3,2,1,0:T(8,128)(2,1)S(1)}, bf16[3,8,24,256]{3,2,1,0:T(8,128)(2,1)S(1)}, u32[]{:S(2)}, u32[]{:S(2)}) collective-permute-start(bf16[3,8,24,256]{3,2,1,0:T(8,128)(2,1)S(1)} %pad_maximum_fusion.1.refs_1_), channel_id=1, source_target_pairs={{0,15},{1,0},{2,1},{3,2},{4,3},{5,4},{6,5},{7,6},{8,7},{9,8},{10,9... | collective-permute-start | bytes 884744 | tf_op jit(solution)/shard_map/ppermute | solution.py:134
  53.0 1.9 %collective-permute-start.3 = (bf16[3,8,24,256]{3,2,1,0:T(8,128)(2,1)S(1)}, bf16[3,8,24,256]{3,2,1,0:T(8,128)(2,1)S(1)}, u32[]{:S(2)}, u32[]{:S(2)}) collective-permute-start(bf16[3,8,24,256]{3,2,1,0:T(8,128)(2,1)S(1)} %pad_maximum_fusion.1.refs_1_), channel_id=1, source_target_pairs={{0,1},{1,2},{2,3},{3,4},{4,5},{5,6},{6,7},{7,8},{8,9},{9,10},{10,1... | collective-permute-start | bytes 884744 | tf_op jit(solution)/shard_map/ppermute | solution.py:134
  55.0 5.3 %collective-permute-done.4.refs_3_ = bf16[3,8,24,256]{3,2,1,0:T(8,128)(2,1)S(1)} collective-permute-done((bf16[3,8,24,256]{3,2,1,0:T(8,128)(2,1)S(1)}, bf16[3,8,24,256]{3,2,1,0:T(8,128)(2,1)S(1)}, u32[]{:S(2)}, u32[]{:S(2)}) %collective-permute-start.4) | collective-permute-done | bytes 294944 | tf_op jit(solution)/shard_map/ppermute | solution.py:134
  60.3 0.0 copy-start.3
  60.3 5.6 %collective-permute-start.6 = (bf16[3,8,24,256]{3,2,1,0:T(8,128)(2,1)S(1)}, bf16[3,8,24,256]{3,2,1,0:T(8,128)(2,1)S(1)}, u32[]{:S(2)}, u32[]{:S(2)}) collective-permute-start(bf16[3,8,24,256]{3,2,1,0:T(8,128)(2,1)S(1)} %collective-permute-done.4.refs_3_), channel_id=1, source_target_pairs={{0,15},{1,0},{2,1},{3,2},{4,3},{5,4},{6,5},{7,6},{8,7},{9,8},{10,9... | collective-permute-start | bytes 884744 | tf_op jit(solution)/shard_map/ppermute | solution.py:134
  65.9 1.9 %collective-permute-start.8 = (bf16[3,8,24,256]{3,2,1,0:T(8,128)(2,1)S(1)}, bf16[3,8,24,256]{3,2,1,0:T(8,128)(2,1)S(1)}, u32[]{:S(2)}, u32[]{:S(2)}) collective-permute-start(bf16[3,8,24,256]{3,2,1,0:T(8,128)(2,1)S(1)} %pad_maximum_fusion.1.refs_1_), channel_id=1, source_target_pairs={{0,16},{1,17},{2,18},{3,19},{4,20},{5,21},{6,22},{7,23},{8,24},{9,... | collective-permute-start | bytes 884744 | tf_op jit(solution)/shard_map/ppermute | solution.py:137
  67.8 0.0 collective-permute-done.3.refs_2_
  67.8 0.0 copy-start.6
  67.8 1.9 %collective-permute-start.5 = (bf16[3,8,24,256]{3,2,1,0:T(8,128)(2,1)S(1)}, bf16[3,8,24,256]{3,2,1,0:T(8,128)(2,1)S(1)}, u32[]{:S(2)}, u32[]{:S(2)}) collective-permute-start(bf16[3,8,24,256]{3,2,1,0:T(8,128)(2,1)S(1)} %collective-permute-done.3.refs_2_), channel_id=1, source_target_pairs={{0,1},{1,2},{2,3},{3,4},{4,5},{5,6},{6,7},{7,8},{8,9},{9,10},{10,1... | collective-permute-start | bytes 884744 | tf_op jit(solution)/shard_map/ppermute | solution.py:134
  69.8 3.4 %collective-permute-start.7 = (bf16[1,8,24,256]{3,2,1,0:T(8,128)(2,1)S(1)}, bf16[1,8,24,256]{3,2,1,0:T(8,128)(2,1)S(1)}, u32[]{:S(2)}, u32[]{:S(2)}) collective-permute-start(bf16[1,8,24,256]{3,2,1,0:T(8,128)(2,1)S(1)} %slice.4), channel_id=1, source_target_pairs={{0,14},{1,15},{2,0},{3,1},{4,2},{5,3},{6,4},{7,5},{8,6},{9,7},{10,... | collective-permute-start | bytes 294920 | tf_op jit(solution)/shard_map/ppermute | solution.py:134
  73.2 0.0 all-to-all-done.refs_0_
  73.2 0.0 copy-start
  73.2 1.1 %copy-done = bf16[16,8,24,256]{3,2,1,0:T(8,128)(2,1)} copy-done((bf16[16,8,24,256]{3,2,1,0:T(8,128)(2,1)}, bf16[16,8,24,256]{3,2,1,0:T(8,128)(2,1)S(1)}, u32[]{:S(2)}) %copy-start) | copy-done | bytes 1572888
  74.3 4.0 %receiver_pairs.1.refs_12_ = bf16[8,16,24,512]{3,2,1,0:T(8,128)(2,1)} custom-call(bf16[16,8,24,256]{3,2,1,0:T(8,128)(2,1)} %copy-done), custom_call_target="tpu_custom_call" | custom-call | tf_op jit(solution)/shard_map/receiver_pairs/pallas_call | solution.py:73
  78.3 0.0 collective-permute-done.7.refs_6_
  78.3 0.0 copy-start.4
  78.3 0.0 collective-permute-done.6.refs_5_
  78.3 0.0 copy-start.1
  78.3 3.9 %collective-permute-start.12 = (bf16[4,8,24,256]{3,2,1,0:T(8,128)(2,1)S(1)}, bf16[4,8,24,256]{3,2,1,0:T(8,128)(2,1)S(1)}, u32[]{:S(2)}, u32[]{:S(2)}) collective-permute-start(bf16[4,8,24,256]{3,2,1,0:T(8,128)(2,1)S(1)} %pad_maximum_fusion), channel_id=1, source_target_pairs={{0,16},{1,17},{2,18},{3,19},{4,20},{5,21},{6,22},{7,23},{8,24},{9,... | collective-permute-start | bytes 1179656 | tf_op jit(solution)/shard_map/ppermute | solution.py:137
  82.3 0.0 collective-permute-done.8.refs_7_
  82.3 0.0 copy-start.7
  82.3 6.2 %collective-permute-start.10 = (bf16[3,8,24,256]{3,2,1,0:T(8,128)(2,1)S(1)}, bf16[3,8,24,256]{3,2,1,0:T(8,128)(2,1)S(1)}, u32[]{:S(2)}, u32[]{:S(2)}) collective-permute-start(bf16[3,8,24,256]{3,2,1,0:T(8,128)(2,1)S(1)} %collective-permute-done.8.refs_7_), channel_id=1, source_target_pairs={{0,15},{1,0},{2,1},{3,2},{4,3},{5,4},{6,5},{7,6},{8,7},{9,8},{10,9... | collective-permute-start | bytes 884744 | tf_op jit(solution)/shard_map/ppermute | solution.py:134
  88.5 1.9 %collective-permute-start.9 = (bf16[3,8,24,256]{3,2,1,0:T(8,128)(2,1)S(1)}, bf16[3,8,24,256]{3,2,1,0:T(8,128)(2,1)S(1)}, u32[]{:S(2)}, u32[]{:S(2)}) collective-permute-start(bf16[3,8,24,256]{3,2,1,0:T(8,128)(2,1)S(1)} %collective-permute-done.8.refs_7_), channel_id=1, source_target_pairs={{0,1},{1,2},{2,3},{3,4},{4,5},{5,6},{6,7},{7,8},{8,9},{9,10},{10,1... | collective-permute-start | bytes 884744 | tf_op jit(solution)/shard_map/ppermute | solution.py:134
  90.5 0.0 collective-permute-done.5.refs_4_
  90.5 0.0 copy-start.8
  90.5 1.9 %collective-permute-start.11 = (bf16[3,8,24,256]{3,2,1,0:T(8,128)(2,1)S(1)}, bf16[3,8,24,256]{3,2,1,0:T(8,128)(2,1)S(1)}, u32[]{:S(2)}, u32[]{:S(2)}) collective-permute-start(bf16[3,8,24,256]{3,2,1,0:T(8,128)(2,1)S(1)} %collective-permute-done.5.refs_4_), channel_id=1, source_target_pairs={{0,16},{1,17},{2,18},{3,19},{4,20},{5,21},{6,22},{7,23},{8,24},{9,... | collective-permute-start | bytes 884744 | tf_op jit(solution)/shard_map/ppermute | solution.py:137
  92.4 0.0 copy-done.12
  92.4 0.0 copy-done.13
  92.5 0.6 pad_add_fusion.refs_0_
  93.1 1.6 %collective-permute-done.10.refs_9_ = bf16[3,8,24,256]{3,2,1,0:T(8,128)(2,1)S(1)} collective-permute-done((bf16[3,8,24,256]{3,2,1,0:T(8,128)(2,1)S(1)}, bf16[3,8,24,256]{3,2,1,0:T(8,128)(2,1)S(1)}, u32[]{:S(2)}, u32[]{:S(2)}) %collective-permute-start.10) | collective-permute-done | bytes 294944 | tf_op jit(solution)/shard_map/ppermute | solution.py:134
  94.7 0.0 copy-start.9
  94.7 5.3 %collective-permute-done.9.refs_8_ = bf16[3,8,24,256]{3,2,1,0:T(8,128)(2,1)S(1)} collective-permute-done((bf16[3,8,24,256]{3,2,1,0:T(8,128)(2,1)S(1)}, bf16[3,8,24,256]{3,2,1,0:T(8,128)(2,1)S(1)}, u32[]{:S(2)}, u32[]{:S(2)}) %collective-permute-start.9) | collective-permute-done | bytes 294944 | tf_op jit(solution)/shard_map/ppermute | solution.py:134
  100.0 0.0 copy-start.10
  100.0 0.7 collective-permute-done.11.refs_10_
  100.7 0.0 copy-start.11
  100.7 0.7 copy-done.11
  101.5 0.0 collective-permute-done.12.refs_11_
  101.5 0.0 copy-done.2
  101.5 0.0 copy-done.3
  101.5 0.0 copy-done.6
  101.5 0.0 copy-done.4
  101.5 0.0 copy-done.1
  101.5 0.0 copy-done.7
  101.5 0.0 copy-done.8
  101.5 0.0 copy-done.9
  101.5 0.0 copy-done.10
  101.5 0.0 copy-start.5
  101.5 0.7 copy-done.5
  102.3 6.0 %stack.1 = bf16[2,8,512,256]{3,2,1,0:T(8,128)(2,1)} custom-call(s32[33]{0:T(128)} %pad_add_fusion.refs_0_, bf16[3,8,24,256]{3,2,1,0:T(8,128)(2,1)} %copy-done.2, bf16[3,8,24,256]{3,2,1,0:T(8,128)(2,1)} %copy-done.6, bf16[3,8,24,256]{3,2,1,0:T(8,128)(2,1)} %copy-done.3, bf16[3,8,24,256]{3,2,1,0:T(8,128)(2,1)} %copy-done.8, bf16[3,8,24,256]{3,2,1,0:T(8,128)(2,1)} %copy-done.1, ...), custom_call_target="tpu_custom_call" | custom-call | tf_op jit(solution)/shard_map/stack/pallas_call | solution.py:112
  (4 shorter events, 0.1 us)
Async XLA Ops:
  2.3 9.4 %copy-start.14 = (bf16[8,24,256]{2,1,0:T(8,128)(2,1)S(1)}, bf16[8,24,256]{2,1,0:T(8,128)(2,1)}, u32[]{:S(2)}) copy-start(bf16[8,24,256]{2,1,0:T(8,128)(2,1)} %get-tuple-element.9) | copy-start | bytes 294916
  2.3 70.9 %all-to-all-start = ((bf16[16,8,24,256]{3,2,1,0:T(8,128)(2,1)}), bf16[16,8,24,256]{3,2,1,0:T(8,128)(2,1)S(1)}, u32[]{:S(2)}, u32[]{:S(2)}) async-start(bf16[16,8,24,256]{3,2,1,0:T(8,128)(2,1)} %get-tuple-element.10), calls=%async_computation | async-start | bytes 3145728 | tf_op jit(solution)/shard_map/all_to_all | solution.py:153
  11.6 22.8 %collective-permute-start.2 = (bf16[8,24,256]{2,1,0:T(8,128)(2,1)S(1)}, bf16[8,24,256]{2,1,0:T(8,128)(2,1)S(1)}, u32[]{:S(2)}, u32[]{:S(2)}) collective-permute-start(bf16[8,24,256]{2,1,0:T(8,128)(2,1)S(1)} %copy-done.14), channel_id=1, source_target_pairs={{0,11},{1,12},{2,43},{3,44},{4,75},{5,76},{6,107},{7,108},{8,139},... | collective-permute-start | bytes 294920 | tf_op jit(solution)/shard_map/ppermute | solution.py:146
  14.9 19.5 %collective-permute-start.1 = (bf16[8,24,256]{2,1,0:T(8,128)(2,1)S(1)}, bf16[8,24,256]{2,1,0:T(8,128)(2,1)S(1)}, u32[]{:S(2)}, u32[]{:S(2)}) collective-permute-start(bf16[8,24,256]{2,1,0:T(8,128)(2,1)S(1)} %copy-done.14), channel_id=1, source_target_pairs={{0,5},{1,6},{2,37},{3,38},{4,69},{5,70},{6,101},{7,102},{8,133},{9... | collective-permute-start | bytes 294920 | tf_op jit(solution)/shard_map/ppermute | solution.py:146
  27.9 18.6 %collective-permute-start = (bf16[8,24,256]{2,1,0:T(8,128)(2,1)S(1)}, bf16[8,24,256]{2,1,0:T(8,128)(2,1)S(1)}, u32[]{:S(2)}, u32[]{:S(2)}) collective-permute-start(bf16[8,24,256]{2,1,0:T(8,128)(2,1)S(1)} %copy-done.14), channel_id=1, source_target_pairs={{0,0},{1,1},{2,32},{3,33},{4,64},{5,65},{6,96},{7,97},{8,128},{9,1... | collective-permute-start | bytes 294920 | tf_op jit(solution)/shard_map/ppermute | solution.py:146
  46.5 46.0 %copy-start.12 = (s32[32]{0:T(128)S(1)}, s32[32]{0:T(128)}, u32[]{:S(2)}) copy-start(s32[32]{0:T(128)} %constant.60.clone) | copy-start | bytes 388
  46.5 46.0 %copy-start.13 = (pred[32]{0:T(512)(128)(4,1)S(1)}, pred[32]{0:T(512)(128)(4,1)}, u32[]{:S(2)}) copy-start(pred[32]{0:T(512)(128)(4,1)} %constant.59.clone) | copy-start | bytes 100
  46.5 55.0 %copy-start.2 = (bf16[3,8,24,256]{3,2,1,0:T(8,128)(2,1)}, bf16[3,8,24,256]{3,2,1,0:T(8,128)(2,1)S(1)}, u32[]{:S(2)}) copy-start(bf16[3,8,24,256]{3,2,1,0:T(8,128)(2,1)S(1)} %pad_maximum_fusion.1.refs_1_) | copy-start | bytes 884740
  46.5 13.8 %collective-permute-start.4 = (bf16[3,8,24,256]{3,2,1,0:T(8,128)(2,1)S(1)}, bf16[3,8,24,256]{3,2,1,0:T(8,128)(2,1)S(1)}, u32[]{:S(2)}, u32[]{:S(2)}) collective-permute-start(bf16[3,8,24,256]{3,2,1,0:T(8,128)(2,1)S(1)} %pad_maximum_fusion.1.refs_1_), channel_id=1, source_target_pairs={{0,15},{1,0},{2,1},{3,2},{4,3},{5,4},{6,5},{7,6},{8,7},{9,8},{10,9... | collective-permute-start | bytes 884744 | tf_op jit(solution)/shard_map/ppermute | solution.py:134
  53.0 14.8 %collective-permute-start.3 = (bf16[3,8,24,256]{3,2,1,0:T(8,128)(2,1)S(1)}, bf16[3,8,24,256]{3,2,1,0:T(8,128)(2,1)S(1)}, u32[]{:S(2)}, u32[]{:S(2)}) collective-permute-start(bf16[3,8,24,256]{3,2,1,0:T(8,128)(2,1)S(1)} %pad_maximum_fusion.1.refs_1_), channel_id=1, source_target_pairs={{0,1},{1,2},{2,3},{3,4},{4,5},{5,6},{6,7},{7,8},{8,9},{9,10},{10,1... | collective-permute-start | bytes 884744 | tf_op jit(solution)/shard_map/ppermute | solution.py:134
  60.3 41.2 %copy-start.3 = (bf16[3,8,24,256]{3,2,1,0:T(8,128)(2,1)}, bf16[3,8,24,256]{3,2,1,0:T(8,128)(2,1)S(1)}, u32[]{:S(2)}) copy-start(bf16[3,8,24,256]{3,2,1,0:T(8,128)(2,1)S(1)} %collective-permute-done.4.refs_3_) | copy-start | bytes 884740
  60.3 18.0 %collective-permute-start.6 = (bf16[3,8,24,256]{3,2,1,0:T(8,128)(2,1)S(1)}, bf16[3,8,24,256]{3,2,1,0:T(8,128)(2,1)S(1)}, u32[]{:S(2)}, u32[]{:S(2)}) collective-permute-start(bf16[3,8,24,256]{3,2,1,0:T(8,128)(2,1)S(1)} %collective-permute-done.4.refs_3_), channel_id=1, source_target_pairs={{0,15},{1,0},{2,1},{3,2},{4,3},{5,4},{6,5},{7,6},{8,7},{9,8},{10,9... | collective-permute-start | bytes 884744 | tf_op jit(solution)/shard_map/ppermute | solution.py:134
  65.9 16.4 %collective-permute-start.8 = (bf16[3,8,24,256]{3,2,1,0:T(8,128)(2,1)S(1)}, bf16[3,8,24,256]{3,2,1,0:T(8,128)(2,1)S(1)}, u32[]{:S(2)}, u32[]{:S(2)}) collective-permute-start(bf16[3,8,24,256]{3,2,1,0:T(8,128)(2,1)S(1)} %pad_maximum_fusion.1.refs_1_), channel_id=1, source_target_pairs={{0,16},{1,17},{2,18},{3,19},{4,20},{5,21},{6,22},{7,23},{8,24},{9,... | collective-permute-start | bytes 884744 | tf_op jit(solution)/shard_map/ppermute | solution.py:137
  67.8 33.6 %copy-start.6 = (bf16[3,8,24,256]{3,2,1,0:T(8,128)(2,1)}, bf16[3,8,24,256]{3,2,1,0:T(8,128)(2,1)S(1)}, u32[]{:S(2)}) copy-start(bf16[3,8,24,256]{3,2,1,0:T(8,128)(2,1)S(1)} %collective-permute-done.3.refs_2_) | copy-start | bytes 884740
  67.8 22.6 %collective-permute-start.5 = (bf16[3,8,24,256]{3,2,1,0:T(8,128)(2,1)S(1)}, bf16[3,8,24,256]{3,2,1,0:T(8,128)(2,1)S(1)}, u32[]{:S(2)}, u32[]{:S(2)}) collective-permute-start(bf16[3,8,24,256]{3,2,1,0:T(8,128)(2,1)S(1)} %collective-permute-done.3.refs_2_), channel_id=1, source_target_pairs={{0,1},{1,2},{2,3},{3,4},{4,5},{5,6},{6,7},{7,8},{8,9},{9,10},{10,1... | collective-permute-start | bytes 884744 | tf_op jit(solution)/shard_map/ppermute | solution.py:134
  69.8 8.5 %collective-permute-start.7 = (bf16[1,8,24,256]{3,2,1,0:T(8,128)(2,1)S(1)}, bf16[1,8,24,256]{3,2,1,0:T(8,128)(2,1)S(1)}, u32[]{:S(2)}, u32[]{:S(2)}) collective-permute-start(bf16[1,8,24,256]{3,2,1,0:T(8,128)(2,1)S(1)} %slice.4), channel_id=1, source_target_pairs={{0,14},{1,15},{2,0},{3,1},{4,2},{5,3},{6,4},{7,5},{8,6},{9,7},{10,... | collective-permute-start | bytes 294920 | tf_op jit(solution)/shard_map/ppermute | solution.py:134
  73.2 1.1 %copy-start = (bf16[16,8,24,256]{3,2,1,0:T(8,128)(2,1)}, bf16[16,8,24,256]{3,2,1,0:T(8,128)(2,1)S(1)}, u32[]{:S(2)}) copy-start(bf16[16,8,24,256]{3,2,1,0:T(8,128)(2,1)S(1)} %all-to-all-done.refs_0_) | copy-start | bytes 4718596
  78.3 23.2 %copy-start.4 = (bf16[1,8,24,256]{3,2,1,0:T(8,128)(2,1)}, bf16[1,8,24,256]{3,2,1,0:T(8,128)(2,1)S(1)}, u32[]{:S(2)}) copy-start(bf16[1,8,24,256]{3,2,1,0:T(8,128)(2,1)S(1)} %collective-permute-done.7.refs_6_) | copy-start | bytes 294916
  78.3 23.2 %copy-start.1 = (bf16[3,8,24,256]{3,2,1,0:T(8,128)(2,1)}, bf16[3,8,24,256]{3,2,1,0:T(8,128)(2,1)S(1)}, u32[]{:S(2)}) copy-start(bf16[3,8,24,256]{3,2,1,0:T(8,128)(2,1)S(1)} %collective-permute-done.6.refs_5_) | copy-start | bytes 884740
  78.3 23.1 %collective-permute-start.12 = (bf16[4,8,24,256]{3,2,1,0:T(8,128)(2,1)S(1)}, bf16[4,8,24,256]{3,2,1,0:T(8,128)(2,1)S(1)}, u32[]{:S(2)}, u32[]{:S(2)}) collective-permute-start(bf16[4,8,24,256]{3,2,1,0:T(8,128)(2,1)S(1)} %pad_maximum_fusion), channel_id=1, source_target_pairs={{0,16},{1,17},{2,18},{3,19},{4,20},{5,21},{6,22},{7,23},{8,24},{9,... | collective-permute-start | bytes 1179656 | tf_op jit(solution)/shard_map/ppermute | solution.py:137
  82.3 19.2 %copy-start.7 = (bf16[3,8,24,256]{3,2,1,0:T(8,128)(2,1)}, bf16[3,8,24,256]{3,2,1,0:T(8,128)(2,1)S(1)}, u32[]{:S(2)}) copy-start(bf16[3,8,24,256]{3,2,1,0:T(8,128)(2,1)S(1)} %collective-permute-done.8.refs_7_) | copy-start | bytes 884740
  82.3 12.4 %collective-permute-start.10 = (bf16[3,8,24,256]{3,2,1,0:T(8,128)(2,1)S(1)}, bf16[3,8,24,256]{3,2,1,0:T(8,128)(2,1)S(1)}, u32[]{:S(2)}, u32[]{:S(2)}) collective-permute-start(bf16[3,8,24,256]{3,2,1,0:T(8,128)(2,1)S(1)} %collective-permute-done.8.refs_7_), channel_id=1, source_target_pairs={{0,15},{1,0},{2,1},{3,2},{4,3},{5,4},{6,5},{7,6},{8,7},{9,8},{10,9... | collective-permute-start | bytes 884744 | tf_op jit(solution)/shard_map/ppermute | solution.py:134
  88.5 11.5 %collective-permute-start.9 = (bf16[3,8,24,256]{3,2,1,0:T(8,128)(2,1)S(1)}, bf16[3,8,24,256]{3,2,1,0:T(8,128)(2,1)S(1)}, u32[]{:S(2)}, u32[]{:S(2)}) collective-permute-start(bf16[3,8,24,256]{3,2,1,0:T(8,128)(2,1)S(1)} %collective-permute-done.8.refs_7_), channel_id=1, source_target_pairs={{0,1},{1,2},{2,3},{3,4},{4,5},{5,6},{6,7},{7,8},{8,9},{9,10},{10,1... | collective-permute-start | bytes 884744 | tf_op jit(solution)/shard_map/ppermute | solution.py:134
  90.5 11.0 %copy-start.8 = (bf16[3,8,24,256]{3,2,1,0:T(8,128)(2,1)}, bf16[3,8,24,256]{3,2,1,0:T(8,128)(2,1)S(1)}, u32[]{:S(2)}) copy-start(bf16[3,8,24,256]{3,2,1,0:T(8,128)(2,1)S(1)} %collective-permute-done.5.refs_4_) | copy-start | bytes 884740
  90.5 10.3 %collective-permute-start.11 = (bf16[3,8,24,256]{3,2,1,0:T(8,128)(2,1)S(1)}, bf16[3,8,24,256]{3,2,1,0:T(8,128)(2,1)S(1)}, u32[]{:S(2)}, u32[]{:S(2)}) collective-permute-start(bf16[3,8,24,256]{3,2,1,0:T(8,128)(2,1)S(1)} %collective-permute-done.5.refs_4_), channel_id=1, source_target_pairs={{0,16},{1,17},{2,18},{3,19},{4,20},{5,21},{6,22},{7,23},{8,24},{9,... | collective-permute-start | bytes 884744 | tf_op jit(solution)/shard_map/ppermute | solution.py:137
  94.7 6.8 %copy-start.9 = (bf16[3,8,24,256]{3,2,1,0:T(8,128)(2,1)}, bf16[3,8,24,256]{3,2,1,0:T(8,128)(2,1)S(1)}, u32[]{:S(2)}) copy-start(bf16[3,8,24,256]{3,2,1,0:T(8,128)(2,1)S(1)} %collective-permute-done.10.refs_9_) | copy-start | bytes 884740
  100.0 1.5 %copy-start.10 = (bf16[3,8,24,256]{3,2,1,0:T(8,128)(2,1)}, bf16[3,8,24,256]{3,2,1,0:T(8,128)(2,1)S(1)}, u32[]{:S(2)}) copy-start(bf16[3,8,24,256]{3,2,1,0:T(8,128)(2,1)S(1)} %collective-permute-done.9.refs_8_) | copy-start | bytes 884740
  100.7 0.7 copy-start.11
  101.5 0.8 copy-start.5

commit v4 on v3

--- a/solution.py
+++ b/solution.py
@@ -11,7 +11,7 @@
 STEP = 2
 
 OWN_SLOTS = ((0, -5, 5), (-1, -6, 4), (1, -4, 6), (-2, -7, 3), (2, -3, 7), (8,))
-NEIGHBOUR_SLOTS = ((0, -5, 5), (-1, -6, 4), (1, -4, 6), (-2, -7, 3), (2, -3, 7, 8))
+NEIGHBOUR_SLOTS = ((0, -5, 5), (-1, -6, 4), (1, -4, 6), (-2, -7, 3, 8), (2, -3, 7))
 
 
 def row_of(part, window, windows):
@@ -154,10 +154,10 @@
     first = jnp.concatenate(dealt, axis=0)
     up, down, other = shift(first, 1), shift(first, -1), trade(first)
     up2, down2, far = shift(up, 1), shift(down, -1), shift(down[2:], -2)
-    far, pairs = lax.optimization_barrier((far, receiver_pairs(receivers)))
+    up2, pairs = lax.optimization_barrier((up2, receiver_pairs(receivers)))
     other_up, other_down = shift(other, 1), shift(other, -1)
-    other_up2 = trade(up2)
-    last = trade(jnp.concatenate((down2, far), axis=0))
+    other_up2 = trade(jnp.concatenate((up2, far), axis=0))
+    last = trade(down2)
 
     groups = (first, up, down, up2, down2, far, other, other_up, other_down, other_up2, last)
     own = lax.axis_index("rcv") // length

time: 109 us -> 109 us (level)
  the two profiles are of different devices: /device:TPU:20 before, /device:TPU:72 now
where the time goes in v4:
time: 109 us; the launch traced here: 108 us
  starting transfers between devices  73.5 us (67%)
  waiting for transfers between devices  18.5 us (17%)
  Pallas kernels  12.3 us (11%)
  local copies, waits for them, and re-layouts  2.65 us (2%)
    ppermute x7, starting transfers between devices, shift(): lax.ppermute(block, 'rcv', [(r, along(r, step)) for r in range(cols_n)])  34.5 us
    ppermute x3, starting transfers between devices, deal(): return lax.ppermute(block, ('src', 'rcv'), pairs)  25 us
    ppermute x7, waiting for transfers between devices, shift(): lax.ppermute(block, 'rcv', [(r, along(r, step)) for r in range(cols_n)])  10.7 us
    ppermute x3, starting transfers between devices, trade(): lax.ppermute(block, 'rcv', [(r, (r + length) % cols_n) for r in range(col...  7.76 us
    all_to_all x1, starting transfers between devices, body(): receivers = (lax.all_to_all(copies, 'src', 0, 0),)  6.27 us
    pallas_call x1, Pallas kernels, stack(): pl.pallas_call(lambda *refs: stack_kernel(parities, scale, *refs), grid=(...  6.04 us
    ppermute x3, waiting for transfers between devices, trade(): lax.ppermute(block, 'rcv', [(r, (r + length) % cols_n) for r in range(col...  3.95 us
    pallas_call x1, Pallas kernels, receiver_pairs(): pl.pallas_call(receiver_kernel, grid=(bins // STEP,), in_specs=[pl.BlockS...  3.95 us
  transfers between devices with their start and end apart: 14, of which 5 were waited for; matrix products, arithmetic and copies ran while one was open for 1% of the time, Pallas kernels for 4%

profile of v4, /device:TPU:72, one launch (start us, length us, event | category | flops | bytes accessed | tf_op | source)
XLA Modules:
  0.0 107.9 jit_solution(13936181756927682501)
XLA Ops:
  0.0 2.3 %whiten.1 = (bf16[8,24,256]{2,1,0:T(8,128)(2,1)}, bf16[16,8,24,256]{3,2,1,0:T(8,128)(2,1)}) custom-call(bf16[2,12,8,256]{3,2,1,0:T(8,128)(2,1)} %bitcast.8, s32[12,256]{1,0:T(8,128)} %refs_1_.1), custom_call_target="tpu_custom_call" | custom-call | tf_op jit(solution)/shard_map/whiten/pallas_call | solution.py:42
  2.3 0.0 copy-start.14
  2.3 6.3 %all-to-all-start = ((bf16[16,8,24,256]{3,2,1,0:T(8,128)(2,1)}), bf16[16,8,24,256]{3,2,1,0:T(8,128)(2,1)S(1)}, u32[]{:S(2)}, u32[]{:S(2)}) async-start(bf16[16,8,24,256]{3,2,1,0:T(8,128)(2,1)} %get-tuple-element.10), calls=%async_computation | async-start | bytes 3145728 | tf_op jit(solution)/shard_map/all_to_all | solution.py:153
  8.5 0.0 copy-done.14
  8.6 15.4 %collective-permute-start.2 = (bf16[8,24,256]{2,1,0:T(8,128)(2,1)S(1)}, bf16[8,24,256]{2,1,0:T(8,128)(2,1)S(1)}, u32[]{:S(2)}, u32[]{:S(2)}) collective-permute-start(bf16[8,24,256]{2,1,0:T(8,128)(2,1)S(1)} %copy-done.14), channel_id=1, source_target_pairs={{0,11},{1,12},{2,43},{3,44},{4,75},{5,76},{6,107},{7,108},{8,139},... | collective-permute-start | bytes 294920 | tf_op jit(solution)/shard_map/ppermute | solution.py:146
  23.9 3.9 %collective-permute-start.1 = (bf16[8,24,256]{2,1,0:T(8,128)(2,1)S(1)}, bf16[8,24,256]{2,1,0:T(8,128)(2,1)S(1)}, u32[]{:S(2)}, u32[]{:S(2)}) collective-permute-start(bf16[8,24,256]{2,1,0:T(8,128)(2,1)S(1)} %copy-done.14), channel_id=1, source_target_pairs={{0,5},{1,6},{2,37},{3,38},{4,69},{5,70},{6,101},{7,102},{8,133},{9... | collective-permute-start | bytes 294920 | tf_op jit(solution)/shard_map/ppermute | solution.py:146
  27.9 5.7 %collective-permute-start = (bf16[8,24,256]{2,1,0:T(8,128)(2,1)S(1)}, bf16[8,24,256]{2,1,0:T(8,128)(2,1)S(1)}, u32[]{:S(2)}, u32[]{:S(2)}) collective-permute-start(bf16[8,24,256]{2,1,0:T(8,128)(2,1)S(1)} %copy-done.14), channel_id=1, source_target_pairs={{0,0},{1,1},{2,32},{3,33},{4,64},{5,65},{6,96},{7,97},{8,128},{9,1... | collective-permute-start | bytes 294920 | tf_op jit(solution)/shard_map/ppermute | solution.py:146
  33.6 0.0 collective-permute-done.2
  33.6 3.9 %collective-permute-done.1 = bf16[8,24,256]{2,1,0:T(8,128)(2,1)S(1)} collective-permute-done((bf16[8,24,256]{2,1,0:T(8,128)(2,1)S(1)}, bf16[8,24,256]{2,1,0:T(8,128)(2,1)S(1)}, u32[]{:S(2)}, u32[]{:S(2)}) %collective-permute-start.1) | collective-permute-done | bytes 98336 | tf_op jit(solution)/shard_map/ppermute | solution.py:146
  37.4 0.0 collective-permute-done
  37.4 0.0 copy-start.12
  37.4 0.0 copy-start.13
  37.5 0.0 copy-start.2
  37.5 9.8 %collective-permute-start.3 = (bf16[3,8,24,256]{3,2,1,0:T(8,128)(2,1)S(1)}, bf16[3,8,24,256]{3,2,1,0:T(8,128)(2,1)S(1)}, u32[]{:S(2)}, u32[]{:S(2)}) collective-permute-start(bf16[3,8,24,256]{3,2,1,0:T(8,128)(2,1)S(1)} %pad_maximum_fusion.1.refs_1_), channel_id=1, source_target_pairs={{0,1},{1,2},{2,3},{3,4},{4,5},{5,6},{6,7},{7,8},{8,9},{9,10},{10,1... | collective-permute-start | bytes 884744 | tf_op jit(solution)/shard_map/ppermute | solution.py:134
  47.4 1.9 %collective-permute-start.4 = (bf16[3,8,24,256]{3,2,1,0:T(8,128)(2,1)S(1)}, bf16[3,8,24,256]{3,2,1,0:T(8,128)(2,1)S(1)}, u32[]{:S(2)}, u32[]{:S(2)}) collective-permute-start(bf16[3,8,24,256]{3,2,1,0:T(8,128)(2,1)S(1)} %pad_maximum_fusion.1.refs_1_), channel_id=1, source_target_pairs={{0,15},{1,0},{2,1},{3,2},{4,3},{5,4},{6,5},{7,6},{8,7},{9,8},{10,9... | collective-permute-start | bytes 884744 | tf_op jit(solution)/shard_map/ppermute | solution.py:134
  49.3 2.4 %collective-permute-done.3.refs_2_ = bf16[3,8,24,256]{3,2,1,0:T(8,128)(2,1)S(1)} collective-permute-done((bf16[3,8,24,256]{3,2,1,0:T(8,128)(2,1)S(1)}, bf16[3,8,24,256]{3,2,1,0:T(8,128)(2,1)S(1)}, u32[]{:S(2)}, u32[]{:S(2)}) %collective-permute-start.3) | collective-permute-done | bytes 294944 | tf_op jit(solution)/shard_map/ppermute | solution.py:134
  51.7 0.0 copy-start.6
  51.7 10.2 %collective-permute-start.5 = (bf16[3,8,24,256]{3,2,1,0:T(8,128)(2,1)S(1)}, bf16[3,8,24,256]{3,2,1,0:T(8,128)(2,1)S(1)}, u32[]{:S(2)}, u32[]{:S(2)}) collective-permute-start(bf16[3,8,24,256]{3,2,1,0:T(8,128)(2,1)S(1)} %collective-permute-done.3.refs_2_), channel_id=1, source_target_pairs={{0,1},{1,2},{2,3},{3,4},{4,5},{5,6},{6,7},{7,8},{8,9},{9,10},{10,1... | collective-permute-start | bytes 884744 | tf_op jit(solution)/shard_map/ppermute | solution.py:134
  61.9 1.9 %collective-permute-start.8 = (bf16[3,8,24,256]{3,2,1,0:T(8,128)(2,1)S(1)}, bf16[3,8,24,256]{3,2,1,0:T(8,128)(2,1)S(1)}, u32[]{:S(2)}, u32[]{:S(2)}) collective-permute-start(bf16[3,8,24,256]{3,2,1,0:T(8,128)(2,1)S(1)} %pad_maximum_fusion.1.refs_1_), channel_id=1, source_target_pairs={{0,16},{1,17},{2,18},{3,19},{4,20},{5,21},{6,22},{7,23},{8,24},{9,... | collective-permute-start | bytes 884744 | tf_op jit(solution)/shard_map/ppermute | solution.py:137
  63.8 0.0 collective-permute-done.4.refs_3_
  63.8 0.0 copy-start.3
  63.8 1.9 %collective-permute-start.6 = (bf16[3,8,24,256]{3,2,1,0:T(8,128)(2,1)S(1)}, bf16[3,8,24,256]{3,2,1,0:T(8,128)(2,1)S(1)}, u32[]{:S(2)}, u32[]{:S(2)}) collective-permute-start(bf16[3,8,24,256]{3,2,1,0:T(8,128)(2,1)S(1)} %collective-permute-done.4.refs_3_), channel_id=1, source_target_pairs={{0,15},{1,0},{2,1},{3,2},{4,3},{5,4},{6,5},{7,6},{8,7},{9,8},{10,9... | collective-permute-start | bytes 884744 | tf_op jit(solution)/shard_map/ppermute | solution.py:134
  65.8 4.8 %collective-permute-start.7 = (bf16[1,8,24,256]{3,2,1,0:T(8,128)(2,1)S(1)}, bf16[1,8,24,256]{3,2,1,0:T(8,128)(2,1)S(1)}, u32[]{:S(2)}, u32[]{:S(2)}) collective-permute-start(bf16[1,8,24,256]{3,2,1,0:T(8,128)(2,1)S(1)} %slice.4), channel_id=1, source_target_pairs={{0,14},{1,15},{2,0},{3,1},{4,2},{5,3},{6,4},{7,5},{8,6},{9,7},{10,... | collective-permute-start | bytes 294920 | tf_op jit(solution)/shard_map/ppermute | solution.py:134
  70.5 0.0 all-to-all-done.refs_0_
  70.5 0.0 copy-start
  70.6 1.1 %copy-done = bf16[16,8,24,256]{3,2,1,0:T(8,128)(2,1)} copy-done((bf16[16,8,24,256]{3,2,1,0:T(8,128)(2,1)}, bf16[16,8,24,256]{3,2,1,0:T(8,128)(2,1)S(1)}, u32[]{:S(2)}) %copy-start) | copy-done | bytes 1572888
  71.7 4.0 %receiver_pairs.1.refs_12_ = bf16[8,16,24,512]{3,2,1,0:T(8,128)(2,1)} custom-call(bf16[16,8,24,256]{3,2,1,0:T(8,128)(2,1)} %copy-done), custom_call_target="tpu_custom_call" | custom-call | tf_op jit(solution)/shard_map/receiver_pairs/pallas_call | solution.py:73
  75.6 0.0 collective-permute-done.5.refs_4_
  75.6 0.0 copy-start.1
  75.6 6.4 %collective-permute-done.7.refs_6_ = bf16[1,8,24,256]{3,2,1,0:T(8,128)(2,1)S(1)} collective-permute-done((bf16[1,8,24,256]{3,2,1,0:T(8,128)(2,1)S(1)}, bf16[1,8,24,256]{3,2,1,0:T(8,128)(2,1)S(1)}, u32[]{:S(2)}, u32[]{:S(2)}) %collective-permute-start.7) | collective-permute-done | bytes 98336 | tf_op jit(solution)/shard_map/ppermute | solution.py:134
  82.1 0.0 copy-start.4
  82.1 3.6 %collective-permute-start.11 = (bf16[4,8,24,256]{3,2,1,0:T(8,128)(2,1)S(1)}, bf16[4,8,24,256]{3,2,1,0:T(8,128)(2,1)S(1)}, u32[]{:S(2)}, u32[]{:S(2)}) collective-permute-start(bf16[4,8,24,256]{3,2,1,0:T(8,128)(2,1)S(1)} %pad_maximum_fusion), channel_id=1, source_target_pairs={{0,16},{1,17},{2,18},{3,19},{4,20},{5,21},{6,22},{7,23},{8,24},{9,... | collective-permute-start | bytes 1179656 | tf_op jit(solution)/shard_map/ppermute | solution.py:137
  85.8 0.0 collective-permute-done.8.refs_7_
  85.8 0.0 copy-start.7
  85.8 1.9 %collective-permute-start.10 = (bf16[3,8,24,256]{3,2,1,0:T(8,128)(2,1)S(1)}, bf16[3,8,24,256]{3,2,1,0:T(8,128)(2,1)S(1)}, u32[]{:S(2)}, u32[]{:S(2)}) collective-permute-start(bf16[3,8,24,256]{3,2,1,0:T(8,128)(2,1)S(1)} %collective-permute-done.8.refs_7_), channel_id=1, source_target_pairs={{0,15},{1,0},{2,1},{3,2},{4,3},{5,4},{6,5},{7,6},{8,7},{9,8},{10,9... | collective-permute-start | bytes 884744 | tf_op jit(solution)/shard_map/ppermute | solution.py:134
  87.8 3.9 %collective-permute-start.9 = (bf16[3,8,24,256]{3,2,1,0:T(8,128)(2,1)S(1)}, bf16[3,8,24,256]{3,2,1,0:T(8,128)(2,1)S(1)}, u32[]{:S(2)}, u32[]{:S(2)}) collective-permute-start(bf16[3,8,24,256]{3,2,1,0:T(8,128)(2,1)S(1)} %collective-permute-done.8.refs_7_), channel_id=1, source_target_pairs={{0,1},{1,2},{2,3},{3,4},{4,5},{5,6},{6,7},{7,8},{8,9},{9,10},{10,1... | collective-permute-start | bytes 884744 | tf_op jit(solution)/shard_map/ppermute | solution.py:134
  91.7 0.0 collective-permute-done.6.refs_5_
  91.7 0.0 copy-start.8
  91.7 2.2 %collective-permute-start.12 = (bf16[3,8,24,256]{3,2,1,0:T(8,128)(2,1)S(1)}, bf16[3,8,24,256]{3,2,1,0:T(8,128)(2,1)S(1)}, u32[]{:S(2)}, u32[]{:S(2)}) collective-permute-start(bf16[3,8,24,256]{3,2,1,0:T(8,128)(2,1)S(1)} %collective-permute-done.6.refs_5_), channel_id=1, source_target_pairs={{0,16},{1,17},{2,18},{3,19},{4,20},{5,21},{6,22},{7,23},{8,24},{9,... | collective-permute-start | bytes 884744 | tf_op jit(solution)/shard_map/ppermute | solution.py:137
  93.9 0.0 copy-done.12
  93.9 0.0 copy-done.13
  94.0 0.6 pad_add_fusion.refs_0_
  94.6 0.0 collective-permute-done.10.refs_9_
  94.6 0.0 copy-start.9
  94.6 1.8 %collective-permute-done.9.refs_8_ = bf16[3,8,24,256]{3,2,1,0:T(8,128)(2,1)S(1)} collective-permute-done((bf16[3,8,24,256]{3,2,1,0:T(8,128)(2,1)S(1)}, bf16[3,8,24,256]{3,2,1,0:T(8,128)(2,1)S(1)}, u32[]{:S(2)}, u32[]{:S(2)}) %collective-permute-start.9) | collective-permute-done | bytes 294944 | tf_op jit(solution)/shard_map/ppermute | solution.py:134
  96.4 0.0 copy-start.10
  96.4 3.9 %collective-permute-done.12.refs_11_ = bf16[3,8,24,256]{3,2,1,0:T(8,128)(2,1)S(1)} collective-permute-done((bf16[3,8,24,256]{3,2,1,0:T(8,128)(2,1)S(1)}, bf16[3,8,24,256]{3,2,1,0:T(8,128)(2,1)S(1)}, u32[]{:S(2)}, u32[]{:S(2)}) %collective-permute-start.12) | collective-permute-done | bytes 294944 | tf_op jit(solution)/shard_map/ppermute | solution.py:137
  100.3 0.0 copy-start.11
  100.3 0.7 copy-done.11
  101.0 0.0 collective-permute-done.11.refs_10_
  101.0 0.0 copy-done.2
  101.0 0.0 copy-done.6
  101.0 0.0 copy-done.3
  101.1 0.0 copy-done.1
  101.1 0.0 copy-done.4
  101.1 0.0 copy-done.7
  101.1 0.0 copy-done.8
  101.1 0.0 copy-done.9
  101.1 0.0 copy-done.10
  101.1 0.0 copy-start.5
  101.1 0.7 copy-done.5
  101.9 6.0 %stack.1 = bf16[2,8,512,256]{3,2,1,0:T(8,128)(2,1)} custom-call(s32[33]{0:T(128)} %pad_add_fusion.refs_0_, bf16[3,8,24,256]{3,2,1,0:T(8,128)(2,1)} %copy-done.2, bf16[3,8,24,256]{3,2,1,0:T(8,128)(2,1)} %copy-done.6, bf16[3,8,24,256]{3,2,1,0:T(8,128)(2,1)} %copy-done.3, bf16[3,8,24,256]{3,2,1,0:T(8,128)(2,1)} %copy-done.1, bf16[3,8,24,256]{3,2,1,0:T(8,128)(2,1)} %copy-done.8, ...), custom_call_target="tpu_custom_call" | custom-call | tf_op jit(solution)/shard_map/stack/pallas_call | solution.py:112
  (4 shorter events, 0.1 us)
Async XLA Ops:
  2.3 6.3 %copy-start.14 = (bf16[8,24,256]{2,1,0:T(8,128)(2,1)S(1)}, bf16[8,24,256]{2,1,0:T(8,128)(2,1)}, u32[]{:S(2)}) copy-start(bf16[8,24,256]{2,1,0:T(8,128)(2,1)} %get-tuple-element.9) | copy-start | bytes 294916
  2.3 68.3 %all-to-all-start = ((bf16[16,8,24,256]{3,2,1,0:T(8,128)(2,1)}), bf16[16,8,24,256]{3,2,1,0:T(8,128)(2,1)S(1)}, u32[]{:S(2)}, u32[]{:S(2)}) async-start(bf16[16,8,24,256]{3,2,1,0:T(8,128)(2,1)} %get-tuple-element.10), calls=%async_computation | async-start | bytes 3145728 | tf_op jit(solution)/shard_map/all_to_all | solution.py:153
  8.6 25.0 %collective-permute-start.2 = (bf16[8,24,256]{2,1,0:T(8,128)(2,1)S(1)}, bf16[8,24,256]{2,1,0:T(8,128)(2,1)S(1)}, u32[]{:S(2)}, u32[]{:S(2)}) collective-permute-start(bf16[8,24,256]{2,1,0:T(8,128)(2,1)S(1)} %copy-done.14), channel_id=1, source_target_pairs={{0,11},{1,12},{2,43},{3,44},{4,75},{5,76},{6,107},{7,108},{8,139},... | collective-permute-start | bytes 294920 | tf_op jit(solution)/shard_map/ppermute | solution.py:146
  23.9 13.5 %collective-permute-start.1 = (bf16[8,24,256]{2,1,0:T(8,128)(2,1)S(1)}, bf16[8,24,256]{2,1,0:T(8,128)(2,1)S(1)}, u32[]{:S(2)}, u32[]{:S(2)}) collective-permute-start(bf16[8,24,256]{2,1,0:T(8,128)(2,1)S(1)} %copy-done.14), channel_id=1, source_target_pairs={{0,5},{1,6},{2,37},{3,38},{4,69},{5,70},{6,101},{7,102},{8,133},{9... | collective-permute-start | bytes 294920 | tf_op jit(solution)/shard_map/ppermute | solution.py:146
  27.9 9.6 %collective-permute-start = (bf16[8,24,256]{2,1,0:T(8,128)(2,1)S(1)}, bf16[8,24,256]{2,1,0:T(8,128)(2,1)S(1)}, u32[]{:S(2)}, u32[]{:S(2)}) collective-permute-start(bf16[8,24,256]{2,1,0:T(8,128)(2,1)S(1)} %copy-done.14), channel_id=1, source_target_pairs={{0,0},{1,1},{2,32},{3,33},{4,64},{5,65},{6,96},{7,97},{8,128},{9,1... | collective-permute-start | bytes 294920 | tf_op jit(solution)/shard_map/ppermute | solution.py:146
  37.4 56.5 %copy-start.12 = (s32[32]{0:T(128)S(1)}, s32[32]{0:T(128)}, u32[]{:S(2)}) copy-start(s32[32]{0:T(128)} %constant.60.clone) | copy-start | bytes 388
  37.4 56.5 %copy-start.13 = (pred[32]{0:T(512)(128)(4,1)S(1)}, pred[32]{0:T(512)(128)(4,1)}, u32[]{:S(2)}) copy-start(pred[32]{0:T(512)(128)(4,1)} %constant.59.clone) | copy-start | bytes 100
  37.5 63.6 %copy-start.2 = (bf16[3,8,24,256]{3,2,1,0:T(8,128)(2,1)}, bf16[3,8,24,256]{3,2,1,0:T(8,128)(2,1)S(1)}, u32[]{:S(2)}) copy-start(bf16[3,8,24,256]{3,2,1,0:T(8,128)(2,1)S(1)} %pad_maximum_fusion.1.refs_1_) | copy-start | bytes 884740
  37.5 14.2 %collective-permute-start.3 = (bf16[3,8,24,256]{3,2,1,0:T(8,128)(2,1)S(1)}, bf16[3,8,24,256]{3,2,1,0:T(8,128)(2,1)S(1)}, u32[]{:S(2)}, u32[]{:S(2)}) collective-permute-start(bf16[3,8,24,256]{3,2,1,0:T(8,128)(2,1)S(1)} %pad_maximum_fusion.1.refs_1_), channel_id=1, source_target_pairs={{0,1},{1,2},{2,3},{3,4},{4,5},{5,6},{6,7},{7,8},{8,9},{9,10},{10,1... | collective-permute-start | bytes 884744 | tf_op jit(solution)/shard_map/ppermute | solution.py:134
  47.4 16.4 %collective-permute-start.4 = (bf16[3,8,24,256]{3,2,1,0:T(8,128)(2,1)S(1)}, bf16[3,8,24,256]{3,2,1,0:T(8,128)(2,1)S(1)}, u32[]{:S(2)}, u32[]{:S(2)}) collective-permute-start(bf16[3,8,24,256]{3,2,1,0:T(8,128)(2,1)S(1)} %pad_maximum_fusion.1.refs_1_), channel_id=1, source_target_pairs={{0,15},{1,0},{2,1},{3,2},{4,3},{5,4},{6,5},{7,6},{8,7},{9,8},{10,9... | collective-permute-start | bytes 884744 | tf_op jit(solution)/shard_map/ppermute | solution.py:134
  51.7 49.4 %copy-start.6 = (bf16[3,8,24,256]{3,2,1,0:T(8,128)(2,1)}, bf16[3,8,24,256]{3,2,1,0:T(8,128)(2,1)S(1)}, u32[]{:S(2)}) copy-start(bf16[3,8,24,256]{3,2,1,0:T(8,128)(2,1)S(1)} %collective-permute-done.3.refs_2_) | copy-start | bytes 884740
  51.7 23.9 %collective-permute-start.5 = (bf16[3,8,24,256]{3,2,1,0:T(8,128)(2,1)S(1)}, bf16[3,8,24,256]{3,2,1,0:T(8,128)(2,1)S(1)}, u32[]{:S(2)}, u32[]{:S(2)}) collective-permute-start(bf16[3,8,24,256]{3,2,1,0:T(8,128)(2,1)S(1)} %collective-permute-done.3.refs_2_), channel_id=1, source_target_pairs={{0,1},{1,2},{2,3},{3,4},{4,5},{5,6},{6,7},{7,8},{8,9},{9,10},{10,1... | collective-permute-start | bytes 884744 | tf_op jit(solution)/shard_map/ppermute | solution.py:134
  61.9 23.9 %collective-permute-start.8 = (bf16[3,8,24,256]{3,2,1,0:T(8,128)(2,1)S(1)}, bf16[3,8,24,256]{3,2,1,0:T(8,128)(2,1)S(1)}, u32[]{:S(2)}, u32[]{:S(2)}) collective-permute-start(bf16[3,8,24,256]{3,2,1,0:T(8,128)(2,1)S(1)} %pad_maximum_fusion.1.refs_1_), channel_id=1, source_target_pairs={{0,16},{1,17},{2,18},{3,19},{4,20},{5,21},{6,22},{7,23},{8,24},{9,... | collective-permute-start | bytes 884744 | tf_op jit(solution)/shard_map/ppermute | solution.py:137
  63.8 37.2 %copy-start.3 = (bf16[3,8,24,256]{3,2,1,0:T(8,128)(2,1)}, bf16[3,8,24,256]{3,2,1,0:T(8,128)(2,1)S(1)}, u32[]{:S(2)}) copy-start(bf16[3,8,24,256]{3,2,1,0:T(8,128)(2,1)S(1)} %collective-permute-done.4.refs_3_) | copy-start | bytes 884740
  63.8 27.9 %collective-permute-start.6 = (bf16[3,8,24,256]{3,2,1,0:T(8,128)(2,1)S(1)}, bf16[3,8,24,256]{3,2,1,0:T(8,128)(2,1)S(1)}, u32[]{:S(2)}, u32[]{:S(2)}) collective-permute-start(bf16[3,8,24,256]{3,2,1,0:T(8,128)(2,1)S(1)} %collective-permute-done.4.refs_3_), channel_id=1, source_target_pairs={{0,15},{1,0},{2,1},{3,2},{4,3},{5,4},{6,5},{7,6},{8,7},{9,8},{10,9... | collective-permute-start | bytes 884744 | tf_op jit(solution)/shard_map/ppermute | solution.py:134
  65.8 16.3 %collective-permute-start.7 = (bf16[1,8,24,256]{3,2,1,0:T(8,128)(2,1)S(1)}, bf16[1,8,24,256]{3,2,1,0:T(8,128)(2,1)S(1)}, u32[]{:S(2)}, u32[]{:S(2)}) collective-permute-start(bf16[1,8,24,256]{3,2,1,0:T(8,128)(2,1)S(1)} %slice.4), channel_id=1, source_target_pairs={{0,14},{1,15},{2,0},{3,1},{4,2},{5,3},{6,4},{7,5},{8,6},{9,7},{10,... | collective-permute-start | bytes 294920 | tf_op jit(solution)/shard_map/ppermute | solution.py:134
  70.5 1.1 %copy-start = (bf16[16,8,24,256]{3,2,1,0:T(8,128)(2,1)}, bf16[16,8,24,256]{3,2,1,0:T(8,128)(2,1)S(1)}, u32[]{:S(2)}) copy-start(bf16[16,8,24,256]{3,2,1,0:T(8,128)(2,1)S(1)} %all-to-all-done.refs_0_) | copy-start | bytes 4718596
  75.6 25.4 %copy-start.1 = (bf16[3,8,24,256]{3,2,1,0:T(8,128)(2,1)}, bf16[3,8,24,256]{3,2,1,0:T(8,128)(2,1)S(1)}, u32[]{:S(2)}) copy-start(bf16[3,8,24,256]{3,2,1,0:T(8,128)(2,1)S(1)} %collective-permute-done.5.refs_4_) | copy-start | bytes 884740
  82.1 19.0 %copy-start.4 = (bf16[1,8,24,256]{3,2,1,0:T(8,128)(2,1)}, bf16[1,8,24,256]{3,2,1,0:T(8,128)(2,1)S(1)}, u32[]{:S(2)}) copy-start(bf16[1,8,24,256]{3,2,1,0:T(8,128)(2,1)S(1)} %collective-permute-done.7.refs_6_) | copy-start | bytes 294916
  82.1 18.9 %collective-permute-start.11 = (bf16[4,8,24,256]{3,2,1,0:T(8,128)(2,1)S(1)}, bf16[4,8,24,256]{3,2,1,0:T(8,128)(2,1)S(1)}, u32[]{:S(2)}, u32[]{:S(2)}) collective-permute-start(bf16[4,8,24,256]{3,2,1,0:T(8,128)(2,1)S(1)} %pad_maximum_fusion), channel_id=1, source_target_pairs={{0,16},{1,17},{2,18},{3,19},{4,20},{5,21},{6,22},{7,23},{8,24},{9,... | collective-permute-start | bytes 1179656 | tf_op jit(solution)/shard_map/ppermute | solution.py:137
  85.8 15.3 %copy-start.7 = (bf16[3,8,24,256]{3,2,1,0:T(8,128)(2,1)}, bf16[3,8,24,256]{3,2,1,0:T(8,128)(2,1)S(1)}, u32[]{:S(2)}) copy-start(bf16[3,8,24,256]{3,2,1,0:T(8,128)(2,1)S(1)} %collective-permute-done.8.refs_7_) | copy-start | bytes 884740
  85.8 8.7 %collective-permute-start.10 = (bf16[3,8,24,256]{3,2,1,0:T(8,128)(2,1)S(1)}, bf16[3,8,24,256]{3,2,1,0:T(8,128)(2,1)S(1)}, u32[]{:S(2)}, u32[]{:S(2)}) collective-permute-start(bf16[3,8,24,256]{3,2,1,0:T(8,128)(2,1)S(1)} %collective-permute-done.8.refs_7_), channel_id=1, source_target_pairs={{0,15},{1,0},{2,1},{3,2},{4,3},{5,4},{6,5},{7,6},{8,7},{9,8},{10,9... | collective-permute-start | bytes 884744 | tf_op jit(solution)/shard_map/ppermute | solution.py:134
  87.8 8.6 %collective-permute-start.9 = (bf16[3,8,24,256]{3,2,1,0:T(8,128)(2,1)S(1)}, bf16[3,8,24,256]{3,2,1,0:T(8,128)(2,1)S(1)}, u32[]{:S(2)}, u32[]{:S(2)}) collective-permute-start(bf16[3,8,24,256]{3,2,1,0:T(8,128)(2,1)S(1)} %collective-permute-done.8.refs_7_), channel_id=1, source_target_pairs={{0,1},{1,2},{2,3},{3,4},{4,5},{5,6},{6,7},{7,8},{8,9},{9,10},{10,1... | collective-permute-start | bytes 884744 | tf_op jit(solution)/shard_map/ppermute | solution.py:134
  91.7 9.4 %copy-start.8 = (bf16[3,8,24,256]{3,2,1,0:T(8,128)(2,1)}, bf16[3,8,24,256]{3,2,1,0:T(8,128)(2,1)S(1)}, u32[]{:S(2)}) copy-start(bf16[3,8,24,256]{3,2,1,0:T(8,128)(2,1)S(1)} %collective-permute-done.6.refs_5_) | copy-start | bytes 884740
  91.7 8.6 %collective-permute-start.12 = (bf16[3,8,24,256]{3,2,1,0:T(8,128)(2,1)S(1)}, bf16[3,8,24,256]{3,2,1,0:T(8,128)(2,1)S(1)}, u32[]{:S(2)}, u32[]{:S(2)}) collective-permute-start(bf16[3,8,24,256]{3,2,1,0:T(8,128)(2,1)S(1)} %collective-permute-done.6.refs_5_), channel_id=1, source_target_pairs={{0,16},{1,17},{2,18},{3,19},{4,20},{5,21},{6,22},{7,23},{8,24},{9,... | collective-permute-start | bytes 884744 | tf_op jit(solution)/shard_map/ppermute | solution.py:137
  94.6 6.5 %copy-start.9 = (bf16[3,8,24,256]{3,2,1,0:T(8,128)(2,1)}, bf16[3,8,24,256]{3,2,1,0:T(8,128)(2,1)S(1)}, u32[]{:S(2)}) copy-start(bf16[3,8,24,256]{3,2,1,0:T(8,128)(2,1)S(1)} %collective-permute-done.10.refs_9_) | copy-start | bytes 884740
  96.4 4.7 %copy-start.10 = (bf16[3,8,24,256]{3,2,1,0:T(8,128)(2,1)}, bf16[3,8,24,256]{3,2,1,0:T(8,128)(2,1)S(1)}, u32[]{:S(2)}) copy-start(bf16[3,8,24,256]{3,2,1,0:T(8,128)(2,1)S(1)} %collective-permute-done.9.refs_8_) | copy-start | bytes 884740
  100.3 0.7 copy-start.11
  101.1 0.8 copy-start.5

commit v5 on v4

--- a/solution.py
+++ b/solution.py
@@ -153,7 +153,7 @@
     receivers = (lax.all_to_all(copies, "src", 0, 0),)
     first = jnp.concatenate(dealt, axis=0)
     up, down, other = shift(first, 1), shift(first, -1), trade(first)
-    up2, down2, far = shift(up, 1), shift(down, -1), shift(down[2:], -2)
+    up2, down2, far = shift(up, 1), shift(down, -1), shift(up[1:2], 2)
     up2, pairs = lax.optimization_barrier((up2, receiver_pairs(receivers)))
     other_up, other_down = shift(other, 1), shift(other, -1)
     other_up2 = trade(jnp.concatenate((up2, far), axis=0))

time: 109 us -> 108 us (level)
  the two profiles are of different devices: /device:TPU:72 before, /device:TPU:18 now
where the time goes in v5:
time: 108 us
  starting transfers between devices  61.3 us (57%)
  waiting for transfers between devices  30.4 us (28%)
  Pallas kernels  12.3 us (11%)
  local copies, waits for them, and re-layouts  2.65 us (2%)
    ppermute x3, starting transfers between devices, deal(): return lax.ppermute(block, ('src', 'rcv'), pairs)  22.4 us
    ppermute x7, starting transfers between devices, shift(): lax.ppermute(block, 'rcv', [(r, along(r, step)) for r in range(cols_n)])  21.9 us
    ppermute x3, waiting for transfers between devices, deal(): return lax.ppermute(block, ('src', 'rcv'), pairs)  20 us
    all_to_all x1, starting transfers between devices, body(): receivers = (lax.all_to_all(copies, 'src', 0, 0),)  9.37 us
    ppermute x3, starting transfers between devices, trade(): lax.ppermute(block, 'rcv', [(r, (r + length) % cols_n) for r in range(col...  7.76 us
    ppermute x7, waiting for transfers between devices, shift(): lax.ppermute(block, 'rcv', [(r, along(r, step)) for r in range(cols_n)])  7.65 us
    pallas_call x1, Pallas kernels, stack(): pl.pallas_call(lambda *refs: stack_kernel(parities, scale, *refs), grid=(...  6.04 us
    pallas_call x1, Pallas kernels, receiver_pairs(): pl.pallas_call(receiver_kernel, grid=(bins // STEP,), in_specs=[pl.BlockS...  3.95 us
  transfers between devices with their start and end apart: 14, of which 7 were waited for; matrix products, arithmetic and copies ran while one was open for 1% of the time, Pallas kernels for 4%

profile of v5, /device:TPU:18, one launch (start us, length us, event | category | flops | bytes accessed | tf_op | source)
XLA Modules:
  0.0 107.7 jit_solution(6997122991335372521)
XLA Ops:
  0.0 2.3 %whiten.1 = (bf16[8,24,256]{2,1,0:T(8,128)(2,1)}, bf16[16,8,24,256]{3,2,1,0:T(8,128)(2,1)}) custom-call(bf16[2,12,8,256]{3,2,1,0:T(8,128)(2,1)} %bitcast.8, s32[12,256]{1,0:T(8,128)} %refs_1_.1), custom_call_target="tpu_custom_call" | custom-call | tf_op jit(solution)/shard_map/whiten/pallas_call | solution.py:42
  2.3 0.0 copy-start.14
  2.3 9.4 %all-to-all-start = ((bf16[16,8,24,256]{3,2,1,0:T(8,128)(2,1)}), bf16[16,8,24,256]{3,2,1,0:T(8,128)(2,1)S(1)}, u32[]{:S(2)}, u32[]{:S(2)}) async-start(bf16[16,8,24,256]{3,2,1,0:T(8,128)(2,1)} %get-tuple-element.10), calls=%async_computation | async-start | bytes 3145728 | tf_op jit(solution)/shard_map/all_to_all | solution.py:153
  11.6 0.0 copy-done.14
  11.6 8.2 %collective-permute-start.2 = (bf16[8,24,256]{2,1,0:T(8,128)(2,1)S(1)}, bf16[8,24,256]{2,1,0:T(8,128)(2,1)S(1)}, u32[]{:S(2)}, u32[]{:S(2)}) collective-permute-start(bf16[8,24,256]{2,1,0:T(8,128)(2,1)S(1)} %copy-done.14), channel_id=1, source_target_pairs={{0,11},{1,12},{2,43},{3,44},{4,75},{5,76},{6,107},{7,108},{8,139},... | collective-permute-start | bytes 294920 | tf_op jit(solution)/shard_map/ppermute | solution.py:146
  19.8 12.3 %collective-permute-start.1 = (bf16[8,24,256]{2,1,0:T(8,128)(2,1)S(1)}, bf16[8,24,256]{2,1,0:T(8,128)(2,1)S(1)}, u32[]{:S(2)}, u32[]{:S(2)}) collective-permute-start(bf16[8,24,256]{2,1,0:T(8,128)(2,1)S(1)} %copy-done.14), channel_id=1, source_target_pairs={{0,5},{1,6},{2,37},{3,38},{4,69},{5,70},{6,101},{7,102},{8,133},{9... | collective-permute-start | bytes 294920 | tf_op jit(solution)/shard_map/ppermute | solution.py:146
  32.1 1.9 %collective-permute-start = (bf16[8,24,256]{2,1,0:T(8,128)(2,1)S(1)}, bf16[8,24,256]{2,1,0:T(8,128)(2,1)S(1)}, u32[]{:S(2)}, u32[]{:S(2)}) collective-permute-start(bf16[8,24,256]{2,1,0:T(8,128)(2,1)S(1)} %copy-done.14), channel_id=1, source_target_pairs={{0,0},{1,1},{2,32},{3,33},{4,64},{5,65},{6,96},{7,97},{8,128},{9,1... | collective-permute-start | bytes 294920 | tf_op jit(solution)/shard_map/ppermute | solution.py:146
  34.0 0.0 collective-permute-done.2
  34.0 2.8 %collective-permute-done.1 = bf16[8,24,256]{2,1,0:T(8,128)(2,1)S(1)} collective-permute-done((bf16[8,24,256]{2,1,0:T(8,128)(2,1)S(1)}, bf16[8,24,256]{2,1,0:T(8,128)(2,1)S(1)}, u32[]{:S(2)}, u32[]{:S(2)}) %collective-permute-start.1) | collective-permute-done | bytes 98336 | tf_op jit(solution)/shard_map/ppermute | solution.py:146
  36.9 17.1 %collective-permute-done = bf16[8,24,256]{2,1,0:T(8,128)(2,1)S(1)} collective-permute-done((bf16[8,24,256]{2,1,0:T(8,128)(2,1)S(1)}, bf16[8,24,256]{2,1,0:T(8,128)(2,1)S(1)}, u32[]{:S(2)}, u32[]{:S(2)}) %collective-permute-start) | collective-permute-done | bytes 98336 | tf_op jit(solution)/shard_map/ppermute | solution.py:146
  54.0 0.0 copy-start.12
  54.0 0.0 copy-start.13
  54.1 0.0 copy-start.2
  54.1 1.9 %collective-permute-start.3 = (bf16[3,8,24,256]{3,2,1,0:T(8,128)(2,1)S(1)}, bf16[3,8,24,256]{3,2,1,0:T(8,128)(2,1)S(1)}, u32[]{:S(2)}, u32[]{:S(2)}) collective-permute-start(bf16[3,8,24,256]{3,2,1,0:T(8,128)(2,1)S(1)} %pad_maximum_fusion.1.refs_1_), channel_id=1, source_target_pairs={{0,1},{1,2},{2,3},{3,4},{4,5},{5,6},{6,7},{7,8},{8,9},{9,10},{10,1... | collective-permute-start | bytes 884744 | tf_op jit(solution)/shard_map/ppermute | solution.py:134
  56.0 5.1 %collective-permute-start.4 = (bf16[3,8,24,256]{3,2,1,0:T(8,128)(2,1)S(1)}, bf16[3,8,24,256]{3,2,1,0:T(8,128)(2,1)S(1)}, u32[]{:S(2)}, u32[]{:S(2)}) collective-permute-start(bf16[3,8,24,256]{3,2,1,0:T(8,128)(2,1)S(1)} %pad_maximum_fusion.1.refs_1_), channel_id=1, source_target_pairs={{0,15},{1,0},{2,1},{3,2},{4,3},{5,4},{6,5},{7,6},{8,7},{9,8},{10,9... | collective-permute-start | bytes 884744 | tf_op jit(solution)/shard_map/ppermute | solution.py:134
  61.1 2.8 %collective-permute-done.3.refs_2_ = bf16[3,8,24,256]{3,2,1,0:T(8,128)(2,1)S(1)} collective-permute-done((bf16[3,8,24,256]{3,2,1,0:T(8,128)(2,1)S(1)}, bf16[3,8,24,256]{3,2,1,0:T(8,128)(2,1)S(1)}, u32[]{:S(2)}, u32[]{:S(2)}) %collective-permute-start.3) | collective-permute-done | bytes 294944 | tf_op jit(solution)/shard_map/ppermute | solution.py:134
  63.9 0.0 copy-start.3
  63.9 1.9 %collective-permute-start.5 = (bf16[3,8,24,256]{3,2,1,0:T(8,128)(2,1)S(1)}, bf16[3,8,24,256]{3,2,1,0:T(8,128)(2,1)S(1)}, u32[]{:S(2)}, u32[]{:S(2)}) collective-permute-start(bf16[3,8,24,256]{3,2,1,0:T(8,128)(2,1)S(1)} %collective-permute-done.3.refs_2_), channel_id=1, source_target_pairs={{0,1},{1,2},{2,3},{3,4},{4,5},{5,6},{6,7},{7,8},{8,9},{9,10},{10,1... | collective-permute-start | bytes 884744 | tf_op jit(solution)/shard_map/ppermute | solution.py:134
  65.8 1.9 %collective-permute-start.8 = (bf16[3,8,24,256]{3,2,1,0:T(8,128)(2,1)S(1)}, bf16[3,8,24,256]{3,2,1,0:T(8,128)(2,1)S(1)}, u32[]{:S(2)}, u32[]{:S(2)}) collective-permute-start(bf16[3,8,24,256]{3,2,1,0:T(8,128)(2,1)S(1)} %pad_maximum_fusion.1.refs_1_), channel_id=1, source_target_pairs={{0,16},{1,17},{2,18},{3,19},{4,20},{5,21},{6,22},{7,23},{8,24},{9,... | collective-permute-start | bytes 884744 | tf_op jit(solution)/shard_map/ppermute | solution.py:137
  67.7 0.0 collective-permute-done.4.refs_3_
  67.8 0.0 copy-start.6
  67.8 5.1 %collective-permute-start.6 = (bf16[3,8,24,256]{3,2,1,0:T(8,128)(2,1)S(1)}, bf16[3,8,24,256]{3,2,1,0:T(8,128)(2,1)S(1)}, u32[]{:S(2)}, u32[]{:S(2)}) collective-permute-start(bf16[3,8,24,256]{3,2,1,0:T(8,128)(2,1)S(1)} %collective-permute-done.4.refs_3_), channel_id=1, source_target_pairs={{0,15},{1,0},{2,1},{3,2},{4,3},{5,4},{6,5},{7,6},{8,7},{9,8},{10,9... | collective-permute-start | bytes 884744 | tf_op jit(solution)/shard_map/ppermute | solution.py:134
  72.9 1.9 %collective-permute-start.7 = (bf16[1,8,24,256]{3,2,1,0:T(8,128)(2,1)S(1)}, bf16[1,8,24,256]{3,2,1,0:T(8,128)(2,1)S(1)}, u32[]{:S(2)}, u32[]{:S(2)}) collective-permute-start(bf16[1,8,24,256]{3,2,1,0:T(8,128)(2,1)S(1)} %slice.4), channel_id=1, source_target_pairs={{0,2},{1,3},{2,4},{3,5},{4,6},{5,7},{6,8},{7,9},{8,10},{9,11},{10,... | collective-permute-start | bytes 294920 | tf_op jit(solution)/shard_map/ppermute | solution.py:134
  74.9 0.0 all-to-all-done.refs_0_
  74.9 0.0 copy-start
  74.9 1.1 %copy-done = bf16[16,8,24,256]{3,2,1,0:T(8,128)(2,1)} copy-done((bf16[16,8,24,256]{3,2,1,0:T(8,128)(2,1)}, bf16[16,8,24,256]{3,2,1,0:T(8,128)(2,1)S(1)}, u32[]{:S(2)}) %copy-start) | copy-done | bytes 1572888
  76.0 4.0 %receiver_pairs.1.refs_12_ = bf16[8,16,24,512]{3,2,1,0:T(8,128)(2,1)} custom-call(bf16[16,8,24,256]{3,2,1,0:T(8,128)(2,1)} %copy-done), custom_call_target="tpu_custom_call" | custom-call | tf_op jit(solution)/shard_map/receiver_pairs/pallas_call | solution.py:73
  80.0 0.0 collective-permute-done.5.refs_4_
  80.0 0.0 copy-start.1
  80.0 1.6 %collective-permute-done.7.refs_6_ = bf16[1,8,24,256]{3,2,1,0:T(8,128)(2,1)S(1)} collective-permute-done((bf16[1,8,24,256]{3,2,1,0:T(8,128)(2,1)S(1)}, bf16[1,8,24,256]{3,2,1,0:T(8,128)(2,1)S(1)}, u32[]{:S(2)}, u32[]{:S(2)}) %collective-permute-start.7) | collective-permute-done | bytes 98336 | tf_op jit(solution)/shard_map/ppermute | solution.py:134
  81.5 0.0 copy-start.4
  81.6 3.9 %collective-permute-start.11 = (bf16[4,8,24,256]{3,2,1,0:T(8,128)(2,1)S(1)}, bf16[4,8,24,256]{3,2,1,0:T(8,128)(2,1)S(1)}, u32[]{:S(2)}, u32[]{:S(2)}) collective-permute-start(bf16[4,8,24,256]{3,2,1,0:T(8,128)(2,1)S(1)} %pad_maximum_fusion), channel_id=1, source_target_pairs={{0,16},{1,17},{2,18},{3,19},{4,20},{5,21},{6,22},{7,23},{8,24},{9,... | collective-permute-start | bytes 1179656 | tf_op jit(solution)/shard_map/ppermute | solution.py:137
  85.6 0.0 collective-permute-done.8.refs_7_
  85.6 0.0 copy-start.7
  85.6 1.9 %collective-permute-start.10 = (bf16[3,8,24,256]{3,2,1,0:T(8,128)(2,1)S(1)}, bf16[3,8,24,256]{3,2,1,0:T(8,128)(2,1)S(1)}, u32[]{:S(2)}, u32[]{:S(2)}) collective-permute-start(bf16[3,8,24,256]{3,2,1,0:T(8,128)(2,1)S(1)} %collective-permute-done.8.refs_7_), channel_id=1, source_target_pairs={{0,15},{1,0},{2,1},{3,2},{4,3},{5,4},{6,5},{7,6},{8,7},{9,8},{10,9... | collective-permute-start | bytes 884744 | tf_op jit(solution)/shard_map/ppermute | solution.py:134
  87.5 3.9 %collective-permute-start.9 = (bf16[3,8,24,256]{3,2,1,0:T(8,128)(2,1)S(1)}, bf16[3,8,24,256]{3,2,1,0:T(8,128)(2,1)S(1)}, u32[]{:S(2)}, u32[]{:S(2)}) collective-permute-start(bf16[3,8,24,256]{3,2,1,0:T(8,128)(2,1)S(1)} %collective-permute-done.8.refs_7_), channel_id=1, source_target_pairs={{0,1},{1,2},{2,3},{3,4},{4,5},{5,6},{6,7},{7,8},{8,9},{9,10},{10,1... | collective-permute-start | bytes 884744 | tf_op jit(solution)/shard_map/ppermute | solution.py:134
  91.4 0.0 collective-permute-done.6.refs_5_
  91.4 0.0 copy-start.8
  91.5 1.9 %collective-permute-start.12 = (bf16[3,8,24,256]{3,2,1,0:T(8,128)(2,1)S(1)}, bf16[3,8,24,256]{3,2,1,0:T(8,128)(2,1)S(1)}, u32[]{:S(2)}, u32[]{:S(2)}) collective-permute-start(bf16[3,8,24,256]{3,2,1,0:T(8,128)(2,1)S(1)} %collective-permute-done.6.refs_5_), channel_id=1, source_target_pairs={{0,16},{1,17},{2,18},{3,19},{4,20},{5,21},{6,22},{7,23},{8,24},{9,... | collective-permute-start | bytes 884744 | tf_op jit(solution)/shard_map/ppermute | solution.py:137
  93.4 0.0 copy-done.12
  93.4 0.0 copy-done.13
  93.4 0.6 pad_add_fusion.refs_0_
  94.0 0.2 collective-permute-done.10.refs_9_
  94.2 0.0 copy-start.9
  94.2 3.1 %collective-permute-done.9.refs_8_ = bf16[3,8,24,256]{3,2,1,0:T(8,128)(2,1)S(1)} collective-permute-done((bf16[3,8,24,256]{3,2,1,0:T(8,128)(2,1)S(1)}, bf16[3,8,24,256]{3,2,1,0:T(8,128)(2,1)S(1)}, u32[]{:S(2)}, u32[]{:S(2)}) %collective-permute-start.9) | collective-permute-done | bytes 294944 | tf_op jit(solution)/shard_map/ppermute | solution.py:134
  97.3 0.0 copy-start.10
  97.3 2.7 %collective-permute-done.12.refs_11_ = bf16[3,8,24,256]{3,2,1,0:T(8,128)(2,1)S(1)} collective-permute-done((bf16[3,8,24,256]{3,2,1,0:T(8,128)(2,1)S(1)}, bf16[3,8,24,256]{3,2,1,0:T(8,128)(2,1)S(1)}, u32[]{:S(2)}, u32[]{:S(2)}) %collective-permute-start.12) | collective-permute-done | bytes 294944 | tf_op jit(solution)/shard_map/ppermute | solution.py:137
  100.1 0.0 copy-start.11
  100.1 0.7 copy-done.11
  100.8 0.0 collective-permute-done.11.refs_10_
  100.8 0.0 copy-done.2
  100.8 0.0 copy-done.3
  100.8 0.0 copy-done.6
  100.8 0.0 copy-done.1
  100.8 0.0 copy-done.4
  100.8 0.0 copy-done.7
  100.8 0.0 copy-done.8
  100.8 0.0 copy-done.9
  100.8 0.0 copy-done.10
  100.9 0.0 copy-start.5
  100.9 0.7 copy-done.5
  101.6 6.0 %stack.1 = bf16[2,8,512,256]{3,2,1,0:T(8,128)(2,1)} custom-call(s32[33]{0:T(128)} %pad_add_fusion.refs_0_, bf16[3,8,24,256]{3,2,1,0:T(8,128)(2,1)} %copy-done.2, bf16[3,8,24,256]{3,2,1,0:T(8,128)(2,1)} %copy-done.3, bf16[3,8,24,256]{3,2,1,0:T(8,128)(2,1)} %copy-done.6, bf16[3,8,24,256]{3,2,1,0:T(8,128)(2,1)} %copy-done.1, bf16[3,8,24,256]{3,2,1,0:T(8,128)(2,1)} %copy-done.8, ...), custom_call_target="tpu_custom_call" | custom-call | tf_op jit(solution)/shard_map/stack/pallas_call | solution.py:112
  (4 shorter events, 0.1 us)
Async XLA Ops:
  2.3 9.4 %copy-start.14 = (bf16[8,24,256]{2,1,0:T(8,128)(2,1)S(1)}, bf16[8,24,256]{2,1,0:T(8,128)(2,1)}, u32[]{:S(2)}) copy-start(bf16[8,24,256]{2,1,0:T(8,128)(2,1)} %get-tuple-element.9) | copy-start | bytes 294916
  2.3 72.6 %all-to-all-start = ((bf16[16,8,24,256]{3,2,1,0:T(8,128)(2,1)}), bf16[16,8,24,256]{3,2,1,0:T(8,128)(2,1)S(1)}, u32[]{:S(2)}, u32[]{:S(2)}) async-start(bf16[16,8,24,256]{3,2,1,0:T(8,128)(2,1)} %get-tuple-element.10), calls=%async_computation | async-start | bytes 3145728 | tf_op jit(solution)/shard_map/all_to_all | solution.py:153
  11.6 22.4 %collective-permute-start.2 = (bf16[8,24,256]{2,1,0:T(8,128)(2,1)S(1)}, bf16[8,24,256]{2,1,0:T(8,128)(2,1)S(1)}, u32[]{:S(2)}, u32[]{:S(2)}) collective-permute-start(bf16[8,24,256]{2,1,0:T(8,128)(2,1)S(1)} %copy-done.14), channel_id=1, source_target_pairs={{0,11},{1,12},{2,43},{3,44},{4,75},{5,76},{6,107},{7,108},{8,139},... | collective-permute-start | bytes 294920 | tf_op jit(solution)/shard_map/ppermute | solution.py:146
  19.8 17.0 %collective-permute-start.1 = (bf16[8,24,256]{2,1,0:T(8,128)(2,1)S(1)}, bf16[8,24,256]{2,1,0:T(8,128)(2,1)S(1)}, u32[]{:S(2)}, u32[]{:S(2)}) collective-permute-start(bf16[8,24,256]{2,1,0:T(8,128)(2,1)S(1)} %copy-done.14), channel_id=1, source_target_pairs={{0,5},{1,6},{2,37},{3,38},{4,69},{5,70},{6,101},{7,102},{8,133},{9... | collective-permute-start | bytes 294920 | tf_op jit(solution)/shard_map/ppermute | solution.py:146
  32.1 21.9 %collective-permute-start = (bf16[8,24,256]{2,1,0:T(8,128)(2,1)S(1)}, bf16[8,24,256]{2,1,0:T(8,128)(2,1)S(1)}, u32[]{:S(2)}, u32[]{:S(2)}) collective-permute-start(bf16[8,24,256]{2,1,0:T(8,128)(2,1)S(1)} %copy-done.14), channel_id=1, source_target_pairs={{0,0},{1,1},{2,32},{3,33},{4,64},{5,65},{6,96},{7,97},{8,128},{9,1... | collective-permute-start | bytes 294920 | tf_op jit(solution)/shard_map/ppermute | solution.py:146
  54.0 39.4 %copy-start.12 = (s32[32]{0:T(128)S(1)}, s32[32]{0:T(128)}, u32[]{:S(2)}) copy-start(s32[32]{0:T(128)} %constant.60.clone) | copy-start | bytes 388
  54.0 39.4 %copy-start.13 = (pred[32]{0:T(512)(128)(4,1)S(1)}, pred[32]{0:T(512)(128)(4,1)}, u32[]{:S(2)}) copy-start(pred[32]{0:T(512)(128)(4,1)} %constant.59.clone) | copy-start | bytes 100
  54.1 46.7 %copy-start.2 = (bf16[3,8,24,256]{3,2,1,0:T(8,128)(2,1)}, bf16[3,8,24,256]{3,2,1,0:T(8,128)(2,1)S(1)}, u32[]{:S(2)}) copy-start(bf16[3,8,24,256]{3,2,1,0:T(8,128)(2,1)S(1)} %pad_maximum_fusion.1.refs_1_) | copy-start | bytes 884740
  54.1 9.8 %collective-permute-start.3 = (bf16[3,8,24,256]{3,2,1,0:T(8,128)(2,1)S(1)}, bf16[3,8,24,256]{3,2,1,0:T(8,128)(2,1)S(1)}, u32[]{:S(2)}, u32[]{:S(2)}) collective-permute-start(bf16[3,8,24,256]{3,2,1,0:T(8,128)(2,1)S(1)} %pad_maximum_fusion.1.refs_1_), channel_id=1, source_target_pairs={{0,1},{1,2},{2,3},{3,4},{4,5},{5,6},{6,7},{7,8},{8,9},{9,10},{10,1... | collective-permute-start | bytes 884744 | tf_op jit(solution)/shard_map/ppermute | solution.py:134
  56.0 11.7 %collective-permute-start.4 = (bf16[3,8,24,256]{3,2,1,0:T(8,128)(2,1)S(1)}, bf16[3,8,24,256]{3,2,1,0:T(8,128)(2,1)S(1)}, u32[]{:S(2)}, u32[]{:S(2)}) collective-permute-start(bf16[3,8,24,256]{3,2,1,0:T(8,128)(2,1)S(1)} %pad_maximum_fusion.1.refs_1_), channel_id=1, source_target_pairs={{0,15},{1,0},{2,1},{3,2},{4,3},{5,4},{6,5},{7,6},{8,7},{9,8},{10,9... | collective-permute-start | bytes 884744 | tf_op jit(solution)/shard_map/ppermute | solution.py:134
  63.9 36.9 %copy-start.3 = (bf16[3,8,24,256]{3,2,1,0:T(8,128)(2,1)}, bf16[3,8,24,256]{3,2,1,0:T(8,128)(2,1)S(1)}, u32[]{:S(2)}) copy-start(bf16[3,8,24,256]{3,2,1,0:T(8,128)(2,1)S(1)} %collective-permute-done.3.refs_2_) | copy-start | bytes 884740
  63.9 16.1 %collective-permute-start.5 = (bf16[3,8,24,256]{3,2,1,0:T(8,128)(2,1)S(1)}, bf16[3,8,24,256]{3,2,1,0:T(8,128)(2,1)S(1)}, u32[]{:S(2)}, u32[]{:S(2)}) collective-permute-start(bf16[3,8,24,256]{3,2,1,0:T(8,128)(2,1)S(1)} %collective-permute-done.3.refs_2_), channel_id=1, source_target_pairs={{0,1},{1,2},{2,3},{3,4},{4,5},{5,6},{6,7},{7,8},{8,9},{9,10},{10,1... | collective-permute-start | bytes 884744 | tf_op jit(solution)/shard_map/ppermute | solution.py:134
  65.8 19.7 %collective-permute-start.8 = (bf16[3,8,24,256]{3,2,1,0:T(8,128)(2,1)S(1)}, bf16[3,8,24,256]{3,2,1,0:T(8,128)(2,1)S(1)}, u32[]{:S(2)}, u32[]{:S(2)}) collective-permute-start(bf16[3,8,24,256]{3,2,1,0:T(8,128)(2,1)S(1)} %pad_maximum_fusion.1.refs_1_), channel_id=1, source_target_pairs={{0,16},{1,17},{2,18},{3,19},{4,20},{5,21},{6,22},{7,23},{8,24},{9,... | collective-permute-start | bytes 884744 | tf_op jit(solution)/shard_map/ppermute | solution.py:137
  67.8 33.0 %copy-start.6 = (bf16[3,8,24,256]{3,2,1,0:T(8,128)(2,1)}, bf16[3,8,24,256]{3,2,1,0:T(8,128)(2,1)S(1)}, u32[]{:S(2)}) copy-start(bf16[3,8,24,256]{3,2,1,0:T(8,128)(2,1)S(1)} %collective-permute-done.4.refs_3_) | copy-start | bytes 884740
  67.8 23.7 %collective-permute-start.6 = (bf16[3,8,24,256]{3,2,1,0:T(8,128)(2,1)S(1)}, bf16[3,8,24,256]{3,2,1,0:T(8,128)(2,1)S(1)}, u32[]{:S(2)}, u32[]{:S(2)}) collective-permute-start(bf16[3,8,24,256]{3,2,1,0:T(8,128)(2,1)S(1)} %collective-permute-done.4.refs_3_), channel_id=1, source_target_pairs={{0,15},{1,0},{2,1},{3,2},{4,3},{5,4},{6,5},{7,6},{8,7},{9,8},{10,9... | collective-permute-start | bytes 884744 | tf_op jit(solution)/shard_map/ppermute | solution.py:134
  72.9 8.6 %collective-permute-start.7 = (bf16[1,8,24,256]{3,2,1,0:T(8,128)(2,1)S(1)}, bf16[1,8,24,256]{3,2,1,0:T(8,128)(2,1)S(1)}, u32[]{:S(2)}, u32[]{:S(2)}) collective-permute-start(bf16[1,8,24,256]{3,2,1,0:T(8,128)(2,1)S(1)} %slice.4), channel_id=1, source_target_pairs={{0,2},{1,3},{2,4},{3,5},{4,6},{5,7},{6,8},{7,9},{8,10},{9,11},{10,... | collective-permute-start | bytes 294920 | tf_op jit(solution)/shard_map/ppermute | solution.py:134
  74.9 1.1 %copy-start = (bf16[16,8,24,256]{3,2,1,0:T(8,128)(2,1)}, bf16[16,8,24,256]{3,2,1,0:T(8,128)(2,1)S(1)}, u32[]{:S(2)}) copy-start(bf16[16,8,24,256]{3,2,1,0:T(8,128)(2,1)S(1)} %all-to-all-done.refs_0_) | copy-start | bytes 4718596
  80.0 20.8 %copy-start.1 = (bf16[3,8,24,256]{3,2,1,0:T(8,128)(2,1)}, bf16[3,8,24,256]{3,2,1,0:T(8,128)(2,1)S(1)}, u32[]{:S(2)}) copy-start(bf16[3,8,24,256]{3,2,1,0:T(8,128)(2,1)S(1)} %collective-permute-done.5.refs_4_) | copy-start | bytes 884740
  81.5 19.3 %copy-start.4 = (bf16[1,8,24,256]{3,2,1,0:T(8,128)(2,1)}, bf16[1,8,24,256]{3,2,1,0:T(8,128)(2,1)S(1)}, u32[]{:S(2)}) copy-start(bf16[1,8,24,256]{3,2,1,0:T(8,128)(2,1)S(1)} %collective-permute-done.7.refs_6_) | copy-start | bytes 294916
  81.6 19.2 %collective-permute-start.11 = (bf16[4,8,24,256]{3,2,1,0:T(8,128)(2,1)S(1)}, bf16[4,8,24,256]{3,2,1,0:T(8,128)(2,1)S(1)}, u32[]{:S(2)}, u32[]{:S(2)}) collective-permute-start(bf16[4,8,24,256]{3,2,1,0:T(8,128)(2,1)S(1)} %pad_maximum_fusion), channel_id=1, source_target_pairs={{0,16},{1,17},{2,18},{3,19},{4,20},{5,21},{6,22},{7,23},{8,24},{9,... | collective-permute-start | bytes 1179656 | tf_op jit(solution)/shard_map/ppermute | solution.py:137
  85.6 15.3 %copy-start.7 = (bf16[3,8,24,256]{3,2,1,0:T(8,128)(2,1)}, bf16[3,8,24,256]{3,2,1,0:T(8,128)(2,1)S(1)}, u32[]{:S(2)}) copy-start(bf16[3,8,24,256]{3,2,1,0:T(8,128)(2,1)S(1)} %collective-permute-done.8.refs_7_) | copy-start | bytes 884740
  85.6 8.6 %collective-permute-start.10 = (bf16[3,8,24,256]{3,2,1,0:T(8,128)(2,1)S(1)}, bf16[3,8,24,256]{3,2,1,0:T(8,128)(2,1)S(1)}, u32[]{:S(2)}, u32[]{:S(2)}) collective-permute-start(bf16[3,8,24,256]{3,2,1,0:T(8,128)(2,1)S(1)} %collective-permute-done.8.refs_7_), channel_id=1, source_target_pairs={{0,15},{1,0},{2,1},{3,2},{4,3},{5,4},{6,5},{7,6},{8,7},{9,8},{10,9... | collective-permute-start | bytes 884744 | tf_op jit(solution)/shard_map/ppermute | solution.py:134
  87.5 9.8 %collective-permute-start.9 = (bf16[3,8,24,256]{3,2,1,0:T(8,128)(2,1)S(1)}, bf16[3,8,24,256]{3,2,1,0:T(8,128)(2,1)S(1)}, u32[]{:S(2)}, u32[]{:S(2)}) collective-permute-start(bf16[3,8,24,256]{3,2,1,0:T(8,128)(2,1)S(1)} %collective-permute-done.8.refs_7_), channel_id=1, source_target_pairs={{0,1},{1,2},{2,3},{3,4},{4,5},{5,6},{6,7},{7,8},{8,9},{9,10},{10,1... | collective-permute-start | bytes 884744 | tf_op jit(solution)/shard_map/ppermute | solution.py:134
  91.4 9.4 %copy-start.8 = (bf16[3,8,24,256]{3,2,1,0:T(8,128)(2,1)}, bf16[3,8,24,256]{3,2,1,0:T(8,128)(2,1)S(1)}, u32[]{:S(2)}) copy-start(bf16[3,8,24,256]{3,2,1,0:T(8,128)(2,1)S(1)} %collective-permute-done.6.refs_5_) | copy-start | bytes 884740
  91.5 8.6 %collective-permute-start.12 = (bf16[3,8,24,256]{3,2,1,0:T(8,128)(2,1)S(1)}, bf16[3,8,24,256]{3,2,1,0:T(8,128)(2,1)S(1)}, u32[]{:S(2)}, u32[]{:S(2)}) collective-permute-start(bf16[3,8,24,256]{3,2,1,0:T(8,128)(2,1)S(1)} %collective-permute-done.6.refs_5_), channel_id=1, source_target_pairs={{0,16},{1,17},{2,18},{3,19},{4,20},{5,21},{6,22},{7,23},{8,24},{9,... | collective-permute-start | bytes 884744 | tf_op jit(solution)/shard_map/ppermute | solution.py:137
  94.2 6.7 %copy-start.9 = (bf16[3,8,24,256]{3,2,1,0:T(8,128)(2,1)}, bf16[3,8,24,256]{3,2,1,0:T(8,128)(2,1)S(1)}, u32[]{:S(2)}) copy-start(bf16[3,8,24,256]{3,2,1,0:T(8,128)(2,1)S(1)} %collective-permute-done.10.refs_9_) | copy-start | bytes 884740
  97.3 3.5 %copy-start.10 = (bf16[3,8,24,256]{3,2,1,0:T(8,128)(2,1)}, bf16[3,8,24,256]{3,2,1,0:T(8,128)(2,1)S(1)}, u32[]{:S(2)}) copy-start(bf16[3,8,24,256]{3,2,1,0:T(8,128)(2,1)S(1)} %collective-permute-done.9.refs_8_) | copy-start | bytes 884740
  100.1 0.7 copy-start.11
  100.9 0.8 copy-start.5

commit v6 on v5

--- a/solution.py
+++ b/solution.py
@@ -8,7 +8,7 @@
 
 TILE = 8
 STACK_STEP = 4
-STEP = 2
+STEP = 4
 
 OWN_SLOTS = ((0, -5, 5), (-1, -6, 4), (1, -4, 6), (-2, -7, 3), (2, -3, 7), (8,))
 NEIGHBOUR_SLOTS = ((0, -5, 5), (-1, -6, 4), (1, -4, 6), (-2, -7, 3, 8), (2, -3, 7))

time: 108 us -> 108 us (level)
  Pallas kernels: 12.3 us -> 11.2 us
  transfers between devices with their start and end apart: 14 -> 14, of which waited for: 7 -> 7; matrix products, arithmetic and copies ran while one was open for 1% -> 1% of each run, Pallas kernels for 4% -> 3%
where the time goes in v6:
time: 108 us
  starting transfers between devices  61.3 us (57%)
  waiting for transfers between devices  31.4 us (29%)
  Pallas kernels  11.2 us (10%)
  local copies, waits for them, and re-layouts  2.65 us (2%)
    ppermute x3, starting transfers between devices, deal(): return lax.ppermute(block, ('src', 'rcv'), pairs)  22.4 us
    ppermute x7, starting transfers between devices, shift(): lax.ppermute(block, 'rcv', [(r, along(r, step)) for r in range(cols_n)])  21.9 us
    ppermute x3, waiting for transfers between devices, deal(): return lax.ppermute(block, ('src', 'rcv'), pairs)  20 us
    all_to_all x1, starting transfers between devices, body(): receivers = (lax.all_to_all(copies, 'src', 0, 0),)  9.37 us
    ppermute x7, waiting for transfers between devices, shift(): lax.ppermute(block, 'rcv', [(r, along(r, step)) for r in range(cols_n)])  8.7 us
    ppermute x3, starting transfers between devices, trade(): lax.ppermute(block, 'rcv', [(r, (r + length) % cols_n) for r in range(col...  7.76 us
    pallas_call x1, Pallas kernels, stack(): pl.pallas_call(lambda *refs: stack_kernel(parities, scale, *refs), grid=(...  6.04 us
    pallas_call x1, Pallas kernels, receiver_pairs(): pl.pallas_call(receiver_kernel, grid=(bins // STEP,), in_specs=[pl.BlockS...  2.91 us
  transfers between devices with their start and end apart: 14, of which 7 were waited for; matrix products, arithmetic and copies ran while one was open for 1% of the time, Pallas kernels for 3%

profile of v6, /device:TPU:18, one launch (start us, length us, event | category | flops | bytes accessed | tf_op | source)
XLA Modules:
  0.0 107.7 jit_solution(12953968438987608233)
XLA Ops:
  0.0 2.3 %whiten.1 = (bf16[8,24,256]{2,1,0:T(8,128)(2,1)}, bf16[16,8,24,256]{3,2,1,0:T(8,128)(2,1)}) custom-call(bf16[2,12,8,256]{3,2,1,0:T(8,128)(2,1)} %bitcast.8, s32[12,256]{1,0:T(8,128)} %refs_1_.1), custom_call_target="tpu_custom_call" | custom-call | tf_op jit(solution)/shard_map/whiten/pallas_call | solution.py:42
  2.3 0.0 copy-start.14
  2.3 9.4 %all-to-all-start = ((bf16[16,8,24,256]{3,2,1,0:T(8,128)(2,1)}), bf16[16,8,24,256]{3,2,1,0:T(8,128)(2,1)S(1)}, u32[]{:S(2)}, u32[]{:S(2)}) async-start(bf16[16,8,24,256]{3,2,1,0:T(8,128)(2,1)} %get-tuple-element.10), calls=%async_computation | async-start | bytes 3145728 | tf_op jit(solution)/shard_map/all_to_all | solution.py:153
  11.6 0.0 copy-done.14
  11.6 8.2 %collective-permute-start.2 = (bf16[8,24,256]{2,1,0:T(8,128)(2,1)S(1)}, bf16[8,24,256]{2,1,0:T(8,128)(2,1)S(1)}, u32[]{:S(2)}, u32[]{:S(2)}) collective-permute-start(bf16[8,24,256]{2,1,0:T(8,128)(2,1)S(1)} %copy-done.14), channel_id=1, source_target_pairs={{0,11},{1,12},{2,43},{3,44},{4,75},{5,76},{6,107},{7,108},{8,139},... | collective-permute-start | bytes 294920 | tf_op jit(solution)/shard_map/ppermute | solution.py:146
  19.8 12.3 %collective-permute-start.1 = (bf16[8,24,256]{2,1,0:T(8,128)(2,1)S(1)}, bf16[8,24,256]{2,1,0:T(8,128)(2,1)S(1)}, u32[]{:S(2)}, u32[]{:S(2)}) collective-permute-start(bf16[8,24,256]{2,1,0:T(8,128)(2,1)S(1)} %copy-done.14), channel_id=1, source_target_pairs={{0,5},{1,6},{2,37},{3,38},{4,69},{5,70},{6,101},{7,102},{8,133},{9... | collective-permute-start | bytes 294920 | tf_op jit(solution)/shard_map/ppermute | solution.py:146
  32.1 1.9 %collective-permute-start = (bf16[8,24,256]{2,1,0:T(8,128)(2,1)S(1)}, bf16[8,24,256]{2,1,0:T(8,128)(2,1)S(1)}, u32[]{:S(2)}, u32[]{:S(2)}) collective-permute-start(bf16[8,24,256]{2,1,0:T(8,128)(2,1)S(1)} %copy-done.14), channel_id=1, source_target_pairs={{0,0},{1,1},{2,32},{3,33},{4,64},{5,65},{6,96},{7,97},{8,128},{9,1... | collective-permute-start | bytes 294920 | tf_op jit(solution)/shard_map/ppermute | solution.py:146
  34.0 0.0 collective-permute-done.2
  34.0 2.8 %collective-permute-done.1 = bf16[8,24,256]{2,1,0:T(8,128)(2,1)S(1)} collective-permute-done((bf16[8,24,256]{2,1,0:T(8,128)(2,1)S(1)}, bf16[8,24,256]{2,1,0:T(8,128)(2,1)S(1)}, u32[]{:S(2)}, u32[]{:S(2)}) %collective-permute-start.1) | collective-permute-done | bytes 98336 | tf_op jit(solution)/shard_map/ppermute | solution.py:146
  36.9 17.1 %collective-permute-done = bf16[8,24,256]{2,1,0:T(8,128)(2,1)S(1)} collective-permute-done((bf16[8,24,256]{2,1,0:T(8,128)(2,1)S(1)}, bf16[8,24,256]{2,1,0:T(8,128)(2,1)S(1)}, u32[]{:S(2)}, u32[]{:S(2)}) %collective-permute-start) | collective-permute-done | bytes 98336 | tf_op jit(solution)/shard_map/ppermute | solution.py:146
  54.0 0.0 copy-start.12
  54.0 0.0 copy-start.13
  54.1 0.0 copy-start.2
  54.1 1.9 %collective-permute-start.3 = (bf16[3,8,24,256]{3,2,1,0:T(8,128)(2,1)S(1)}, bf16[3,8,24,256]{3,2,1,0:T(8,128)(2,1)S(1)}, u32[]{:S(2)}, u32[]{:S(2)}) collective-permute-start(bf16[3,8,24,256]{3,2,1,0:T(8,128)(2,1)S(1)} %pad_maximum_fusion.1.refs_1_), channel_id=1, source_target_pairs={{0,1},{1,2},{2,3},{3,4},{4,5},{5,6},{6,7},{7,8},{8,9},{9,10},{10,1... | collective-permute-start | bytes 884744 | tf_op jit(solution)/shard_map/ppermute | solution.py:134
  56.0 5.1 %collective-permute-start.4 = (bf16[3,8,24,256]{3,2,1,0:T(8,128)(2,1)S(1)}, bf16[3,8,24,256]{3,2,1,0:T(8,128)(2,1)S(1)}, u32[]{:S(2)}, u32[]{:S(2)}) collective-permute-start(bf16[3,8,24,256]{3,2,1,0:T(8,128)(2,1)S(1)} %pad_maximum_fusion.1.refs_1_), channel_id=1, source_target_pairs={{0,15},{1,0},{2,1},{3,2},{4,3},{5,4},{6,5},{7,6},{8,7},{9,8},{10,9... | collective-permute-start | bytes 884744 | tf_op jit(solution)/shard_map/ppermute | solution.py:134
  61.1 2.8 %collective-permute-done.3.refs_2_ = bf16[3,8,24,256]{3,2,1,0:T(8,128)(2,1)S(1)} collective-permute-done((bf16[3,8,24,256]{3,2,1,0:T(8,128)(2,1)S(1)}, bf16[3,8,24,256]{3,2,1,0:T(8,128)(2,1)S(1)}, u32[]{:S(2)}, u32[]{:S(2)}) %collective-permute-start.3) | collective-permute-done | bytes 294944 | tf_op jit(solution)/shard_map/ppermute | solution.py:134
  63.9 0.0 copy-start.3
  63.9 1.9 %collective-permute-start.5 = (bf16[3,8,24,256]{3,2,1,0:T(8,128)(2,1)S(1)}, bf16[3,8,24,256]{3,2,1,0:T(8,128)(2,1)S(1)}, u32[]{:S(2)}, u32[]{:S(2)}) collective-permute-start(bf16[3,8,24,256]{3,2,1,0:T(8,128)(2,1)S(1)} %collective-permute-done.3.refs_2_), channel_id=1, source_target_pairs={{0,1},{1,2},{2,3},{3,4},{4,5},{5,6},{6,7},{7,8},{8,9},{9,10},{10,1... | collective-permute-start | bytes 884744 | tf_op jit(solution)/shard_map/ppermute | solution.py:134
  65.8 1.9 %collective-permute-start.8 = (bf16[3,8,24,256]{3,2,1,0:T(8,128)(2,1)S(1)}, bf16[3,8,24,256]{3,2,1,0:T(8,128)(2,1)S(1)}, u32[]{:S(2)}, u32[]{:S(2)}) collective-permute-start(bf16[3,8,24,256]{3,2,1,0:T(8,128)(2,1)S(1)} %pad_maximum_fusion.1.refs_1_), channel_id=1, source_target_pairs={{0,16},{1,17},{2,18},{3,19},{4,20},{5,21},{6,22},{7,23},{8,24},{9,... | collective-permute-start | bytes 884744 | tf_op jit(solution)/shard_map/ppermute | solution.py:137
  67.7 0.0 collective-permute-done.4.refs_3_
  67.8 0.0 copy-start.6
  67.8 5.1 %collective-permute-start.6 = (bf16[3,8,24,256]{3,2,1,0:T(8,128)(2,1)S(1)}, bf16[3,8,24,256]{3,2,1,0:T(8,128)(2,1)S(1)}, u32[]{:S(2)}, u32[]{:S(2)}) collective-permute-start(bf16[3,8,24,256]{3,2,1,0:T(8,128)(2,1)S(1)} %collective-permute-done.4.refs_3_), channel_id=1, source_target_pairs={{0,15},{1,0},{2,1},{3,2},{4,3},{5,4},{6,5},{7,6},{8,7},{9,8},{10,9... | collective-permute-start | bytes 884744 | tf_op jit(solution)/shard_map/ppermute | solution.py:134
  72.9 1.9 %collective-permute-start.7 = (bf16[1,8,24,256]{3,2,1,0:T(8,128)(2,1)S(1)}, bf16[1,8,24,256]{3,2,1,0:T(8,128)(2,1)S(1)}, u32[]{:S(2)}, u32[]{:S(2)}) collective-permute-start(bf16[1,8,24,256]{3,2,1,0:T(8,128)(2,1)S(1)} %slice.4), channel_id=1, source_target_pairs={{0,2},{1,3},{2,4},{3,5},{4,6},{5,7},{6,8},{7,9},{8,10},{9,11},{10,... | collective-permute-start | bytes 294920 | tf_op jit(solution)/shard_map/ppermute | solution.py:134
  74.9 0.0 all-to-all-done.refs_0_
  74.9 0.0 copy-start
  74.9 1.1 %copy-done = bf16[16,8,24,256]{3,2,1,0:T(8,128)(2,1)} copy-done((bf16[16,8,24,256]{3,2,1,0:T(8,128)(2,1)}, bf16[16,8,24,256]{3,2,1,0:T(8,128)(2,1)S(1)}, u32[]{:S(2)}) %copy-start) | copy-done | bytes 1572888
  76.0 2.9 %receiver_pairs.1.refs_12_ = bf16[8,16,24,512]{3,2,1,0:T(8,128)(2,1)} custom-call(bf16[16,8,24,256]{3,2,1,0:T(8,128)(2,1)} %copy-done), custom_call_target="tpu_custom_call" | custom-call | tf_op jit(solution)/shard_map/receiver_pairs/pallas_call | solution.py:73
  78.9 0.0 collective-permute-done.5.refs_4_
  78.9 0.0 copy-start.1
  78.9 2.6 %collective-permute-done.7.refs_6_ = bf16[1,8,24,256]{3,2,1,0:T(8,128)(2,1)S(1)} collective-permute-done((bf16[1,8,24,256]{3,2,1,0:T(8,128)(2,1)S(1)}, bf16[1,8,24,256]{3,2,1,0:T(8,128)(2,1)S(1)}, u32[]{:S(2)}, u32[]{:S(2)}) %collective-permute-start.7) | collective-permute-done | bytes 98336 | tf_op jit(solution)/shard_map/ppermute | solution.py:134
  81.5 0.0 copy-start.4
  81.6 3.9 %collective-permute-start.11 = (bf16[4,8,24,256]{3,2,1,0:T(8,128)(2,1)S(1)}, bf16[4,8,24,256]{3,2,1,0:T(8,128)(2,1)S(1)}, u32[]{:S(2)}, u32[]{:S(2)}) collective-permute-start(bf16[4,8,24,256]{3,2,1,0:T(8,128)(2,1)S(1)} %pad_maximum_fusion), channel_id=1, source_target_pairs={{0,16},{1,17},{2,18},{3,19},{4,20},{5,21},{6,22},{7,23},{8,24},{9,... | collective-permute-start | bytes 1179656 | tf_op jit(solution)/shard_map/ppermute | solution.py:137
  85.6 0.0 collective-permute-done.8.refs_7_
  85.6 0.0 copy-start.7
  85.6 1.9 %collective-permute-start.10 = (bf16[3,8,24,256]{3,2,1,0:T(8,128)(2,1)S(1)}, bf16[3,8,24,256]{3,2,1,0:T(8,128)(2,1)S(1)}, u32[]{:S(2)}, u32[]{:S(2)}) collective-permute-start(bf16[3,8,24,256]{3,2,1,0:T(8,128)(2,1)S(1)} %collective-permute-done.8.refs_7_), channel_id=1, source_target_pairs={{0,15},{1,0},{2,1},{3,2},{4,3},{5,4},{6,5},{7,6},{8,7},{9,8},{10,9... | collective-permute-start | bytes 884744 | tf_op jit(solution)/shard_map/ppermute | solution.py:134
  87.5 3.9 %collective-permute-start.9 = (bf16[3,8,24,256]{3,2,1,0:T(8,128)(2,1)S(1)}, bf16[3,8,24,256]{3,2,1,0:T(8,128)(2,1)S(1)}, u32[]{:S(2)}, u32[]{:S(2)}) collective-permute-start(bf16[3,8,24,256]{3,2,1,0:T(8,128)(2,1)S(1)} %collective-permute-done.8.refs_7_), channel_id=1, source_target_pairs={{0,1},{1,2},{2,3},{3,4},{4,5},{5,6},{6,7},{7,8},{8,9},{9,10},{10,1... | collective-permute-start | bytes 884744 | tf_op jit(solution)/shard_map/ppermute | solution.py:134
  91.4 0.0 collective-permute-done.6.refs_5_
  91.4 0.0 copy-start.8
  91.5 1.9 %collective-permute-start.12 = (bf16[3,8,24,256]{3,2,1,0:T(8,128)(2,1)S(1)}, bf16[3,8,24,256]{3,2,1,0:T(8,128)(2,1)S(1)}, u32[]{:S(2)}, u32[]{:S(2)}) collective-permute-start(bf16[3,8,24,256]{3,2,1,0:T(8,128)(2,1)S(1)} %collective-permute-done.6.refs_5_), channel_id=1, source_target_pairs={{0,16},{1,17},{2,18},{3,19},{4,20},{5,21},{6,22},{7,23},{8,24},{9,... | collective-permute-start | bytes 884744 | tf_op jit(solution)/shard_map/ppermute | solution.py:137
  93.4 0.0 copy-done.12
  93.4 0.0 copy-done.13
  93.4 0.6 pad_add_fusion.refs_0_
  94.0 0.2 collective-permute-done.10.refs_9_
  94.2 0.0 copy-start.9
  94.2 3.1 %collective-permute-done.9.refs_8_ = bf16[3,8,24,256]{3,2,1,0:T(8,128)(2,1)S(1)} collective-permute-done((bf16[3,8,24,256]{3,2,1,0:T(8,128)(2,1)S(1)}, bf16[3,8,24,256]{3,2,1,0:T(8,128)(2,1)S(1)}, u32[]{:S(2)}, u32[]{:S(2)}) %collective-permute-start.9) | collective-permute-done | bytes 294944 | tf_op jit(solution)/shard_map/ppermute | solution.py:134
  97.3 0.0 copy-start.10
  97.3 2.7 %collective-permute-done.12.refs_11_ = bf16[3,8,24,256]{3,2,1,0:T(8,128)(2,1)S(1)} collective-permute-done((bf16[3,8,24,256]{3,2,1,0:T(8,128)(2,1)S(1)}, bf16[3,8,24,256]{3,2,1,0:T(8,128)(2,1)S(1)}, u32[]{:S(2)}, u32[]{:S(2)}) %collective-permute-start.12) | collective-permute-done | bytes 294944 | tf_op jit(solution)/shard_map/ppermute | solution.py:137
  100.1 0.0 copy-start.11
  100.1 0.7 copy-done.11
  100.8 0.0 collective-permute-done.11.refs_10_
  100.8 0.0 copy-done.2
  100.8 0.0 copy-done.3
  100.8 0.0 copy-done.6
  100.8 0.0 copy-done.1
  100.8 0.0 copy-done.4
  100.8 0.0 copy-done.7
  100.8 0.0 copy-done.8
  100.8 0.0 copy-done.9
  100.8 0.0 copy-done.10
  100.9 0.0 copy-start.5
  100.9 0.7 copy-done.5
  101.6 6.0 %stack.1 = bf16[2,8,512,256]{3,2,1,0:T(8,128)(2,1)} custom-call(s32[33]{0:T(128)} %pad_add_fusion.refs_0_, bf16[3,8,24,256]{3,2,1,0:T(8,128)(2,1)} %copy-done.2, bf16[3,8,24,256]{3,2,1,0:T(8,128)(2,1)} %copy-done.3, bf16[3,8,24,256]{3,2,1,0:T(8,128)(2,1)} %copy-done.6, bf16[3,8,24,256]{3,2,1,0:T(8,128)(2,1)} %copy-done.1, bf16[3,8,24,256]{3,2,1,0:T(8,128)(2,1)} %copy-done.8, ...), custom_call_target="tpu_custom_call" | custom-call | tf_op jit(solution)/shard_map/stack/pallas_call | solution.py:112
  (4 shorter events, 0.1 us)
Async XLA Ops:
  2.3 9.4 %copy-start.14 = (bf16[8,24,256]{2,1,0:T(8,128)(2,1)S(1)}, bf16[8,24,256]{2,1,0:T(8,128)(2,1)}, u32[]{:S(2)}) copy-start(bf16[8,24,256]{2,1,0:T(8,128)(2,1)} %get-tuple-element.9) | copy-start | bytes 294916
  2.3 72.6 %all-to-all-start = ((bf16[16,8,24,256]{3,2,1,0:T(8,128)(2,1)}), bf16[16,8,24,256]{3,2,1,0:T(8,128)(2,1)S(1)}, u32[]{:S(2)}, u32[]{:S(2)}) async-start(bf16[16,8,24,256]{3,2,1,0:T(8,128)(2,1)} %get-tuple-element.10), calls=%async_computation | async-start | bytes 3145728 | tf_op jit(solution)/shard_map/all_to_all | solution.py:153
  11.6 22.4 %collective-permute-start.2 = (bf16[8,24,256]{2,1,0:T(8,128)(2,1)S(1)}, bf16[8,24,256]{2,1,0:T(8,128)(2,1)S(1)}, u32[]{:S(2)}, u32[]{:S(2)}) collective-permute-start(bf16[8,24,256]{2,1,0:T(8,128)(2,1)S(1)} %copy-done.14), channel_id=1, source_target_pairs={{0,11},{1,12},{2,43},{3,44},{4,75},{5,76},{6,107},{7,108},{8,139},... | collective-permute-start | bytes 294920 | tf_op jit(solution)/shard_map/ppermute | solution.py:146
  19.8 17.0 %collective-permute-start.1 = (bf16[8,24,256]{2,1,0:T(8,128)(2,1)S(1)}, bf16[8,24,256]{2,1,0:T(8,128)(2,1)S(1)}, u32[]{:S(2)}, u32[]{:S(2)}) collective-permute-start(bf16[8,24,256]{2,1,0:T(8,128)(2,1)S(1)} %copy-done.14), channel_id=1, source_target_pairs={{0,5},{1,6},{2,37},{3,38},{4,69},{5,70},{6,101},{7,102},{8,133},{9... | collective-permute-start | bytes 294920 | tf_op jit(solution)/shard_map/ppermute | solution.py:146
  32.1 21.9 %collective-permute-start = (bf16[8,24,256]{2,1,0:T(8,128)(2,1)S(1)}, bf16[8,24,256]{2,1,0:T(8,128)(2,1)S(1)}, u32[]{:S(2)}, u32[]{:S(2)}) collective-permute-start(bf16[8,24,256]{2,1,0:T(8,128)(2,1)S(1)} %copy-done.14), channel_id=1, source_target_pairs={{0,0},{1,1},{2,32},{3,33},{4,64},{5,65},{6,96},{7,97},{8,128},{9,1... | collective-permute-start | bytes 294920 | tf_op jit(solution)/shard_map/ppermute | solution.py:146
  54.0 39.4 %copy-start.12 = (s32[32]{0:T(128)S(1)}, s32[32]{0:T(128)}, u32[]{:S(2)}) copy-start(s32[32]{0:T(128)} %constant.60.clone) | copy-start | bytes 388
  54.0 39.4 %copy-start.13 = (pred[32]{0:T(512)(128)(4,1)S(1)}, pred[32]{0:T(512)(128)(4,1)}, u32[]{:S(2)}) copy-start(pred[32]{0:T(512)(128)(4,1)} %constant.59.clone) | copy-start | bytes 100
  54.1 46.7 %copy-start.2 = (bf16[3,8,24,256]{3,2,1,0:T(8,128)(2,1)}, bf16[3,8,24,256]{3,2,1,0:T(8,128)(2,1)S(1)}, u32[]{:S(2)}) copy-start(bf16[3,8,24,256]{3,2,1,0:T(8,128)(2,1)S(1)} %pad_maximum_fusion.1.refs_1_) | copy-start | bytes 884740
  54.1 9.8 %collective-permute-start.3 = (bf16[3,8,24,256]{3,2,1,0:T(8,128)(2,1)S(1)}, bf16[3,8,24,256]{3,2,1,0:T(8,128)(2,1)S(1)}, u32[]{:S(2)}, u32[]{:S(2)}) collective-permute-start(bf16[3,8,24,256]{3,2,1,0:T(8,128)(2,1)S(1)} %pad_maximum_fusion.1.refs_1_), channel_id=1, source_target_pairs={{0,1},{1,2},{2,3},{3,4},{4,5},{5,6},{6,7},{7,8},{8,9},{9,10},{10,1... | collective-permute-start | bytes 884744 | tf_op jit(solution)/shard_map/ppermute | solution.py:134
  56.0 11.7 %collective-permute-start.4 = (bf16[3,8,24,256]{3,2,1,0:T(8,128)(2,1)S(1)}, bf16[3,8,24,256]{3,2,1,0:T(8,128)(2,1)S(1)}, u32[]{:S(2)}, u32[]{:S(2)}) collective-permute-start(bf16[3,8,24,256]{3,2,1,0:T(8,128)(2,1)S(1)} %pad_maximum_fusion.1.refs_1_), channel_id=1, source_target_pairs={{0,15},{1,0},{2,1},{3,2},{4,3},{5,4},{6,5},{7,6},{8,7},{9,8},{10,9... | collective-permute-start | bytes 884744 | tf_op jit(solution)/shard_map/ppermute | solution.py:134
  63.9 36.9 %copy-start.3 = (bf16[3,8,24,256]{3,2,1,0:T(8,128)(2,1)}, bf16[3,8,24,256]{3,2,1,0:T(8,128)(2,1)S(1)}, u32[]{:S(2)}) copy-start(bf16[3,8,24,256]{3,2,1,0:T(8,128)(2,1)S(1)} %collective-permute-done.3.refs_2_) | copy-start | bytes 884740
  63.9 15.0 %collective-permute-start.5 = (bf16[3,8,24,256]{3,2,1,0:T(8,128)(2,1)S(1)}, bf16[3,8,24,256]{3,2,1,0:T(8,128)(2,1)S(1)}, u32[]{:S(2)}, u32[]{:S(2)}) collective-permute-start(bf16[3,8,24,256]{3,2,1,0:T(8,128)(2,1)S(1)} %collective-permute-done.3.refs_2_), channel_id=1, source_target_pairs={{0,1},{1,2},{2,3},{3,4},{4,5},{5,6},{6,7},{7,8},{8,9},{9,10},{10,1... | collective-permute-start | bytes 884744 | tf_op jit(solution)/shard_map/ppermute | solution.py:134
  65.8 19.7 %collective-permute-start.8 = (bf16[3,8,24,256]{3,2,1,0:T(8,128)(2,1)S(1)}, bf16[3,8,24,256]{3,2,1,0:T(8,128)(2,1)S(1)}, u32[]{:S(2)}, u32[]{:S(2)}) collective-permute-start(bf16[3,8,24,256]{3,2,1,0:T(8,128)(2,1)S(1)} %pad_maximum_fusion.1.refs_1_), channel_id=1, source_target_pairs={{0,16},{1,17},{2,18},{3,19},{4,20},{5,21},{6,22},{7,23},{8,24},{9,... | collective-permute-start | bytes 884744 | tf_op jit(solution)/shard_map/ppermute | solution.py:137
  67.8 33.0 %copy-start.6 = (bf16[3,8,24,256]{3,2,1,0:T(8,128)(2,1)}, bf16[3,8,24,256]{3,2,1,0:T(8,128)(2,1)S(1)}, u32[]{:S(2)}) copy-start(bf16[3,8,24,256]{3,2,1,0:T(8,128)(2,1)S(1)} %collective-permute-done.4.refs_3_) | copy-start | bytes 884740
  67.8 23.7 %collective-permute-start.6 = (bf16[3,8,24,256]{3,2,1,0:T(8,128)(2,1)S(1)}, bf16[3,8,24,256]{3,2,1,0:T(8,128)(2,1)S(1)}, u32[]{:S(2)}, u32[]{:S(2)}) collective-permute-start(bf16[3,8,24,256]{3,2,1,0:T(8,128)(2,1)S(1)} %collective-permute-done.4.refs_3_), channel_id=1, source_target_pairs={{0,15},{1,0},{2,1},{3,2},{4,3},{5,4},{6,5},{7,6},{8,7},{9,8},{10,9... | collective-permute-start | bytes 884744 | tf_op jit(solution)/shard_map/ppermute | solution.py:134
  72.9 8.6 %collective-permute-start.7 = (bf16[1,8,24,256]{3,2,1,0:T(8,128)(2,1)S(1)}, bf16[1,8,24,256]{3,2,1,0:T(8,128)(2,1)S(1)}, u32[]{:S(2)}, u32[]{:S(2)}) collective-permute-start(bf16[1,8,24,256]{3,2,1,0:T(8,128)(2,1)S(1)} %slice.4), channel_id=1, source_target_pairs={{0,2},{1,3},{2,4},{3,5},{4,6},{5,7},{6,8},{7,9},{8,10},{9,11},{10,... | collective-permute-start | bytes 294920 | tf_op jit(solution)/shard_map/ppermute | solution.py:134
  74.9 1.1 %copy-start = (bf16[16,8,24,256]{3,2,1,0:T(8,128)(2,1)}, bf16[16,8,24,256]{3,2,1,0:T(8,128)(2,1)S(1)}, u32[]{:S(2)}) copy-start(bf16[16,8,24,256]{3,2,1,0:T(8,128)(2,1)S(1)} %all-to-all-done.refs_0_) | copy-start | bytes 4718596
  78.9 21.9 %copy-start.1 = (bf16[3,8,24,256]{3,2,1,0:T(8,128)(2,1)}, bf16[3,8,24,256]{3,2,1,0:T(8,128)(2,1)S(1)}, u32[]{:S(2)}) copy-start(bf16[3,8,24,256]{3,2,1,0:T(8,128)(2,1)S(1)} %collective-permute-done.5.refs_4_) | copy-start | bytes 884740
  81.5 19.3 %copy-start.4 = (bf16[1,8,24,256]{3,2,1,0:T(8,128)(2,1)}, bf16[1,8,24,256]{3,2,1,0:T(8,128)(2,1)S(1)}, u32[]{:S(2)}) copy-start(bf16[1,8,24,256]{3,2,1,0:T(8,128)(2,1)S(1)} %collective-permute-done.7.refs_6_) | copy-start | bytes 294916
  81.6 19.2 %collective-permute-start.11 = (bf16[4,8,24,256]{3,2,1,0:T(8,128)(2,1)S(1)}, bf16[4,8,24,256]{3,2,1,0:T(8,128)(2,1)S(1)}, u32[]{:S(2)}, u32[]{:S(2)}) collective-permute-start(bf16[4,8,24,256]{3,2,1,0:T(8,128)(2,1)S(1)} %pad_maximum_fusion), channel_id=1, source_target_pairs={{0,16},{1,17},{2,18},{3,19},{4,20},{5,21},{6,22},{7,23},{8,24},{9,... | collective-permute-start | bytes 1179656 | tf_op jit(solution)/shard_map/ppermute | solution.py:137
  85.6 15.3 %copy-start.7 = (bf16[3,8,24,256]{3,2,1,0:T(8,128)(2,1)}, bf16[3,8,24,256]{3,2,1,0:T(8,128)(2,1)S(1)}, u32[]{:S(2)}) copy-start(bf16[3,8,24,256]{3,2,1,0:T(8,128)(2,1)S(1)} %collective-permute-done.8.refs_7_) | copy-start | bytes 884740
  85.6 8.6 %collective-permute-start.10 = (bf16[3,8,24,256]{3,2,1,0:T(8,128)(2,1)S(1)}, bf16[3,8,24,256]{3,2,1,0:T(8,128)(2,1)S(1)}, u32[]{:S(2)}, u32[]{:S(2)}) collective-permute-start(bf16[3,8,24,256]{3,2,1,0:T(8,128)(2,1)S(1)} %collective-permute-done.8.refs_7_), channel_id=1, source_target_pairs={{0,15},{1,0},{2,1},{3,2},{4,3},{5,4},{6,5},{7,6},{8,7},{9,8},{10,9... | collective-permute-start | bytes 884744 | tf_op jit(solution)/shard_map/ppermute | solution.py:134
  87.5 9.8 %collective-permute-start.9 = (bf16[3,8,24,256]{3,2,1,0:T(8,128)(2,1)S(1)}, bf16[3,8,24,256]{3,2,1,0:T(8,128)(2,1)S(1)}, u32[]{:S(2)}, u32[]{:S(2)}) collective-permute-start(bf16[3,8,24,256]{3,2,1,0:T(8,128)(2,1)S(1)} %collective-permute-done.8.refs_7_), channel_id=1, source_target_pairs={{0,1},{1,2},{2,3},{3,4},{4,5},{5,6},{6,7},{7,8},{8,9},{9,10},{10,1... | collective-permute-start | bytes 884744 | tf_op jit(solution)/shard_map/ppermute | solution.py:134
  91.4 9.4 %copy-start.8 = (bf16[3,8,24,256]{3,2,1,0:T(8,128)(2,1)}, bf16[3,8,24,256]{3,2,1,0:T(8,128)(2,1)S(1)}, u32[]{:S(2)}) copy-start(bf16[3,8,24,256]{3,2,1,0:T(8,128)(2,1)S(1)} %collective-permute-done.6.refs_5_) | copy-start | bytes 884740
  91.5 8.6 %collective-permute-start.12 = (bf16[3,8,24,256]{3,2,1,0:T(8,128)(2,1)S(1)}, bf16[3,8,24,256]{3,2,1,0:T(8,128)(2,1)S(1)}, u32[]{:S(2)}, u32[]{:S(2)}) collective-permute-start(bf16[3,8,24,256]{3,2,1,0:T(8,128)(2,1)S(1)} %collective-permute-done.6.refs_5_), channel_id=1, source_target_pairs={{0,16},{1,17},{2,18},{3,19},{4,20},{5,21},{6,22},{7,23},{8,24},{9,... | collective-permute-start | bytes 884744 | tf_op jit(solution)/shard_map/ppermute | solution.py:137
  94.2 6.7 %copy-start.9 = (bf16[3,8,24,256]{3,2,1,0:T(8,128)(2,1)}, bf16[3,8,24,256]{3,2,1,0:T(8,128)(2,1)S(1)}, u32[]{:S(2)}) copy-start(bf16[3,8,24,256]{3,2,1,0:T(8,128)(2,1)S(1)} %collective-permute-done.10.refs_9_) | copy-start | bytes 884740
  97.3 3.5 %copy-start.10 = (bf16[3,8,24,256]{3,2,1,0:T(8,128)(2,1)}, bf16[3,8,24,256]{3,2,1,0:T(8,128)(2,1)S(1)}, u32[]{:S(2)}) copy-start(bf16[3,8,24,256]{3,2,1,0:T(8,128)(2,1)S(1)} %collective-permute-done.9.refs_8_) | copy-start | bytes 884740
  100.1 0.7 copy-start.11
  100.9 0.8 copy-start.5
